TPU v7x, 128 devices: a whole 4x4x4 slice. The times are simulated.
128 devices in a mesh: tile: 16 (over y, z), slab: 8 (over x, core).
Axes of the slice: x: 4, y: 4, z: 4, core: 2. Of those that a mesh axis runs over, the one named last changes fastest.
Arguments:
- volume: bfloat16 [16, 128, 64, 256], P('tile', 'slab'), may hold values from -24 to 24
- partner: int32 [16], replicated, may hold values from 0 to 15, as said below
- offsets: int32 [16], replicated, may hold values from 0 to 7
- starts: int32 [2048], P(('tile', 'slab')), may hold values from 0 to 192
- classifier: int32 [2048, 1], P(('tile', 'slab')), may hold values from 0 to 15; in each aligned block of 16 rows (0 to 15, 16 to 31, ...) at most 2 rows name the same one
- stem_weight: bfloat16 [16, 512, 256], P('tile'), may hold values from -0.25 to 0.25
- expand_weight: bfloat16 [16, 1, 256, 1024], P('tile'), may hold values from -0.375 to 0.375
- shrink_weight: bfloat16 [16, 1, 1024, 256], P('tile'), may hold values from -0.1875 to 0.1875
- head_weight: bfloat16 [16, 256, 8], P('tile'), may hold values from -0.375 to 0.375
Outputs:
- log_response: float32 [16, 128, 64, 256], P('tile', 'slab')
- logits: float32 [2048, 8], P(('tile', 'slab'))
Inputs may be any that keep to these rules, and one draw needn't show every extreme that they name: partner[partner[t]] = t and partner[t] != t for every tile t. Among the 16 candidates of one device at most 2 name the same classifier.
All inputs are finite; a program needn't handle non-finite values.
Results may differ from a plain program's by a relative error of at most 0.0024.
Values may be sent and summed in bfloat16 or wider, within the bound.
No kernel may reach another device: no remote copies, remote signals or barrier semaphores. Data moves between devices by JAX's collectives and lax.ppermute only.
A program may use at most 320 MiB of HBM per device.

v0:
```python
import math

import jax
import jax.numpy as jnp
from jax import lax
from jax.sharding import PartitionSpec as P

OV = 32
CX = 64
CAP = 2


RADIUS = 3


def extended(value, sides, width):
    for axis, dim in sides:
        peers, length = (lax.axis_size(axis), value.shape[dim])
        up = [(i, (i + 1) % peers) for i in range(peers - 1)]
        down = [(j, i) for i, j in up]
        last = lax.slice_in_dim(value, length - width, length, axis=dim)
        first = lax.slice_in_dim(value, 0, width, axis=dim)
        before = lax.ppermute(last, axis, up)
        after = lax.ppermute(first, axis, down)
        value = jnp.concatenate([before, value, after], axis=dim)
    return value


def gauss_taps():
    weights_raw = [math.exp(-0.5 * j * j) for j in range(-RADIUS, RADIUS + 1)]
    summed = sum(weights_raw)
    return [value / summed for value in weights_raw]


def taps_sum(padded, axis, length):
    coeffs = gauss_taps()
    running = coeffs[0] * lax.slice_in_dim(padded, 0, length, axis=axis)
    for offset_tap in range(1, 2 * RADIUS + 1):
        running = running + coeffs[offset_tap] * lax.slice_in_dim(
            padded, offset_tap, offset_tap + length, axis=axis
        )
    return running


def smooth_lateral(values):
    padded = jnp.pad(values, ((0, 0), (0, 0), (RADIUS, RADIUS), (0, 0)))
    values = taps_sum(padded, 2, values.shape[2])
    padded = jnp.pad(values, ((0, 0), (0, 0), (0, 0), (RADIUS, RADIUS)))
    return taps_sum(padded, 3, values.shape[3])


def laplace_rimmed(rimmed):
    center = rimmed[:, 1:-1]
    lateral = jnp.pad(center, ((0, 0), (0, 0), (1, 1), (1, 1)))
    beside = rimmed[:, 2:] + rimmed[:, :-2]
    beside = beside + lateral[:, :, 2:, 1:-1] + lateral[:, :, :-2, 1:-1]
    beside = beside + lateral[:, :, 1:-1, 2:] + lateral[:, :, 1:-1, :-2]
    return beside - 6.0 * center


def patchify(cube_block):
    chans, planes, height, across = cube_block.shape
    shaped = cube_block.reshape(chans, planes // 4, 4, height // 8, 8, across // 8, 8)
    shaped = shaped.transpose(1, 3, 5, 0, 2, 4, 6)
    return shaped.reshape(planes // 4 * (height // 8) * (across // 8), chans * 256)


def classify(hidden, expands, shrinks, heads):
    mix_up = "npk,kh->nph"
    mix_down = "nph,hk->npk"
    mix_head = "nk,kc->nc"
    wide = hidden.astype(jnp.float32)
    normed = (wide * lax.rsqrt(jnp.mean(wide * wide, axis=-1, keepdims=True) + 1e-05)).astype(
        jnp.bfloat16
    )
    up_part = expands[0]
    down_part = shrinks[0]
    expanded = jax.nn.relu(
        jnp.einsum(mix_up, normed, up_part, preferred_element_type=jnp.float32)
    ).astype(jnp.bfloat16)
    hidden = (
        wide + jnp.einsum(mix_down, expanded, down_part, preferred_element_type=jnp.float32)
    ).astype(jnp.bfloat16)
    pooled = jnp.mean(hidden.astype(jnp.float32), axis=1)
    return jnp.einsum(mix_head, pooled, heads.astype(jnp.float32), precision=lax.Precision.HIGHEST)


def body(
    volume,
    partner,
    offsets,
    starts,
    classifier,
    stem_weight,
    expand_weight,
    shrink_weight,
    head_weight,
):
    tile_count = lax.axis_size("tile")
    tile_me = lax.axis_index("tile")
    planes_dev, rows_dev, width_dev = (volume.shape[1], volume.shape[2], volume.shape[3])
    partner_tile = partner[tile_me]
    piece = lax.all_gather(volume[:, :, :, :OV], "tile", axis=0, tiled=True)
    tile_ids = jnp.arange(piece.shape[0], dtype=jnp.int32)
    selected = (tile_ids == partner_tile).astype(jnp.float32)[:, None, None, None]
    mate_strip = jnp.sum(piece.astype(jnp.float32) * selected, axis=0, keepdims=True)
    rows_back = (jnp.arange(rows_dev, dtype=jnp.int32) - offsets[tile_me]) % rows_dev
    mate_strip = jnp.take(mate_strip, rows_back, axis=2)
    values = volume.astype(jnp.float32)
    column = jnp.arange(OV, dtype=jnp.float32)
    ramp = 0.25 + 0.5 * (column + 0.5) / OV
    joined = jnp.concatenate(
        [ramp * values[..., :OV] + (1.0 - ramp) * mate_strip, values[..., OV:]], axis=3
    )
    rimmed = extended(joined.astype(jnp.bfloat16), (("slab", 1),), RADIUS).astype(joined.dtype)
    smooth = smooth_lateral(taps_sum(rimmed, 1, planes_dev))
    smooth_rimmed = extended(smooth, (("slab", 1),), 1)
    log_response = laplace_rimmed(smooth_rimmed)
    channel_pair = jnp.stack(
        [smooth[0].astype(jnp.bfloat16), log_response[0].astype(jnp.bfloat16)], axis=0
    )
    zero = jnp.zeros((), jnp.int32)

    def cut(begin):
        return patchify(
            lax.dynamic_slice(
                channel_pair, (zero, zero, zero, begin), (2, planes_dev, rows_dev, CX)
            )
        )

    routes = classifier[:, 0]
    cand_count = routes.shape[0]
    cand_ids = jnp.arange(cand_count, dtype=jnp.int32)
    same_dest = routes[:, None] == routes[None, :]
    earlier = cand_ids[None, :] < cand_ids[:, None]
    slot_rank = jnp.sum((same_dest & earlier).astype(jnp.int32), axis=1)
    slot_ids = routes * CAP + slot_rank
    slot_count = tile_count * CAP
    slot_hits = slot_ids[None, :] == jnp.arange(slot_count, dtype=jnp.int32)[:, None]
    filled = jnp.any(slot_hits, axis=1)
    source = jnp.sum(slot_hits.astype(jnp.int32) * cand_ids[None, :], axis=1)
    slot_patches = jax.vmap(cut)(starts[source]) * filled.astype(jnp.bfloat16)[:, None, None]
    slot_patches = slot_patches.reshape(
        tile_count, CAP, slot_patches.shape[1], slot_patches.shape[2]
    )
    pos_count = slot_patches.shape[2]
    arrived = lax.all_to_all(slot_patches, "tile", split_axis=0, concat_axis=0, tiled=True)
    senders = arrived.shape[0]
    items = arrived.shape[1]
    flat = arrived.reshape(senders * items, pos_count, arrived.shape[3])
    hidden = jnp.einsum(
        "npf,fk->npk", flat, stem_weight[0], preferred_element_type=jnp.float32
    ).astype(jnp.bfloat16)
    scores = classify(hidden, expand_weight[0], shrink_weight[0], head_weight[0])
    scored = scores.reshape(senders, items, scores.shape[1])
    returned = lax.all_to_all(scored, "tile", split_axis=0, concat_axis=0, tiled=True)
    logits = returned.reshape(slot_count, returned.shape[2])[slot_ids]
    return (log_response, logits)


def solution(mesh):
    return jax.shard_map(
        body,
        mesh=mesh,
        in_specs=(
            P("tile", "slab", None, None),
            P(),
            P(),
            P(("tile", "slab")),
            P(("tile", "slab"), None),
            P("tile", None, None),
            P("tile", None, None, None),
            P("tile", None, None, None),
            P("tile", None, None),
        ),
        out_specs=(P("tile", "slab", None, None), P(("tile", "slab"), None)),
        check_vma=False,
    )
```

profile of v0, /device:TPU:1, one launch (start us, length us, event | category | flops | bytes accessed | tf_op | source)
XLA Modules:
  0.0 731.3 jit_solution(11297855956856211951)
XLA Ops:
  7.2 0.0 copy-start
  7.2 0.0 all-gather.2.cloned.1.call-start
  7.2 1.0 slice.101
  8.2 0.8 copy.49
  9.0 0.0 all-gather.2.cloned.1.call-update
  9.1 1.4 copy_convert_fusion
  10.4 0.2 slice.292
  10.6 1.2 dynamic_slice.7
  11.9 1.2 dynamic_slice.6
  13.1 0.9 convert_reduce_fusion.1
  14.0 0.7 multiply_add_fusion
  14.7 0.1 select_reduce_fusion
  14.8 1.4 gather_fusion.1
  16.2 0.6 fusion.63
  16.7 0.6 compare_and_fusion
  17.3 0.7 compare_convert_fusion
  18.0 0.2 slice_bitcast_fusion
  18.2 40.0 %all-gather.2.cloned.1.call-done = bf16[16,16,64,32]{2,3,1,0:T(8,128)(2,1)} async-done(((bf16[1,16,64,32]{2,3,1,0:T(8,128)(2,1)}), bf16[16,16,64,32]{2,3,1,0:T(8,128)(2,1)}) %all-gather.2.cloned.1.call-update) | async-done | bytes 1048592 | tf_op jit(solution)/shard_map/all_gather | solution.py:103
  58.2 2.2 multiply_reduce_fusion
  60.4 1.0 copy.40
  61.5 1.6 gather_fusion
  63.1 0.2 fusion.50
  63.3 0.3 pad_maximum_fusion.4
  63.6 3.6 collective-permute-start.1
  67.3 3.0 collective-permute-start
  70.3 0.3 maximum_bitcast_fusion
  70.6 0.4 collective-permute-done.1
  71.0 1.2 collective-permute-done
  72.2 0.4 maximum_convert_fusion.4
  72.6 0.8 fusion.43
  73.4 0.3 fusion.19
  73.8 1.7 fusion.70
  75.4 0.1 fusion.74
  75.5 4.4 collective-permute-start.3
  79.9 2.1 collective-permute-start.2
  82.0 0.1 fusion.58
  82.1 0.1 reshape.260
  82.2 0.0 collective-permute-done.3
  82.2 3.3 collective-permute-done.2
  85.5 1.6 fusion.72
  87.1 1.1 pad_maximum_fusion.2
  88.1 4.6 copy.41
  92.7 7.3 gather_fusion.2
  100.0 40.6 %copy.42 = bf16[32,2,16,64,64]{0,4,3,2,1:T(8,128)(2,1)} copy(bf16[32,2,16,64,64]{3,2,1,4,0:T(8,128)(2,1)} %gather_fusion.2) | data formatting | bytes 16777216 | tf_op jit(solution)/shard_map/vmap()/gather | solution.py:126
  140.6 202.5 %copy.43 = bf16[32,4,8,8,2,4,8,8]{7,6,5,4,3,2,1,0:T(8,128)(2,1)} copy(bf16[32,4,8,8,2,4,8,8]{0,7,3,6,2,5,1,4:T(8,128)(2,1)} %bitcast.62) | data formatting | bytes 16777216 | tf_op jit(solution)/shard_map/vmap()/transpose | solution.py:64
  343.1 188.7 %reshape.257 = bf16[16,2,256,512]{3,2,1,0:T(8,128)(2,1)} reshape(bf16[32,4,8,8,2,4,8,8]{7,6,5,4,3,2,1,0:T(8,128)(2,1)} %copy.43) | data formatting | bytes 16777216 | tf_op jit(solution)/shard_map/vmap()/reshape | solution.py:65
  531.8 7.2 broadcast_multiply_fusion
  539.0 5.1 all-to-all-start
  544.1 0.0 copy-done.5
  544.2 118.2 %all-to-all-done = bf16[16,2,256,512]{3,2,1,0:T(8,128)(2,1)} async-done(((bf16[16,2,256,512]{3,2,1,0:T(8,128)(2,1)}), bf16[16,2,256,512]{3,2,1,0:T(8,128)(2,1)}, u32[]{:S(2)}, u32[]{:S(2)}) %all-to-all-start) | async-done | bytes 8388640 | tf_op jit(solution)/shard_map/all_to_all | solution.py:147
  662.4 0.0 copy-done.4
  662.4 7.7 %fusion.2 = (f32[32,256]{1,0:T(8,128)S(1)}, bf16[32,256,256]{2,1,0:T(8,128)(2,1)}) fusion(bf16[32,256,512]{2,1,0:T(8,128)(2,1)} %bitcast.15, bf16[1,512,256]{2,1,0:T(8,128)(2,1)S(1)} %copy-done.4), kind=kOutput, calls=%fused_computation.10 | convolution fusion | flops 2155864064 | bytes 12877824 | tf_op jit(solution)/shard_map/npf,fk->npk/dot_general | solution.py:151
  670.1 0.0 copy-done
  670.2 0.0 copy-done.3
  670.2 0.0 copy-start.2
  670.2 0.0 copy-start.1
  670.2 12.9 %convert_reduce_fusion = f32[32,256]{1,0:T(8,128)S(1)} fusion(bf16[32,256,256]{2,1,0:T(8,128)(2,1)} %get-tuple-element.19, f32[32,256]{1,0:T(8,128)S(1)} %add_rsqrt_fusion, bf16[1,1,1024,256]{3,2,1,0:T(8,128)(2,1)S(1)} %copy-done, bf16[1,1,256,1024]{3,2,1,0:T(8,128)(2,1)S(1)} %copy-done.3), kind=kOutput, calls=%fused_computation.13 | convolution fusion | flops 8623480832 | bytes 5308416 | tf_op jit(solution)/shard_map/nph,hk->npk/dot_general | solution.py:82
  683.1 0.1 fusion.56
  683.2 0.7 copy.45
  684.0 32.8 %all-to-all-start.1 = ((f32[16,2,8]{2,1,0:T(2,128)}), f32[16,2,8]{2,1,0:T(2,128)S(1)}, u32[]{:S(2)}, u32[]{:S(2)}) async-start(f32[16,2,8]{2,1,0:T(2,128)} %copy.45), calls=%async_computation.1 | async-start | bytes 32768 | tf_op jit(solution)/shard_map/all_to_all | solution.py:156
  716.8 1.6 copy.46
  718.4 4.9 all-to-all-done.1
  723.2 0.6 gather_fusion.3
  723.8 0.7 copy.47
  (16 shorter events, 0.1 us)
Async XLA Ops:
  7.2 663.0 %copy-start = (bf16[1,1,1024,256]{3,2,1,0:T(8,128)(2,1)S(1)}, bf16[1,1,1024,256]{3,2,1,0:T(8,128)(2,1)}, u32[]{:S(2)}) copy-start(bf16[1,1,1024,256]{3,2,1,0:T(8,128)(2,1)} %param.16) | copy-start | bytes 1572868
  7.2 51.0 %all-gather.2.cloned.1.call-start = ((), (), s32[]{:S(2)}) async-start(), calls=%async_computation.2 | async-start | bytes 2228224 | tf_op jit(solution)/shard_map/all_gather | solution.py:103
  63.6 7.4 %collective-permute-start.1 = (bf16[1,3,64,256]{3,1,2,0:T(4,128)(2,1)S(1)}, bf16[1,3,64,256]{3,1,2,0:T(4,128)(2,1)S(1)}, u32[]{:S(2)}, u32[]{:S(2)}) collective-permute-start(bf16[1,3,64,256]{3,1,2,0:T(4,128)(2,1)S(1)} %get-tuple-element.17), channel_id=1, source_target_pairs={{1,0},{2,1},{3,2},{4,3},{5,4},{6,5},{7,6},{9,8},{10,9},{11,10},{12... | collective-permute-start | bytes 294920 | tf_op jit(solution)/shard_map/ppermute | solution.py:24
  67.3 4.9 collective-permute-start
  75.5 6.7 collective-permute-start.3
  79.9 5.6 collective-permute-start.2
  539.0 5.1 copy-start.5
  539.0 123.3 %copy-start.4 = (bf16[1,512,256]{2,1,0:T(8,128)(2,1)S(1)}, bf16[1,512,256]{2,1,0:T(8,128)(2,1)}, u32[]{:S(2)}) copy-start(bf16[1,512,256]{2,1,0:T(8,128)(2,1)} %param.14) | copy-start | bytes 786436
  539.0 123.3 %all-to-all-start = ((bf16[16,2,256,512]{3,2,1,0:T(8,128)(2,1)}), bf16[16,2,256,512]{3,2,1,0:T(8,128)(2,1)}, u32[]{:S(2)}, u32[]{:S(2)}) async-start(bf16[16,2,256,512]{3,2,1,0:T(8,128)(2,1)} %broadcast_multiply_fusion), calls=%async_computation | async-start | bytes 16777216 | tf_op jit(solution)/shard_map/all_to_all | solution.py:147
  662.4 7.8 %copy-start.3 = (bf16[1,1,256,1024]{3,2,1,0:T(8,128)(2,1)S(1)}, bf16[1,1,256,1024]{3,2,1,0:T(8,128)(2,1)}, u32[]{:S(2)}) copy-start(bf16[1,1,256,1024]{3,2,1,0:T(8,128)(2,1)} %param.15) | copy-start | bytes 1572868
  670.2 12.9 %copy-start.2 = (bf16[1,256,8]{1,2,0:T(8,128)(2,1)S(1)}, bf16[1,256,8]{1,2,0:T(8,128)(2,1)}, u32[]{:S(2)}) copy-start(bf16[1,256,8]{1,2,0:T(8,128)(2,1)} %param.17) | copy-start | bytes 12292
  670.2 46.6 %copy-start.1 = (f32[1,16,64,256]{3,1,2,0:T(8,128)S(1)}, f32[1,16,64,256]{3,1,2,0:T(8,128)}, u32[]{:S(2)}) copy-start(f32[1,16,64,256]{3,1,2,0:T(8,128)} %get-tuple-element.13) | copy-start | bytes 3145732
  684.0 39.2 %all-to-all-start.1 = ((f32[16,2,8]{2,1,0:T(2,128)}), f32[16,2,8]{2,1,0:T(2,128)S(1)}, u32[]{:S(2)}, u32[]{:S(2)}) async-start(f32[16,2,8]{2,1,0:T(2,128)} %copy.45), calls=%async_computation.1 | async-start | bytes 32768 | tf_op jit(solution)/shard_map/all_to_all | solution.py:156
Sparse Core Ops, SparseCore 0:
  10.7 47.4 all-gather.1
where the time goes:
time: 742 us; the launch traced here: 731 us
  local copies, waits for them, and re-layouts  456 us (61%)
  waiting for transfers between devices  168 us (23%)
  starting transfers between devices  51 us (7%)
  other arithmetic  21.1 us (3%)
  matrix products  20.7 us (3%)
  between operations  14.3 us (2%)
    transpose x1, local copies, waits for them, and re-layouts, patchify(): shaped = shaped.transpose(1, 3, 5, 0, 2, 4, 6)  203 us
    reshape x1, local copies, waits for them, and re-layouts, patchify(): shaped.reshape(planes // 4 * (height // 8) * (across // 8), chans * 256)  189 us
    all_to_all x1, waiting for transfers between devices, body(): lax.all_to_all(slot_patches, 'tile', split_axis=0, concat_axis=0, tiled=T...  118 us
    gather x2, local copies, waits for them, and re-layouts, cut(): lax.dynamic_slice(channel_pair, (zero, zero, zero, begin), (2, planes_dev...  47.8 us
    all_gather x1, waiting for transfers between devices, body(): piece = lax.all_gather(volume[:, :, :, :OV], 'tile', axis=0, tiled=True)  40 us
    all_to_all x1, starting transfers between devices, body(): lax.all_to_all(scored, 'tile', split_axis=0, concat_axis=0, tiled=True)  32.8 us
  transfers between devices with their start and end apart: 7, of which 6 were waited for; matrix products, arithmetic and copies ran while one was open for 2% of the time, Pallas kernels for 0%

commit v1 on v0

v1 whole, which is shorter than its diff:
```python
import functools
import math

import jax
import jax.numpy as jnp
from jax import lax
from jax.experimental import pallas as pl
from jax.experimental.pallas import tpu as pltpu
from jax.sharding import PartitionSpec as P

OV = 32
CX = 64
RADIUS = 3
HALO = 4
F32 = jnp.float32
BF16 = jnp.bfloat16
HIGH = lax.Precision.HIGHEST

STEM_ROWS, EXPAND_ROWS, SHRINK_ROWS, HEAD_ROWS = 128, 256, 256, 16
EXPAND_AT = STEM_ROWS
SHRINK_AT = EXPAND_AT + EXPAND_ROWS
HEAD_AT = SHRINK_AT + SHRINK_ROWS
PART_ROWS = HEAD_AT + HEAD_ROWS


def gauss_taps():
    weights_raw = [math.exp(-0.5 * j * j) for j in range(-RADIUS, RADIUS + 1)]
    summed = sum(weights_raw)
    return [value / summed for value in weights_raw]


def pack_kernel(part_ref, stem_ref, expand_ref, shrink_ref, head_ref, out_ref, wide_ref):
    for half in range(2):
        lanes = pl.ds(128 * half, 128)
        wide_ref[...] = stem_ref[:, lanes].astype(F32)
        out_ref[pl.ds(64 * half, 64), :] = wide_ref[pl.ds(part_ref[0], 64, stride=8), :].astype(BF16)
        out_ref[pl.ds(SHRINK_AT + 128 * half, 128), :] = shrink_ref[:, lanes]
    out_ref[pl.ds(EXPAND_AT, 256), :] = expand_ref[...]
    out_ref[pl.ds(HEAD_AT, 16), :] = jnp.concatenate(
        [head_ref[:, :128].astype(F32), head_ref[:, 128:].astype(F32)], axis=0
    ).astype(BF16)


def pack_part(part, stem, expand, shrink, head):
    return pl.pallas_call(
        pack_kernel,
        out_shape=jax.ShapeDtypeStruct((PART_ROWS, 128), BF16),
        grid_spec=pltpu.PrefetchScalarGridSpec(
            num_scalar_prefetch=1,
            grid=(1,),
            in_specs=[
                pl.BlockSpec((512, 256), lambda i, p: (0, 0)),
                pl.BlockSpec((256, 128), lambda i, p: (0, p[0])),
                pl.BlockSpec((128, 256), lambda i, p: (p[0], 0)),
                pl.BlockSpec((8, 256), lambda i, p: (0, 0)),
            ],
            out_specs=pl.BlockSpec((PART_ROWS, 128), lambda i, p: (0, 0)),
            scratch_shapes=[pltpu.VMEM((512, 128), F32)],
        ),
        cost_estimate=pl.CostEstimate(flops=0, bytes_accessed=1 << 20, transcendentals=0),
        name="pack_part",
    )(part, stem, expand, shrink, head)


def band_kernel(
    scalars_ref, before_ref, own_ref, after_ref, mate_ref, log_ref, table_ref,
    joined_ref, rows_ref, smooth_ref, columns_ref,
):
    taps = gauss_taps()
    planes, rows, width = own_ref.shape
    offset, slab, slabs = scalars_ref[1], scalars_ref[2], scalars_ref[3]
    total = planes + 2 * HALO
    group = total // 4

    lane = lax.broadcasted_iota(jnp.int32, (rows, 128), 1)
    ramp = 0.25 + 0.5 * (lane.astype(F32) + 0.5) / OV
    for i in range(group):
        strip = pltpu.roll(mate_ref[0, i].astype(F32), offset, 0)
        for quarter in range(4):
            z = quarter * group + i
            if z < HALO:
                raw = before_ref[z]
            elif z < HALO + planes:
                raw = own_ref[z - HALO]
            else:
                raw = after_ref[z - HALO - planes]
            raw = raw.astype(F32)
            mate = strip if quarter == 0 else pltpu.roll(strip, 128 - 32 * quarter, 1)
            first = raw[:, :128]
            joined_ref[z, :, :128] = jnp.where(
                lane < OV, ramp * first + (1.0 - ramp) * mate, first
            )
            joined_ref[z, :, 128:] = raw[:, 128:]

    source = lax.broadcasted_iota(jnp.int32, (width, width), 0)
    target = lax.broadcasted_iota(jnp.int32, (width, width), 1)

    def band_matrix(shift):
        out = jnp.zeros((width, width), F32)
        for j in range(-RADIUS, RADIUS + 1):
            out = jnp.where(source - target == shift + j, taps[j + RADIUS], out)
        return out

    along = band_matrix(0)
    beside = jnp.where(target < width - 1, band_matrix(1), 0.0)
    beside = beside + jnp.where(target > 0, band_matrix(-1), 0.0)

    margin = jnp.zeros((planes + 2, 8, width), F32)
    rows_ref[:, :8, :] = margin
    rows_ref[:, 8 + rows :, :] = margin
    smooth_ref[:, :8, :] = margin
    smooth_ref[:, 8 + rows :, :] = margin

    for p in range(planes + 2):
        mixed = taps[0] * joined_ref[p]
        for j in range(1, 2 * RADIUS + 1):
            mixed = mixed + taps[j] * joined_ref[p + j]
        rows_ref[p, pl.ds(8, rows), :] = mixed
        mixed = taps[0] * rows_ref[p, pl.ds(8 - RADIUS, rows), :]
        for j in range(1, 2 * RADIUS + 1):
            mixed = mixed + taps[j] * rows_ref[p, pl.ds(8 - RADIUS + j, rows), :]
        smooth = jnp.dot(mixed, along, precision=HIGH, preferred_element_type=F32)
        if p == 0:
            smooth = jnp.where(slab > 0, smooth, 0.0)
        elif p == planes + 1:
            smooth = jnp.where(slab < slabs - 1, smooth, 0.0)
        else:
            log_ref[p - 1] = jnp.dot(mixed, beside, precision=HIGH, preferred_element_type=F32)
        smooth_ref[p, pl.ds(8, rows), :] = smooth
    for z in range(planes):
        p = z + 1
        here = smooth_ref[p, pl.ds(8, rows), :]
        near = smooth_ref[p - 1, pl.ds(8, rows), :] + smooth_ref[p + 1, pl.ds(8, rows), :]
        near = near + (smooth_ref[p, pl.ds(7, rows), :] + smooth_ref[p, pl.ds(9, rows), :])
        log_ref[z] = near + log_ref[z] - 6.0 * here

    count = (planes // 4) * (rows // 8)
    for a in range(planes // 4):
        for b in range(rows // 8):
            pieces = [
                smooth_ref[4 * a + dz + 1, pl.ds(8 + 8 * b, 8), :] for dz in range(4)
            ] + [log_ref[4 * a + dz, pl.ds(8 * b, 8), :] for dz in range(4)]
            block = jnp.concatenate(pieces, axis=0)
            block = jnp.concatenate([block, pltpu.roll(block, width - 1, 1)], axis=0)
            columns_ref[pl.ds(a * (rows // 8) + b, width, stride=count), :] = block.T
    table_ref[...] = columns_ref[...].astype(BF16)


def filter_band(scalars, before, own, after, mates):
    planes, rows, width = own.shape
    count = (planes // 4) * (rows // 8)
    whole3 = lambda i, s: (0, 0, 0)
    return pl.pallas_call(
        band_kernel,
        out_shape=(
            jax.ShapeDtypeStruct((planes, rows, width), F32),
            jax.ShapeDtypeStruct((width * count, 128), BF16),
        ),
        grid_spec=pltpu.PrefetchScalarGridSpec(
            num_scalar_prefetch=1,
            grid=(1,),
            in_specs=[
                pl.BlockSpec((HALO, rows, width), whole3),
                pl.BlockSpec((planes, rows, width), whole3),
                pl.BlockSpec((HALO, rows, width), whole3),
                pl.BlockSpec((1,) + mates.shape[1:], lambda i, s: (s[0], 0, 0, 0)),
            ],
            out_specs=(
                pl.BlockSpec((planes, rows, width), whole3),
                pl.BlockSpec((width * count, 128), lambda i, s: (0, 0)),
            ),
            scratch_shapes=[
                pltpu.VMEM((planes + 2 * HALO, rows, width), F32),
                pltpu.VMEM((planes + 2, rows + 16, width), F32),
                pltpu.VMEM((planes + 2, rows + 16, width), F32),
                pltpu.VMEM((width * count, 128), F32),
            ],
        ),
        compiler_params=pltpu.CompilerParams(vmem_limit_bytes=40 << 20),
        cost_estimate=pl.CostEstimate(
            flops=2_000_000_000, bytes_accessed=6 << 20, transcendentals=0
        ),
        name="filter_band",
    )(scalars, before, own, after, mates)


def classify_kernel(starts_ref, route_ref, table_ref, weight_ref, out_ref, score_ref):
    i = pl.program_id(0)
    begin = starts_ref[i]

    def rows_of(part, at, count):
        return weight_ref[0, part, pl.ds(at, count), :]

    def joined_lanes(parts, at, count):
        halves = [
            jnp.concatenate([rows_of(p, at + h * count, count) for p in parts], axis=0)
            for h in range(2)
        ]
        return jnp.concatenate(halves, axis=1)

    hidden = None
    for half in range(2):
        patches = jnp.concatenate(
            [
                jnp.concatenate(
                    [table_ref[begin + 8 * c + 4 * half + 2 * j] for j in range(2)], axis=1
                )
                for c in range(8)
            ],
            axis=0,
        )
        stem = joined_lanes(range(4 * half, 4 * half + 4), 0, 64)
        term = jnp.dot(patches, stem, preferred_element_type=F32)
        hidden = term if hidden is None else hidden + term
    wide = hidden.astype(BF16).astype(F32)
    power = jnp.mean(wide * wide, axis=-1, keepdims=True)
    normed = (wide * lax.rsqrt(power + 1e-05)).astype(BF16)
    total = wide
    for pair in range(4):
        parts = (2 * pair, 2 * pair + 1)
        expand = jnp.concatenate([rows_of(p, EXPAND_AT, 256) for p in parts], axis=1)
        up = jnp.dot(normed, expand, preferred_element_type=F32)
        up = jnp.maximum(up, 0.0).astype(BF16)
        shrink = joined_lanes(parts, SHRINK_AT, 128)
        total = total + jnp.dot(up, shrink, preferred_element_type=F32)
    last = total.astype(BF16).astype(F32)
    pooled = jnp.sum(last, axis=0, keepdims=True) * (1.0 / last.shape[0])
    head = rows_of(0, HEAD_AT, 16).astype(F32)
    products = head[:8] * pooled[:, :128] + head[8:] * pooled[:, 128:]
    scores = jnp.sum(products, axis=1, keepdims=True)
    lane = lax.broadcasted_iota(jnp.int32, (8, 128), 1)
    score_ref[...] = jnp.where(lane == i, scores, score_ref[...])

    @pl.when(i == pl.num_programs(0) - 1)
    def _():
        out_ref[...] = score_ref[...].T[: out_ref.shape[0], :]


def classify(starts, routes, table, weights):
    count = starts.shape[0]
    parts = weights.shape[1]
    return pl.pallas_call(
        classify_kernel,
        out_shape=jax.ShapeDtypeStruct((count, 8), F32),
        grid_spec=pltpu.PrefetchScalarGridSpec(
            num_scalar_prefetch=2,
            grid=(count,),
            in_specs=[
                pl.BlockSpec(table.shape, lambda i, s, r: (0, 0, 0)),
                pl.BlockSpec((1, parts, PART_ROWS, 128), lambda i, s, r: (r[i], 0, 0, 0)),
            ],
            out_specs=pl.BlockSpec((count, 8), lambda i, s, r: (0, 0)),
            scratch_shapes=[pltpu.VMEM((8, 128), F32)],
        ),
        compiler_params=pltpu.CompilerParams(vmem_limit_bytes=40 << 20),
        cost_estimate=pl.CostEstimate(
            flops=5_500_000_000, bytes_accessed=24 << 20, transcendentals=4096
        ),
        name="classify",
    )(starts, routes, table, weights)


def body(
    volume, partner, offsets, starts, classifier, stem_weight, expand_weight, shrink_weight, head_weight
):
    tile_me, slab_me = lax.axis_index("tile"), lax.axis_index("slab")
    tiles, slabs = lax.axis_size("tile"), lax.axis_size("slab")
    own = volume[0]
    planes, rows, width = own.shape

    part = pack_part(
        jnp.reshape(slab_me, (1,)).astype(jnp.int32),
        stem_weight[0], expand_weight[0, 0], shrink_weight[0, 0], head_weight[0].T,
    )
    weights = lax.all_gather(part, ("tile", "slab"), axis=0, tiled=False)
    weights = weights.reshape(tiles, slabs, PART_ROWS, 128)

    up = [(i, i + 1) for i in range(slabs - 1)]
    down = [(j, i) for i, j in up]
    before = lax.ppermute(own[planes - HALO :], "slab", up)
    after = lax.ppermute(own[:HALO], "slab", down)

    group = (planes + 2 * HALO) // 4
    strip = jnp.concatenate([before[:, :, :OV], own[:, :, :OV], after[:, :, :OV]], axis=0)
    strip = jnp.concatenate([strip[q * group : (q + 1) * group] for q in range(4)], axis=2)
    sent = jnp.broadcast_to(strip[None], (tiles,) + strip.shape)
    mates = lax.all_to_all(sent, "tile", split_axis=0, concat_axis=0, tiled=True)

    scalars = jnp.stack([partner[tile_me], offsets[tile_me], slab_me, jnp.int32(slabs)])
    log_response, table = filter_band(scalars, before, own, after, mates)
    table = table.reshape(width, -1, 128)
    logits = classify(starts, classifier[:, 0], table, weights)
    return (log_response[None], logits)


def solution(mesh):
    return jax.shard_map(
        body,
        mesh=mesh,
        in_specs=(
            P("tile", "slab", None, None),
            P(),
            P(),
            P(("tile", "slab")),
            P(("tile", "slab"), None),
            P("tile", None, None),
            P("tile", None, None, None),
            P("tile", None, None, None),
            P("tile", None, None),
        ),
        out_specs=(P("tile", "slab", None, None), P(("tile", "slab"), None)),
        check_vma=False,
    )
```

time: 742 us -> 141 us (0.19); the launches traced: 731 us -> 141 us
  local copies, waits for them, and re-layouts: 456 us -> 7.24 us
  waiting for transfers between devices: 168 us -> 72.2 us
  starting transfers between devices: 51 us -> 14.2 us
  Pallas kernels: 0 us -> 31.4 us
  matrix products: 20.7 us -> 0 us
  other arithmetic: 21.1 us -> 1.56 us
    transpose x1 -> x0, local copies, waits for them, and re-layouts: 203 us -> none  [patchify(): shaped = shaped.transpose(1, 3, 5, 0, 2, 4, 6)]
    reshape x1 -> x0, local copies, waits for them, and re-layouts: 189 us -> none  [patchify(): shaped.reshape(planes // 4 * (height // 8) * (across // 8), chans * 256)]
    all_to_all x2 -> x1, waiting for transfers between devices: 123 us -> 20.3 us  [body(): lax.all_to_all(sent, 'tile', split_axis=0, concat_axis=0, tiled=True)]
    gather x5 -> x0, local copies, waits for them, and re-layouts: 51.4 us -> none  [the longest x2 47.8 us: cut(): lax.dynamic_slice(channel_pair, (zero, zero, zero, begin), (2, planes_dev...]
    pallas_call x0 -> x3, Pallas kernels: none -> 31.4 us  [the longest x1 20.1 us: classify(): pl.pallas_call(classify_kernel, out_shape=jax.ShapeDtypeStruct((count, 8)...]
    all_to_all x2 -> x1, starting transfers between devices: 37.9 us -> 7.77 us  [body(): lax.all_to_all(sent, 'tile', split_axis=0, concat_axis=0, tiled=True)]
    dot_general x3 -> x0, matrix products: 20.7 us -> none  [the longest x1 12.9 us: classify(): jnp.einsum(mix_down, expanded, down_part, preferred_element_type=jnp.floa...]
    all_gather x1, waiting for transfers between devices: 40 us -> 47.7 us  [body(): weights = lax.all_gather(part, ('tile', 'slab'), axis=0, tiled=False)]
  transfers between devices with their start and end apart: 7 -> 4, of which waited for: 6 -> 3; matrix products, arithmetic and copies ran while one was open for 2% -> 4% of each run, Pallas kernels for 0% -> 7%
where the time goes in v1:
time: 141 us
  waiting for transfers between devices  72.2 us (51%)
  Pallas kernels  31.4 us (22%)
  starting transfers between devices  14.2 us (10%)
  between operations  14.2 us (10%)
  local copies, waits for them, and re-layouts  7.24 us (5%)
  other arithmetic  1.56 us (1%)
    all_gather x1, waiting for transfers between devices, body(): weights = lax.all_gather(part, ('tile', 'slab'), axis=0, tiled=False)  47.7 us
    all_to_all x1, waiting for transfers between devices, body(): lax.all_to_all(sent, 'tile', split_axis=0, concat_axis=0, tiled=True)  20.3 us
    pallas_call x1, Pallas kernels, classify(): pl.pallas_call(classify_kernel, out_shape=jax.ShapeDtypeStruct((count, 8)...  20.1 us
    pallas_call x1, Pallas kernels, filter_band(): pl.pallas_call(band_kernel, out_shape=(jax.ShapeDtypeStruct((planes, rows...  9.49 us
    all_to_all x1, starting transfers between devices, body(): lax.all_to_all(sent, 'tile', split_axis=0, concat_axis=0, tiled=True)  7.77 us
    ppermute x1, starting transfers between devices, body(): before = lax.ppermute(own[planes - HALO:], 'slab', up)  4.51 us
    ppermute x1, waiting for transfers between devices, body(): after = lax.ppermute(own[:HALO], 'slab', down)  4.25 us
    unnamed x15, local copies, waits for them, and re-layouts  3.3 us
  transfers between devices with their start and end apart: 4, of which 3 were waited for; matrix products, arithmetic and copies ran while one was open for 4% of the time, Pallas kernels for 7%

profile of v1, /device:TPU:1, one launch (start us, length us, event | category | flops | bytes accessed | tf_op | source)
XLA Modules:
  0.0 140.8 jit_solution(14399622676773868017)
XLA Ops:
  7.2 0.0 copy-start.2
  7.2 0.0 all-gather.3.cloned.1.call-start
  7.2 1.8 %pack_part.1 = bf16[656,128]{1,0:T(8,128)(2,1)} custom-call(s32[1]{0:T(128)} %bitcast.part_ref, bf16[512,256]{1,0:T(8,128)(2,1)} %bitcast.24, bf16[256,1024]{1,0:T(8,128)(2,1)} %bitcast.22, bf16[1024,256]{1,0:T(8,128)(2,1)} %bitcast.23, bf16[8,256]{1,0:T(8,128)(2,1)} %bitcast.25), custom_call_target="tpu_custom_call" | custom-call | bytes 1048576 | tf_op jit(solution)/shard_map/pack_part/pallas_call | solution.py:45
  9.0 0.0 all-gather.3.cloned.1.call-update
  9.0 1.0 slice_bitcast_fusion
  10.0 4.5 %collective-permute-start = (bf16[4,64,256]{2,1,0:T(8,128)(2,1)S(1)}, bf16[4,64,256]{2,1,0:T(8,128)(2,1)S(1)}, u32[]{:S(2)}, u32[]{:S(2)}) collective-permute-start(bf16[4,64,256]{2,1,0:T(8,128)(2,1)S(1)} %get-tuple-element.11), channel_id=1, source_target_pairs={{0,1},{1,2},{2,3},{3,4},{4,5},{5,6},{6,7},{8,9},{9,10},{10,11},{11... | collective-permute-start | bytes 393224 | tf_op jit(solution)/shard_map/ppermute | solution.py:280
  14.5 1.9 %collective-permute-start.1 = (bf16[4,64,256]{2,1,0:T(8,128)(2,1)S(1)}, bf16[4,64,256]{2,1,0:T(8,128)(2,1)S(1)}, u32[]{:S(2)}, u32[]{:S(2)}) collective-permute-start(bf16[4,64,256]{2,1,0:T(8,128)(2,1)S(1)} %get-tuple-element.10), channel_id=1, source_target_pairs={{1,0},{2,1},{3,2},{4,3},{5,4},{6,5},{7,6},{9,8},{10,9},{11,10},{12... | collective-permute-start | bytes 393224 | tf_op jit(solution)/shard_map/ppermute | solution.py:281
  16.5 0.0 copy-done.2
  16.6 4.2 %collective-permute-done.1.after_ref = bf16[4,64,256]{2,1,0:T(8,128)(2,1)S(1)} collective-permute-done((bf16[4,64,256]{2,1,0:T(8,128)(2,1)S(1)}, bf16[4,64,256]{2,1,0:T(8,128)(2,1)S(1)}, u32[]{:S(2)}, u32[]{:S(2)}) %collective-permute-start.1) | collective-permute-done | bytes 131104 | tf_op jit(solution)/shard_map/ppermute | solution.py:281
  20.8 0.0 collective-permute-done.before_ref
  20.9 0.2 fusion
  21.0 0.0 copy-start.5
  21.0 0.0 copy-start.6
  21.1 1.6 %broadcast_in_dim.4 = bf16[16,6,64,128]{3,2,1,0:T(8,128)(2,1)} broadcast(bf16[6,64,128]{2,1,0:T(8,128)(2,1)S(1)} %fusion), dimensions={1,2,3} | broadcast | bytes 1671168 | tf_op jit(solution)/shard_map/broadcast_in_dim | solution.py:286
  22.6 7.8 %all-to-all-start = ((bf16[16,6,64,128]{3,2,1,0:T(8,128)(2,1)}), bf16[16,6,64,128]{3,2,1,0:T(8,128)(2,1)S(1)}, u32[]{:S(2)}, u32[]{:S(2)}) async-start(bf16[16,6,64,128]{3,2,1,0:T(8,128)(2,1)} %broadcast_in_dim.4), calls=%async_computation | async-start | bytes 3145728 | tf_op jit(solution)/shard_map/all_to_all | solution.py:287
  30.4 0.0 copy-done.5
  30.4 0.6 dynamic_slice.7
  31.0 0.0 copy-done.6
  31.0 0.7 dynamic_slice.6
  31.7 1.4 pad_add_fusion.scalars_ref
  33.1 20.3 %all-to-all-done.mate_ref = bf16[16,6,64,128]{3,2,1,0:T(8,128)(2,1)S(1)} async-done(((bf16[16,6,64,128]{3,2,1,0:T(8,128)(2,1)}), bf16[16,6,64,128]{3,2,1,0:T(8,128)(2,1)S(1)}, u32[]{:S(2)}, u32[]{:S(2)}) %all-to-all-start) | async-done | bytes 1572896 | tf_op jit(solution)/shard_map/all_to_all | solution.py:287
  53.4 0.0 copy-start
  53.4 1.2 copy-done
  54.6 0.0 copy-start.1
  54.6 1.4 copy-done.1
  56.0 0.0 copy-start.3
  56.0 0.0 copy-start.4
  56.0 9.5 %filter_band.1 = (f32[16,64,256]{2,1,0:T(8,128)}, bf16[8192,128]{1,0:T(8,128)(2,1)S(1)}) custom-call(s32[4]{0:T(128)S(1)} %pad_add_fusion.scalars_ref, bf16[4,64,256]{2,1,0:T(8,128)(2,1)S(1)} %collective-permute-done.before_ref, bf16[16,64,256]{2,1,0:T(8,128)(2,1)S(1)} %bitcast.19, bf16[4,64,256]{2,1,0:T(8,128)(2,1)S(1)} %collective-permute-done.1.after_ref, ...), custom_call_target="tpu_custom_call" | custom-call | flops 2000000000 | bytes 6291456 | tf_op jit(solution)/shard_map/filter_band/pallas_call | solution.py:153
  65.5 47.7 %all-gather.3.cloned.1.call-done = bf16[83968,128]{1,0:T(8,128)(2,1)} async-done(((bf16[656,128]{1,0:T(8,128)(2,1)}), bf16[83968,128]{1,0:T(8,128)(2,1)}) %all-gather.3.cloned.1.call-update) | async-done | bytes 21495824 | tf_op jit(solution)/shard_map/all_gather | solution.py:275
  113.1 0.0 copy-done.3
  113.1 0.0 copy-done.4
  113.1 20.1 %classify.1 = f32[16,8]{1,0:T(8,128)S(1)} custom-call(s32[16]{0:T(128)S(1)} %copy-done.3, s32[16]{0:T(128)S(1)} %bitcast.20, bf16[256,32,128]{2,1,0:T(8,128)(2,1)S(1)} %bitcast.16, bf16[16,8,656,128]{3,2,1,0:T(8,128)(2,1)} %bitcast.21), custom_call_target="tpu_custom_call" | custom-call | flops 5500000256 | bytes 25165824 | tf_op jit(solution)/shard_map/classify/pallas_call | solution.py:242
  133.3 0.7 copy.11
  (4 shorter events, 0.1 us)
Async XLA Ops:
  7.2 9.3 %copy-start.2 = (bf16[1,16,64,256]{3,2,1,0:T(8,128)(2,1)S(1)}, bf16[1,16,64,256]{3,2,1,0:T(8,128)(2,1)}, u32[]{:S(2)}) copy-start(bf16[1,16,64,256]{3,2,1,0:T(8,128)(2,1)} %param.9) | copy-start | bytes 1572868
  7.2 106.0 %all-gather.3.cloned.1.call-start = ((), (), s32[]{:S(2)}) async-start(), calls=%async_computation.1 | async-start | bytes 21663744 | tf_op jit(solution)/shard_map/all_gather | solution.py:275
  10.0 10.8 %collective-permute-start = (bf16[4,64,256]{2,1,0:T(8,128)(2,1)S(1)}, bf16[4,64,256]{2,1,0:T(8,128)(2,1)S(1)}, u32[]{:S(2)}, u32[]{:S(2)}) collective-permute-start(bf16[4,64,256]{2,1,0:T(8,128)(2,1)S(1)} %get-tuple-element.11), channel_id=1, source_target_pairs={{0,1},{1,2},{2,3},{3,4},{4,5},{5,6},{6,7},{8,9},{9,10},{10,11},{11... | collective-permute-start | bytes 393224 | tf_op jit(solution)/shard_map/ppermute | solution.py:280
  14.5 6.3 %collective-permute-start.1 = (bf16[4,64,256]{2,1,0:T(8,128)(2,1)S(1)}, bf16[4,64,256]{2,1,0:T(8,128)(2,1)S(1)}, u32[]{:S(2)}, u32[]{:S(2)}) collective-permute-start(bf16[4,64,256]{2,1,0:T(8,128)(2,1)S(1)} %get-tuple-element.10), channel_id=1, source_target_pairs={{1,0},{2,1},{3,2},{4,3},{5,4},{6,5},{7,6},{9,8},{10,9},{11,10},{12... | collective-permute-start | bytes 393224 | tf_op jit(solution)/shard_map/ppermute | solution.py:281
  21.0 9.4 %copy-start.5 = (s32[16]{0:T(128)S(1)}, s32[16]{0:T(128)}, u32[]{:S(2)}) copy-start(s32[16]{0:T(128)} %param.11) | copy-start | bytes 196
  21.0 10.0 %copy-start.6 = (s32[16]{0:T(128)S(1)}, s32[16]{0:T(128)}, u32[]{:S(2)}) copy-start(s32[16]{0:T(128)} %param.10) | copy-start | bytes 196
  22.6 30.7 %all-to-all-start = ((bf16[16,6,64,128]{3,2,1,0:T(8,128)(2,1)}), bf16[16,6,64,128]{3,2,1,0:T(8,128)(2,1)S(1)}, u32[]{:S(2)}, u32[]{:S(2)}) async-start(bf16[16,6,64,128]{3,2,1,0:T(8,128)(2,1)} %broadcast_in_dim.4), calls=%async_computation | async-start | bytes 3145728 | tf_op jit(solution)/shard_map/all_to_all | solution.py:287
  53.4 1.2 copy-start
  54.6 1.4 %copy-start.1 = (bf16[16,6,64,128]{3,2,1,0:T(8,128)(2,1)S(1)}, bf16[16,6,64,128]{3,2,1,0:T(8,128)(2,1)}, u32[]{:S(2)}) copy-start(bf16[16,6,64,128]{3,2,1,0:T(8,128)(2,1)} %copy-done) | copy-start | bytes 4718596
  56.0 57.2 %copy-start.3 = (s32[16]{0:T(128)S(1)}, s32[16]{0:T(128)}, u32[]{:S(2)}) copy-start(s32[16]{0:T(128)} %starts_ref.1) | copy-start | bytes 196
  56.0 57.2 %copy-start.4 = (s32[16,1]{0,1:T(1,128)S(1)}, s32[16,1]{0,1:T(1,128)}, u32[]{:S(2)}) copy-start(s32[16,1]{0,1:T(1,128)} %param.13) | copy-start | bytes 196
Sparse Core Ops, SparseCore 0:
  11.0 102.1 all-gather.2

commit v2 on v1

--- a/solution.py
+++ b/solution.py
@@ -11,6 +11,7 @@
 OV = 32
 CX = 64
 RADIUS = 3
+TOGETHER = 4
 HALO = 4
 F32 = jnp.float32
 BF16 = jnp.bfloat16
@@ -184,87 +185,107 @@
     )(scalars, before, own, after, mates)
 
 
-def classify_kernel(starts_ref, route_ref, table_ref, weight_ref, out_ref, score_ref):
-    i = pl.program_id(0)
-    begin = starts_ref[i]
-
-    def rows_of(part, at, count):
-        return weight_ref[0, part, pl.ds(at, count), :]
-
-    def joined_lanes(parts, at, count):
-        halves = [
-            jnp.concatenate([rows_of(p, at + h * count, count) for p in parts], axis=0)
-            for h in range(2)
-        ]
-        return jnp.concatenate(halves, axis=1)
-
-    hidden = None
-    for half in range(2):
-        patches = jnp.concatenate(
-            [
-                jnp.concatenate(
-                    [table_ref[begin + 8 * c + 4 * half + 2 * j] for j in range(2)], axis=1
+def classify_kernel(starts_ref, route_ref, table_ref, weight_ref, out_ref, held_ref, sem):
+    count = out_ref.shape[1]
+
+    def fetch(i):
+        return pltpu.make_async_copy(weight_ref.at[route_ref[i]], held_ref.at[i], sem.at[i])
+
+    for i in range(count):
+        fetch(i).start()
+    each = range(TOGETHER)
+    lane = lax.broadcasted_iota(jnp.int32, (8, count), 1)
+
+    def group(g, kept):
+        first = TOGETHER * g
+        for k in each:
+            fetch(first + k).wait()
+
+        def rows_of(k, part, at, rows):
+            return held_ref[first + k, part, pl.ds(at, rows), :]
+
+        def joined_lanes(k, parts, at, rows):
+            halves = [
+                jnp.concatenate([rows_of(k, p, at + h * rows, rows) for p in parts], axis=0)
+                for h in range(2)
+            ]
+            return jnp.concatenate(halves, axis=1)
+
+        hidden = [None] * TOGETHER
+        for half in range(2):
+            for k in each:
+                begin = starts_ref[first + k]
+                patches = jnp.concatenate(
+                    [
+                        jnp.concatenate(
+                            [table_ref[begin + 8 * c + 4 * half + 2 * j] for j in range(2)], axis=1
+                        )
+                        for c in range(8)
+                    ],
+                    axis=0,
                 )
-                for c in range(8)
-            ],
-            axis=0,
-        )
-        stem = joined_lanes(range(4 * half, 4 * half + 4), 0, 64)
-        term = jnp.dot(patches, stem, preferred_element_type=F32)
-        hidden = term if hidden is None else hidden + term
-    wide = hidden.astype(BF16).astype(F32)
-    power = jnp.mean(wide * wide, axis=-1, keepdims=True)
-    normed = (wide * lax.rsqrt(power + 1e-05)).astype(BF16)
-    total = wide
-    for pair in range(4):
-        parts = (2 * pair, 2 * pair + 1)
-        expand = jnp.concatenate([rows_of(p, EXPAND_AT, 256) for p in parts], axis=1)
-        up = jnp.dot(normed, expand, preferred_element_type=F32)
-        up = jnp.maximum(up, 0.0).astype(BF16)
-        shrink = joined_lanes(parts, SHRINK_AT, 128)
-        total = total + jnp.dot(up, shrink, preferred_element_type=F32)
-    last = total.astype(BF16).astype(F32)
-    pooled = jnp.sum(last, axis=0, keepdims=True) * (1.0 / last.shape[0])
-    head = rows_of(0, HEAD_AT, 16).astype(F32)
-    products = head[:8] * pooled[:, :128] + head[8:] * pooled[:, 128:]
-    scores = jnp.sum(products, axis=1, keepdims=True)
-    lane = lax.broadcasted_iota(jnp.int32, (8, 128), 1)
-    score_ref[...] = jnp.where(lane == i, scores, score_ref[...])
-
-    @pl.when(i == pl.num_programs(0) - 1)
-    def _():
-        out_ref[...] = score_ref[...].T[: out_ref.shape[0], :]
+                stem = joined_lanes(k, range(4 * half, 4 * half + 4), 0, 64)
+                term = jnp.dot(patches, stem, preferred_element_type=F32)
+                hidden[k] = term if half == 0 else hidden[k] + term
+        total = [hidden[k].astype(BF16).astype(F32) for k in each]
+        normed = []
+        for k in each:
+            power = jnp.mean(total[k] * total[k], axis=-1, keepdims=True)
+            normed.append((total[k] * lax.rsqrt(power + 1e-05)).astype(BF16))
+        for pair in range(4):
+            parts = (2 * pair, 2 * pair + 1)
+            up = []
+            for k in each:
+                expand = jnp.concatenate([rows_of(k, p, EXPAND_AT, 256) for p in parts], axis=1)
+                wide = jnp.dot(normed[k], expand, preferred_element_type=F32)
+                up.append(jnp.maximum(wide, 0.0).astype(BF16))
+            for k in each:
+                shrink = joined_lanes(k, parts, SHRINK_AT, 128)
+                total[k] = total[k] + jnp.dot(up[k], shrink, preferred_element_type=F32)
+        for k in each:
+            last = total[k].astype(BF16).astype(F32)
+            pooled = jnp.sum(last, axis=0, keepdims=True) * (1.0 / last.shape[0])
+            head = rows_of(k, 0, HEAD_AT, 16).astype(F32)
+            products = head[:8] * pooled[:, :128] + head[8:] * pooled[:, 128:]
+            scores = jnp.sum(products, axis=1, keepdims=True)
+            kept = jnp.where(lane == first + k, scores, kept)
+        return kept
+
+    out_ref[...] = lax.fori_loop(0, count // TOGETHER, group, jnp.zeros((8, count), F32))
 
 
 def classify(starts, routes, table, weights):
     count = starts.shape[0]
-    parts = weights.shape[1]
-    return pl.pallas_call(
+    scores = pl.pallas_call(
         classify_kernel,
-        out_shape=jax.ShapeDtypeStruct((count, 8), F32),
-        grid_spec=pltpu.PrefetchScalarGridSpec(
-            num_scalar_prefetch=2,
-            grid=(count,),
-            in_specs=[
-                pl.BlockSpec(table.shape, lambda i, s, r: (0, 0, 0)),
-                pl.BlockSpec((1, parts, PART_ROWS, 128), lambda i, s, r: (r[i], 0, 0, 0)),
-            ],
-            out_specs=pl.BlockSpec((count, 8), lambda i, s, r: (0, 0)),
-            scratch_shapes=[pltpu.VMEM((8, 128), F32)],
-        ),
-        compiler_params=pltpu.CompilerParams(vmem_limit_bytes=40 << 20),
+        out_shape=jax.ShapeDtypeStruct((8, count), F32),
+        in_specs=[
+            pl.BlockSpec(memory_space=pltpu.SMEM),
+            pl.BlockSpec(memory_space=pltpu.SMEM),
+            pl.BlockSpec(memory_space=pltpu.VMEM),
+            pl.BlockSpec(memory_space=pl.ANY),
+        ],
+        out_specs=pl.BlockSpec(memory_space=pltpu.VMEM),
+        scratch_shapes=[
+            pltpu.VMEM((count,) + weights.shape[1:], BF16),
+            pltpu.SemaphoreType.DMA((count,)),
+        ],
+        compiler_params=pltpu.CompilerParams(vmem_limit_bytes=48 << 20),
         cost_estimate=pl.CostEstimate(
             flops=5_500_000_000, bytes_accessed=24 << 20, transcendentals=4096
         ),
         name="classify",
     )(starts, routes, table, weights)
+    return scores.T
 
 
 def body(
     volume, partner, offsets, starts, classifier, stem_weight, expand_weight, shrink_weight, head_weight
 ):
-    tile_me, slab_me = lax.axis_index("tile"), lax.axis_index("slab")
-    tiles, slabs = lax.axis_size("tile"), lax.axis_size("slab")
+    lines, posts = lax.axis_size("line"), lax.axis_size("post")
+    tiles, slabs = lines * posts, lax.axis_size("slab")
+    line_me, post_me = lax.axis_index("line"), lax.axis_index("post")
+    tile_me, slab_me = line_me * posts + post_me, lax.axis_index("slab")
     own = volume[0]
     planes, rows, width = own.shape
 
@@ -272,7 +293,7 @@
         jnp.reshape(slab_me, (1,)).astype(jnp.int32),
         stem_weight[0], expand_weight[0, 0], shrink_weight[0, 0], head_weight[0].T,
     )
-    weights = lax.all_gather(part, ("tile", "slab"), axis=0, tiled=False)
+    weights = lax.all_gather(part, ("line", "post", "slab"), axis=0, tiled=False)
     weights = weights.reshape(tiles, slabs, PART_ROWS, 128)
 
     up = [(i, i + 1) for i in range(slabs - 1)]
@@ -283,10 +304,15 @@
     group = (planes + 2 * HALO) // 4
     strip = jnp.concatenate([before[:, :, :OV], own[:, :, :OV], after[:, :, :OV]], axis=0)
     strip = jnp.concatenate([strip[q * group : (q + 1) * group] for q in range(4)], axis=2)
-    sent = jnp.broadcast_to(strip[None], (tiles,) + strip.shape)
-    mates = lax.all_to_all(sent, "tile", split_axis=0, concat_axis=0, tiled=True)
-
-    scalars = jnp.stack([partner[tile_me], offsets[tile_me], slab_me, jnp.int32(slabs)])
+    sent = jnp.broadcast_to(strip[None], (posts,) + strip.shape)
+    met = lax.all_to_all(sent, "post", split_axis=0, concat_axis=0, tiled=True)
+    wanted = [partner[line * posts + post_me] % posts for line in range(lines)]
+    sent = jnp.stack([lax.dynamic_index_in_dim(met, w, 0, keepdims=False) for w in wanted])
+    mates = lax.all_to_all(sent, "line", split_axis=0, concat_axis=0, tiled=True)
+
+    scalars = jnp.stack(
+        [partner[tile_me] // posts, offsets[tile_me], slab_me, jnp.int32(slabs)]
+    )
     log_response, table = filter_band(scalars, before, own, after, mates)
     table = table.reshape(width, -1, 128)
     logits = classify(starts, classifier[:, 0], table, weights)
@@ -294,20 +320,27 @@
 
 
 def solution(mesh):
+    tiles, slabs = mesh.devices.shape
+    posts = 4 if tiles % 4 == 0 else 1
+    split = jax.sharding.Mesh(
+        mesh.devices.reshape(tiles // posts, posts, slabs), ("line", "post", "slab")
+    )
+    tile = ("line", "post")
+    both = ("line", "post", "slab")
     return jax.shard_map(
         body,
-        mesh=mesh,
+        mesh=split,
         in_specs=(
-            P("tile", "slab", None, None),
+            P(tile, "slab", None, None),
             P(),
             P(),
-            P(("tile", "slab")),
-            P(("tile", "slab"), None),
-            P("tile", None, None),
-            P("tile", None, None, None),
-            P("tile", None, None, None),
-            P("tile", None, None),
-        ),
-        out_specs=(P("tile", "slab", None, None), P(("tile", "slab"), None)),
+            P(both),
+            P(both, None),
+            P(tile, None, None),
+            P(tile, None, None, None),
+            P(tile, None, None, None),
+            P(tile, None, None),
+        ),
+        out_specs=(P(tile, "slab", None, None), P(both, None)),
         check_vma=False,
     )

time: 141 us -> 125 us (0.89)
  waiting for transfers between devices: 72.2 us -> 50.2 us
  between operations: 14.2 us -> 24.3 us
  Pallas kernels: 31.4 us -> 23.9 us
  local copies, waits for them, and re-layouts: 7.24 us -> 8.93 us
  starting transfers between devices: 14.2 us -> 15.7 us
    all_to_all x1 -> x2, waiting for transfers between devices: 20.3 us -> 1.8 us  [the longest x1 1.79 us: body(): lax.all_to_all(sent, 'line', split_axis=0, concat_axis=0, tiled=True)]
    pallas_call x1, Pallas kernels: 20.1 us -> 12.7 us  [classify(): pl.pallas_call(classify_kernel, out_shape=jax.ShapeDtypeStruct((8, count)...]
    ppermute x1, waiting for transfers between devices: 4.25 us -> 2.42 us  [body(): after = lax.ppermute(own[:HALO], 'slab', down)]
    all_gather x1, waiting for transfers between devices: 47.7 us -> 46 us  [body(): lax.all_gather(part, ('line', 'post', 'slab'), axis=0, tiled=False)]
    all_to_all x1 -> x2, starting transfers between devices: 7.77 us -> 9.21 us  [the longest x1 5.03 us: body(): met = lax.all_to_all(sent, 'post', split_axis=0, concat_axis=0, tiled=True)]
    unnamed x15 -> x6, local copies, waits for them, and re-layouts: 3.3 us -> 2.35 us
  transfers between devices with their start and end apart: 4 -> 5, of which waited for: 3 -> 3; matrix products, arithmetic and copies ran while one was open for 4% -> 7% of each run, Pallas kernels for 7% -> 8%
where the time goes in v2:
time: 125 us
  waiting for transfers between devices  50.2 us (40%)
  between operations  24.3 us (19%)
  Pallas kernels  23.9 us (19%)
  starting transfers between devices  15.7 us (13%)
  local copies, waits for them, and re-layouts  8.93 us (7%)
  other arithmetic  1.66 us (1%)
    all_gather x1, waiting for transfers between devices, body(): lax.all_gather(part, ('line', 'post', 'slab'), axis=0, tiled=False)  46 us
    pallas_call x1, Pallas kernels, classify(): pl.pallas_call(classify_kernel, out_shape=jax.ShapeDtypeStruct((8, count)...  12.7 us
    pallas_call x1, Pallas kernels, filter_band(): pl.pallas_call(band_kernel, out_shape=(jax.ShapeDtypeStruct((planes, rows...  9.5 us
    all_to_all x1, starting transfers between devices, body(): met = lax.all_to_all(sent, 'post', split_axis=0, concat_axis=0, tiled=True)  5.03 us
    ppermute x1, starting transfers between devices, body(): before = lax.ppermute(own[planes - HALO:], 'slab', up)  4.51 us
    all_to_all x1, starting transfers between devices, body(): lax.all_to_all(sent, 'line', split_axis=0, concat_axis=0, tiled=True)  4.18 us
  transfers between devices with their start and end apart: 5, of which 3 were waited for; matrix products, arithmetic and copies ran while one was open for 7% of the time, Pallas kernels for 8%

profile of v2, /device:TPU:1, one launch (start us, length us, event | category | flops | bytes accessed | tf_op | source)
XLA Modules:
  0.0 124.7 jit_solution(16962070429726727864)
XLA Ops:
  7.2 0.0 all-gather.3.cloned.1.call-start
  7.2 1.7 %pack_part.1 = bf16[656,128]{1,0:T(8,128)(2,1)} custom-call(s32[1]{0:T(128)} %bitcast.2.part_ref, bf16[512,256]{1,0:T(8,128)(2,1)} %bitcast.31, bf16[256,1024]{1,0:T(8,128)(2,1)} %bitcast.29, bf16[1024,256]{1,0:T(8,128)(2,1)} %bitcast.30, bf16[8,256]{1,0:T(8,128)(2,1)} %bitcast.32), custom_call_target="tpu_custom_call" | custom-call | bytes 1048576 | tf_op jit(solution)/shard_map/pack_part/pallas_call | solution.py:46
  9.0 0.0 all-gather.3.cloned.1.call-update
  9.0 1.0 slice_bitcast_fusion
  10.0 4.5 %collective-permute-start = (bf16[4,64,256]{2,1,0:T(8,128)(2,1)S(1)}, bf16[4,64,256]{2,1,0:T(8,128)(2,1)S(1)}, u32[]{:S(2)}, u32[]{:S(2)}) collective-permute-start(bf16[4,64,256]{2,1,0:T(8,128)(2,1)S(1)} %get-tuple-element.9), channel_id=1, source_target_pairs={{0,1},{1,2},{2,3},{3,4},{4,5},{5,6},{6,7},{8,9},{9,10},{10,11},{11... | collective-permute-start | bytes 393224 | tf_op jit(solution)/shard_map/ppermute | solution.py:301
  14.5 1.9 %collective-permute-start.1 = (bf16[4,64,256]{2,1,0:T(8,128)(2,1)S(1)}, bf16[4,64,256]{2,1,0:T(8,128)(2,1)S(1)}, u32[]{:S(2)}, u32[]{:S(2)}) collective-permute-start(bf16[4,64,256]{2,1,0:T(8,128)(2,1)S(1)} %get-tuple-element.8), channel_id=1, source_target_pairs={{1,0},{2,1},{3,2},{4,3},{5,4},{6,5},{7,6},{9,8},{10,9},{11,10},{12... | collective-permute-start | bytes 393224 | tf_op jit(solution)/shard_map/ppermute | solution.py:302
  16.4 1.0 slice.49
  17.4 1.0 fusion.3
  18.4 2.4 %collective-permute-done.1.after_ref = bf16[4,64,256]{2,1,0:T(8,128)(2,1)S(1)} collective-permute-done((bf16[4,64,256]{2,1,0:T(8,128)(2,1)S(1)}, bf16[4,64,256]{2,1,0:T(8,128)(2,1)S(1)}, u32[]{:S(2)}, u32[]{:S(2)}) %collective-permute-start.1) | collective-permute-done | bytes 131104 | tf_op jit(solution)/shard_map/ppermute | solution.py:302
  20.8 0.0 collective-permute-done.before_ref
  20.8 0.2 fusion
  21.0 0.8 broadcast_in_dim.4
  21.8 5.0 %all-to-all-start = ((bf16[4,6,64,128]{3,2,1,0:T(8,128)(2,1)}), bf16[4,6,64,128]{3,2,1,0:T(8,128)(2,1)S(1)}, u32[]{:S(2)}, u32[]{:S(2)}) async-start(bf16[4,6,64,128]{3,2,1,0:T(8,128)(2,1)} %broadcast_in_dim.4), calls=%async_computation | async-start | bytes 786432 | tf_op jit(solution)/shard_map/all_to_all | solution.py:308
  26.8 1.5 %fusion.4 = (s32[1]{0:T(128)}, s32[1]{0:T(128)}, s32[1]{0:T(128)}, s32[1]{0:T(128)}, s32[1]{0:T(128)}) fusion(s32[16]{0:T(128)} %param.10, s32[]{:T(128)S(6)} %select_n.54, s32[]{:T(128)S(6)} %select_n.57, s32[]{:T(128)S(6)} %select_n.52, s32[]{:T(128)S(6)} %select_n.63, s32[]{:T(128)S(6)} %select_n.60), kind=kLoop, calls=%fused_computation.14 | loop fusion | bytes 60 | tf_op jit(solution)/shard_map/dynamic_slice | solution.py:309
  36.0 0.0 all-to-all-done
  36.0 0.8 pad_maximum_fusion
  36.8 4.2 %all-to-all-start.1 = ((bf16[4,6,64,128]{3,2,1,0:T(8,128)(2,1)}), bf16[4,6,64,128]{3,2,1,0:T(8,128)(2,1)S(1)}, u32[]{:S(2)}, u32[]{:S(2)}) async-start(bf16[4,6,64,128]{3,2,1,0:T(8,128)(2,1)} %pad_maximum_fusion), calls=%async_computation.1 | async-start | bytes 786432 | tf_op jit(solution)/shard_map/all_to_all | solution.py:311
  42.9 1.3 %dynamic_slice.32 = s32[1]{0:T(128)} dynamic-slice(s32[16]{0:T(128)} %param.11, s32[]{:T(128)S(6)} %select_n.52), dynamic_slice_sizes={1} | dynamic-slice | bytes 12 | tf_op jit(solution)/shard_map/dynamic_slice | solution.py:314
  44.8 0.7 pad_add_fusion.scalars_ref
  45.5 1.8 %all-to-all-done.1.mate_ref = bf16[4,6,64,128]{3,2,1,0:T(8,128)(2,1)S(1)} async-done(((bf16[4,6,64,128]{3,2,1,0:T(8,128)(2,1)}), bf16[4,6,64,128]{3,2,1,0:T(8,128)(2,1)S(1)}, u32[]{:S(2)}, u32[]{:S(2)}) %all-to-all-start.1) | async-done | bytes 393248 | tf_op jit(solution)/shard_map/all_to_all | solution.py:311
  47.3 0.0 copy-start
  47.3 1.0 copy-done
  48.4 9.5 %filter_band.1 = (f32[16,64,256]{2,1,0:T(8,128)}, bf16[8192,128]{1,0:T(8,128)(2,1)S(1)}) custom-call(s32[4]{0:T(128)S(1)} %pad_add_fusion.scalars_ref, bf16[4,64,256]{2,1,0:T(8,128)(2,1)S(1)} %collective-permute-done.before_ref, bf16[16,64,256]{2,1,0:T(8,128)(2,1)S(1)} %bitcast.26, bf16[4,64,256]{2,1,0:T(8,128)(2,1)S(1)} %collective-permute-done.1.after_ref, ...), custom_call_target="tpu_custom_call" | custom-call | flops 2000000000 | bytes 6291456 | tf_op jit(solution)/shard_map/filter_band/pallas_call | solution.py:154
  57.9 46.0 %all-gather.3.cloned.1.call-done = bf16[83968,128]{1,0:T(8,128)(2,1)} async-done(((bf16[656,128]{1,0:T(8,128)(2,1)}), bf16[83968,128]{1,0:T(8,128)(2,1)}) %all-gather.3.cloned.1.call-update) | async-done | bytes 21495824 | tf_op jit(solution)/shard_map/all_gather | solution.py:296
  103.8 0.0 copy-start.1
  103.8 0.7 copy-done.1
  104.5 0.0 copy-start.2
  104.5 0.7 copy-done.2
  105.1 12.7 %classify.1 = f32[8,16]{1,0:T(8,128)} custom-call(s32[16]{0:T(128)S(1)} %copy-done.1, s32[16]{0:T(128)S(1)} %bitcast.27, bf16[256,32,128]{2,1,0:T(8,128)(2,1)S(1)} %bitcast.23, bf16[16,8,656,128]{3,2,1,0:T(8,128)(2,1)} %bitcast.28), custom_call_target="tpu_custom_call" | custom-call | flops 5500000256 | bytes 25165824 | tf_op jit(solution)/shard_map/classify/pallas_call | solution.py:259
  (3 shorter events, 0.1 us)
Async XLA Ops:
  7.2 96.7 %all-gather.3.cloned.1.call-start = ((), (), s32[]{:S(2)}) async-start(), calls=%async_computation.2 | async-start | bytes 21663744 | tf_op jit(solution)/shard_map/all_gather | solution.py:296
  10.0 10.8 %collective-permute-start = (bf16[4,64,256]{2,1,0:T(8,128)(2,1)S(1)}, bf16[4,64,256]{2,1,0:T(8,128)(2,1)S(1)}, u32[]{:S(2)}, u32[]{:S(2)}) collective-permute-start(bf16[4,64,256]{2,1,0:T(8,128)(2,1)S(1)} %get-tuple-element.9), channel_id=1, source_target_pairs={{0,1},{1,2},{2,3},{3,4},{4,5},{5,6},{6,7},{8,9},{9,10},{10,11},{11... | collective-permute-start | bytes 393224 | tf_op jit(solution)/shard_map/ppermute | solution.py:301
  14.5 6.3 %collective-permute-start.1 = (bf16[4,64,256]{2,1,0:T(8,128)(2,1)S(1)}, bf16[4,64,256]{2,1,0:T(8,128)(2,1)S(1)}, u32[]{:S(2)}, u32[]{:S(2)}) collective-permute-start(bf16[4,64,256]{2,1,0:T(8,128)(2,1)S(1)} %get-tuple-element.8), channel_id=1, source_target_pairs={{1,0},{2,1},{3,2},{4,3},{5,4},{6,5},{7,6},{9,8},{10,9},{11,10},{12... | collective-permute-start | bytes 393224 | tf_op jit(solution)/shard_map/ppermute | solution.py:302
  21.8 14.1 %all-to-all-start = ((bf16[4,6,64,128]{3,2,1,0:T(8,128)(2,1)}), bf16[4,6,64,128]{3,2,1,0:T(8,128)(2,1)S(1)}, u32[]{:S(2)}, u32[]{:S(2)}) async-start(bf16[4,6,64,128]{3,2,1,0:T(8,128)(2,1)} %broadcast_in_dim.4), calls=%async_computation | async-start | bytes 786432 | tf_op jit(solution)/shard_map/all_to_all | solution.py:308
  36.8 10.5 %all-to-all-start.1 = ((bf16[4,6,64,128]{3,2,1,0:T(8,128)(2,1)}), bf16[4,6,64,128]{3,2,1,0:T(8,128)(2,1)S(1)}, u32[]{:S(2)}, u32[]{:S(2)}) async-start(bf16[4,6,64,128]{3,2,1,0:T(8,128)(2,1)} %pad_maximum_fusion), calls=%async_computation.1 | async-start | bytes 786432 | tf_op jit(solution)/shard_map/all_to_all | solution.py:311
  47.3 1.0 copy-start
  103.8 0.7 copy-start.1
  104.5 0.7 copy-start.2
Sparse Core Ops, SparseCore 0:
  11.0 92.8 all-gather.2

commit v3 on v2

--- a/solution.py
+++ b/solution.py
@@ -30,37 +30,47 @@
     return [value / summed for value in weights_raw]
 
 
-def pack_kernel(part_ref, stem_ref, expand_ref, shrink_ref, head_ref, out_ref, wide_ref):
+def pack_kernel(core_ref, stem_ref, expand_ref, shrink_ref, head_ref, *refs):
+    out_refs, wide_ref = refs[:2], refs[2]
+    head = jnp.concatenate(
+        [head_ref[:, :128].astype(F32), head_ref[:, 128:].astype(F32)], axis=0
+    ).astype(BF16)
     for half in range(2):
         lanes = pl.ds(128 * half, 128)
         wide_ref[...] = stem_ref[:, lanes].astype(F32)
-        out_ref[pl.ds(64 * half, 64), :] = wide_ref[pl.ds(part_ref[0], 64, stride=8), :].astype(BF16)
-        out_ref[pl.ds(SHRINK_AT + 128 * half, 128), :] = shrink_ref[:, lanes]
-    out_ref[pl.ds(EXPAND_AT, 256), :] = expand_ref[...]
-    out_ref[pl.ds(HEAD_AT, 16), :] = jnp.concatenate(
-        [head_ref[:, :128].astype(F32), head_ref[:, 128:].astype(F32)], axis=0
-    ).astype(BF16)
-
-
-def pack_part(part, stem, expand, shrink, head):
+        for local in range(4):
+            out_ref, q = out_refs[local // 2], local % 2
+            rows = pl.ds(4 * core_ref[0] + local, 64, stride=8)
+            out_ref[q, pl.ds(64 * half, 64), :] = wide_ref[rows, :].astype(BF16)
+            out_ref[q, pl.ds(SHRINK_AT + 128 * half, 128), :] = shrink_ref[
+                pl.ds(128 * local, 128), lanes
+            ]
+    for local in range(4):
+        out_ref, q = out_refs[local // 2], local % 2
+        out_ref[q, pl.ds(EXPAND_AT, 256), :] = expand_ref[:, pl.ds(128 * local, 128)]
+        out_ref[q, pl.ds(HEAD_AT, 16), :] = head
+
+
+def pack_parts(core, stem, expand, shrink, head):
+    whole = pl.BlockSpec((2, PART_ROWS, 128), lambda i, c: (0, 0, 0))
     return pl.pallas_call(
         pack_kernel,
-        out_shape=jax.ShapeDtypeStruct((PART_ROWS, 128), BF16),
+        out_shape=(jax.ShapeDtypeStruct((2, PART_ROWS, 128), BF16),) * 2,
         grid_spec=pltpu.PrefetchScalarGridSpec(
             num_scalar_prefetch=1,
             grid=(1,),
             in_specs=[
-                pl.BlockSpec((512, 256), lambda i, p: (0, 0)),
-                pl.BlockSpec((256, 128), lambda i, p: (0, p[0])),
-                pl.BlockSpec((128, 256), lambda i, p: (p[0], 0)),
-                pl.BlockSpec((8, 256), lambda i, p: (0, 0)),
+                pl.BlockSpec((512, 256), lambda i, c: (0, 0)),
+                pl.BlockSpec((256, 512), lambda i, c: (0, c[0])),
+                pl.BlockSpec((512, 256), lambda i, c: (c[0], 0)),
+                pl.BlockSpec((8, 256), lambda i, c: (0, 0)),
             ],
-            out_specs=pl.BlockSpec((PART_ROWS, 128), lambda i, p: (0, 0)),
+            out_specs=(whole, whole),
             scratch_shapes=[pltpu.VMEM((512, 128), F32)],
         ),
-        cost_estimate=pl.CostEstimate(flops=0, bytes_accessed=1 << 20, transcendentals=0),
-        name="pack_part",
-    )(part, stem, expand, shrink, head)
+        cost_estimate=pl.CostEstimate(flops=0, bytes_accessed=2 << 20, transcendentals=0),
+        name="pack_parts",
+    )(core, stem, expand, shrink, head)
 
 
 def band_kernel(
@@ -185,21 +195,43 @@
     )(scalars, before, own, after, mates)
 
 
-def classify_kernel(starts_ref, route_ref, table_ref, weight_ref, out_ref, held_ref, sem):
+def classify_kernel(starts_ref, place_ref, table_ref, *refs):
+    weight_refs, (out_ref, held_ref, sem) = refs[:16], refs[16:]
     count = out_ref.shape[1]
-
-    def fetch(i):
-        return pltpu.make_async_copy(weight_ref.at[route_ref[i]], held_ref.at[i], sem.at[i])
-
-    for i in range(count):
-        fetch(i).start()
+    core = place_ref[8, 0]
+
+    def copy(source, k, i, piece):
+        holder = core if piece < 2 else 1 - core
+        parts = pl.ds(4 * holder + 2 * (piece % 2), 2)
+        return pltpu.make_async_copy(
+            weight_refs[4 * piece + source].at[k], held_ref.at[i, parts], sem.at[i, piece]
+        )
+
+    def start(i, carry):
+        for piece in range(4):
+            chosen, k = place_ref[2 * piece, i], place_ref[2 * piece + 1, i]
+            for source in range(4):
+
+                @pl.when(chosen == source)
+                def _():
+                    copy(source, k, i, piece).start()
+
+        return carry
+
+    lax.fori_loop(0, 2 * TOGETHER, start, 0)
     each = range(TOGETHER)
     lane = lax.broadcasted_iota(jnp.int32, (8, count), 1)
 
     def group(g, kept):
         first = TOGETHER * g
+
+        @pl.when(first + 2 * TOGETHER < count)
+        def _():
+            lax.fori_loop(first + 2 * TOGETHER, first + 3 * TOGETHER, start, 0)
+
         for k in each:
-            fetch(first + k).wait()
+            for piece in range(4):
+                copy(0, 0, first + k, piece).wait()
 
         def rows_of(k, part, at, rows):
             return held_ref[first + k, part, pl.ds(at, rows), :]
@@ -254,7 +286,7 @@
     out_ref[...] = lax.fori_loop(0, count // TOGETHER, group, jnp.zeros((8, count), F32))
 
 
-def classify(starts, routes, table, weights):
+def classify(starts, place, table, weights):
     count = starts.shape[0]
     scores = pl.pallas_call(
         classify_kernel,
@@ -263,43 +295,63 @@
             pl.BlockSpec(memory_space=pltpu.SMEM),
             pl.BlockSpec(memory_space=pltpu.SMEM),
             pl.BlockSpec(memory_space=pltpu.VMEM),
-            pl.BlockSpec(memory_space=pl.ANY),
-        ],
+        ]
+        + [pl.BlockSpec(memory_space=pl.ANY)] * len(weights),
         out_specs=pl.BlockSpec(memory_space=pltpu.VMEM),
         scratch_shapes=[
-            pltpu.VMEM((count,) + weights.shape[1:], BF16),
-            pltpu.SemaphoreType.DMA((count,)),
+            pltpu.VMEM((count, 8, PART_ROWS, 128), BF16),
+            pltpu.SemaphoreType.DMA((count, 4)),
         ],
         compiler_params=pltpu.CompilerParams(vmem_limit_bytes=48 << 20),
         cost_estimate=pl.CostEstimate(
             flops=5_500_000_000, bytes_accessed=24 << 20, transcendentals=4096
         ),
         name="classify",
-    )(starts, routes, table, weights)
+    )(starts, place, table, *weights)
     return scores.T
+
+
+def ring(value, axis):
+    size = lax.axis_size(axis)
+    pairs = []
+    for i in range(size):
+        pairs.append((2 * i, 2 * ((i + 1) % size)))
+        pairs.append((2 * i + 1, 2 * ((i - 1) % size) + 1))
+    return lax.ppermute(value, (axis, "core"), pairs)
+
+
+def around(value, axis):
+    values = [value]
+    for _ in range(lax.axis_size(axis) - 1):
+        values.append(ring(values[-1], axis))
+    return values
 
 
 def body(
     volume, partner, offsets, starts, classifier, stem_weight, expand_weight, shrink_weight, head_weight
 ):
     lines, posts = lax.axis_size("line"), lax.axis_size("post")
-    tiles, slabs = lines * posts, lax.axis_size("slab")
     line_me, post_me = lax.axis_index("line"), lax.axis_index("post")
-    tile_me, slab_me = line_me * posts + post_me, lax.axis_index("slab")
+    slab_axes = ("column", "core")
+    slabs, slab_me = lax.axis_size(slab_axes), lax.axis_index(slab_axes)
+    tile_me, core_me = line_me * posts + post_me, lax.axis_index("core")
     own = volume[0]
     planes, rows, width = own.shape
 
-    part = pack_part(
-        jnp.reshape(slab_me, (1,)).astype(jnp.int32),
+    first, second = pack_parts(
+        jnp.reshape(core_me, (1,)).astype(jnp.int32),
         stem_weight[0], expand_weight[0, 0], shrink_weight[0, 0], head_weight[0].T,
     )
-    weights = lax.all_gather(part, ("line", "post", "slab"), axis=0, tiled=False)
-    weights = weights.reshape(tiles, slabs, PART_ROWS, 128)
+    stream_a = around(jnp.stack(around(first, "post")), "line")
+    stream_b = around(jnp.stack(around(second, "line")), "post")
+    swap = [(0, 1), (1, 0)]
+    weights = stream_a + stream_b
+    weights = weights + [lax.ppermute(value, "core", swap) for value in weights]
 
     up = [(i, i + 1) for i in range(slabs - 1)]
     down = [(j, i) for i, j in up]
-    before = lax.ppermute(own[planes - HALO :], "slab", up)
-    after = lax.ppermute(own[:HALO], "slab", down)
+    before = lax.ppermute(own[planes - HALO :], slab_axes, up)
+    after = lax.ppermute(own[:HALO], slab_axes, down)
 
     group = (planes + 2 * HALO) // 4
     strip = jnp.concatenate([before[:, :, :OV], own[:, :, :OV], after[:, :, :OV]], axis=0)
@@ -315,23 +367,35 @@
     )
     log_response, table = filter_band(scalars, before, own, after, mates)
     table = table.reshape(width, -1, 128)
-    logits = classify(starts, classifier[:, 0], table, weights)
+
+    routes = classifier[:, 0]
+    turn = 1 - 2 * core_me
+    by_line = (turn * (line_me - routes // posts)) % lines
+    by_post = (turn * (post_me - routes % posts)) % posts
+    other_line, other_post = (lines - by_line) % lines, (posts - by_post) % posts
+    place = jnp.stack(
+        [
+            by_line, by_post, by_post, by_line,
+            other_line, other_post, other_post, other_line,
+            jnp.broadcast_to(core_me, routes.shape),
+        ]
+    ).astype(jnp.int32)
+    logits = classify(starts, place, table, weights)
     return (log_response[None], logits)
 
 
 def solution(mesh):
     tiles, slabs = mesh.devices.shape
-    posts = 4 if tiles % 4 == 0 else 1
     split = jax.sharding.Mesh(
-        mesh.devices.reshape(tiles // posts, posts, slabs), ("line", "post", "slab")
+        mesh.devices.reshape(4, tiles // 4, slabs // 2, 2), ("line", "post", "column", "core")
     )
-    tile = ("line", "post")
-    both = ("line", "post", "slab")
+    tile, slab = ("line", "post"), ("column", "core")
+    both = tile + slab
     return jax.shard_map(
         body,
         mesh=split,
         in_specs=(
-            P(tile, "slab", None, None),
+            P(tile, slab, None, None),
             P(),
             P(),
             P(both),
@@ -341,6 +405,6 @@
             P(tile, None, None, None),
             P(tile, None, None),
         ),
-        out_specs=(P(tile, "slab", None, None), P(both, None)),
+        out_specs=(P(tile, slab, None, None), P(both, None)),
         check_vma=False,
     )

time: 125 us -> 149 us (1.19)
  starting transfers between devices: 15.7 us -> 64.5 us
  between operations: 24.3 us -> 11.1 us
  waiting for transfers between devices: 50.2 us -> 38.5 us
  local copies, waits for them, and re-layouts: 8.93 us -> 4.8 us
    ppermute x2 -> x22, starting transfers between devices: 6.43 us -> 56.1 us  [the longest x12 37 us: ring(): return lax.ppermute(value, (axis, 'core'), pairs)]
    all_gather x1 -> x0, waiting for transfers between devices: 46 us -> none  [body(): lax.all_gather(part, ('line', 'post', 'slab'), axis=0, tiled=False)]
    ppermute x2 -> x22, waiting for transfers between devices: 2.43 us -> 31.3 us  [the longest x12 27.1 us: ring(): return lax.ppermute(value, (axis, 'core'), pairs)]
    all_to_all x1, waiting for transfers between devices: 1.79 us -> 7.21 us  [body(): lax.all_to_all(sent, 'line', split_axis=0, concat_axis=0, tiled=True)]
  transfers between devices with their start and end apart: 5 -> 24, of which waited for: 3 -> 8; matrix products, arithmetic and copies ran while one was open for 7% -> 4% of each run, Pallas kernels for 8% -> 7%
where the time goes in v3:
time: 149 us; the launch traced here: 147 us
  starting transfers between devices  64.5 us (43%)
  waiting for transfers between devices  38.5 us (26%)
  Pallas kernels  25.2 us (17%)
  between operations  11.1 us (7%)
  local copies, waits for them, and re-layouts  4.8 us (3%)
  other arithmetic  3.1 us (2%)
    ppermute x12, starting transfers between devices, ring(): return lax.ppermute(value, (axis, 'core'), pairs)  37 us
    ppermute x12, waiting for transfers between devices, ring(): return lax.ppermute(value, (axis, 'core'), pairs)  27.1 us
    ppermute x8, starting transfers between devices, body(): weights = weights + [lax.ppermute(value, 'core', swap) for value in weights]  13.1 us
    pallas_call x1, Pallas kernels, classify(): pl.pallas_call(classify_kernel, out_shape=jax.ShapeDtypeStruct((8, count)...  12.7 us
    pallas_call x1, Pallas kernels, filter_band(): pl.pallas_call(band_kernel, out_shape=(jax.ShapeDtypeStruct((planes, rows...  10.4 us
    all_to_all x1, waiting for transfers between devices, body(): lax.all_to_all(sent, 'line', split_axis=0, concat_axis=0, tiled=True)  7.21 us
    all_to_all x1, starting transfers between devices, body(): lax.all_to_all(sent, 'line', split_axis=0, concat_axis=0, tiled=True)  4.28 us
    ppermute x1, waiting for transfers between devices, body(): after = lax.ppermute(own[:HALO], slab_axes, down)  4.16 us
  transfers between devices with their start and end apart: 24, of which 8 were waited for; matrix products, arithmetic and copies ran while one was open for 4% of the time, Pallas kernels for 7%

profile of v3, /device:TPU:1, one launch (start us, length us, event | category | flops | bytes accessed | tf_op | source)
XLA Modules:
  0.0 147.2 jit_solution(14854055226349795121)
XLA Ops:
  0.6 2.1 %pack_parts.1 = (bf16[2,656,128]{2,1,0:T(8,128)(2,1)}, bf16[2,656,128]{2,1,0:T(8,128)(2,1)}) custom-call(s32[1]{0:T(128)} %bitcast.13.core_ref, bf16[512,256]{1,0:T(8,128)(2,1)} %bitcast.63, bf16[256,1024]{1,0:T(8,128)(2,1)} %bitcast.53, bf16[1024,256]{1,0:T(8,128)(2,1)} %bitcast.54, bf16[8,256]{1,0:T(8,128)(2,1)} %bitcast.64), custom_call_target="tpu_custom_call" | custom-call | bytes 2097152 | tf_op jit(solution)/shard_map/pack_parts/pallas_call | solution.py:56
  2.8 4.6 %collective-permute-start.2 = (bf16[2,656,128]{2,1,0:T(8,128)(2,1)}, bf16[2,656,128]{2,1,0:T(8,128)(2,1)S(1)}, u32[]{:S(2)}, u32[]{:S(2)}) collective-permute-start(bf16[2,656,128]{2,1,0:T(8,128)(2,1)} %get-tuple-element.8), channel_id=1, source_target_pairs={{0,8},{1,25},{8,16},{9,1},{16,24},{17,9},{24,0},{25,17},{2,10},{3,... | collective-permute-start | bytes 1007624 | tf_op jit(solution)/shard_map/ppermute | solution.py:320
  7.4 2.7 %collective-permute-start.8 = (bf16[2,656,128]{2,1,0:T(8,128)(2,1)}, bf16[2,656,128]{2,1,0:T(8,128)(2,1)S(1)}, u32[]{:S(2)}, u32[]{:S(2)}) collective-permute-start(bf16[2,656,128]{2,1,0:T(8,128)(2,1)} %get-tuple-element.9), channel_id=1, source_target_pairs={{0,32},{1,97},{32,64},{33,1},{64,96},{65,33},{96,0},{97,65},{2,34}... | collective-permute-start | bytes 1007624 | tf_op jit(solution)/shard_map/ppermute | solution.py:320
  10.1 1.7 %collective-permute-done.2 = bf16[2,656,128]{2,1,0:T(8,128)(2,1)S(1)} collective-permute-done((bf16[2,656,128]{2,1,0:T(8,128)(2,1)}, bf16[2,656,128]{2,1,0:T(8,128)(2,1)S(1)}, u32[]{:S(2)}, u32[]{:S(2)}) %collective-permute-start.2) | collective-permute-done | bytes 335904 | tf_op jit(solution)/shard_map/ppermute | solution.py:320
  11.8 3.3 %collective-permute-start.3 = (bf16[2,656,128]{2,1,0:T(8,128)(2,1)S(1)}, bf16[2,656,128]{2,1,0:T(8,128)(2,1)S(1)}, u32[]{:S(2)}, u32[]{:S(2)}) collective-permute-start(bf16[2,656,128]{2,1,0:T(8,128)(2,1)S(1)} %collective-permute-done.2), channel_id=1, source_target_pairs={{0,8},{1,25},{8,16},{9,1},{16,24},{17,9},{24,0},{25,17},{2,10},{3,... | collective-permute-start | bytes 1007624 | tf_op jit(solution)/shard_map/ppermute | solution.py:320
  15.1 0.0 collective-permute-done.8
  15.1 2.4 %collective-permute-start.9 = (bf16[2,656,128]{2,1,0:T(8,128)(2,1)S(1)}, bf16[2,656,128]{2,1,0:T(8,128)(2,1)S(1)}, u32[]{:S(2)}, u32[]{:S(2)}) collective-permute-start(bf16[2,656,128]{2,1,0:T(8,128)(2,1)S(1)} %collective-permute-done.8), channel_id=1, source_target_pairs={{0,32},{1,97},{32,64},{33,1},{64,96},{65,33},{96,0},{97,65},{2,34}... | collective-permute-start | bytes 1007624 | tf_op jit(solution)/shard_map/ppermute | solution.py:320
  17.5 1.7 %collective-permute-done.3 = bf16[2,656,128]{2,1,0:T(8,128)(2,1)S(1)} collective-permute-done((bf16[2,656,128]{2,1,0:T(8,128)(2,1)S(1)}, bf16[2,656,128]{2,1,0:T(8,128)(2,1)S(1)}, u32[]{:S(2)}, u32[]{:S(2)}) %collective-permute-start.3) | collective-permute-done | bytes 335904 | tf_op jit(solution)/shard_map/ppermute | solution.py:320
  19.2 3.4 %collective-permute-start.4 = (bf16[2,656,128]{2,1,0:T(8,128)(2,1)S(1)}, bf16[2,656,128]{2,1,0:T(8,128)(2,1)S(1)}, u32[]{:S(2)}, u32[]{:S(2)}) collective-permute-start(bf16[2,656,128]{2,1,0:T(8,128)(2,1)S(1)} %collective-permute-done.3), channel_id=1, source_target_pairs={{0,8},{1,25},{8,16},{9,1},{16,24},{17,9},{24,0},{25,17},{2,10},{3,... | collective-permute-start | bytes 1007624 | tf_op jit(solution)/shard_map/ppermute | solution.py:320
  22.6 0.0 collective-permute-done.9
  22.6 2.1 %collective-permute-start.10 = (bf16[2,656,128]{2,1,0:T(8,128)(2,1)S(1)}, bf16[2,656,128]{2,1,0:T(8,128)(2,1)S(1)}, u32[]{:S(2)}, u32[]{:S(2)}) collective-permute-start(bf16[2,656,128]{2,1,0:T(8,128)(2,1)S(1)} %collective-permute-done.9), channel_id=1, source_target_pairs={{0,32},{1,97},{32,64},{33,1},{64,96},{65,33},{96,0},{97,65},{2,34}... | collective-permute-start | bytes 1007624 | tf_op jit(solution)/shard_map/ppermute | solution.py:320
  24.8 2.0 %collective-permute-done.4 = bf16[2,656,128]{2,1,0:T(8,128)(2,1)S(1)} collective-permute-done((bf16[2,656,128]{2,1,0:T(8,128)(2,1)S(1)}, bf16[2,656,128]{2,1,0:T(8,128)(2,1)S(1)}, u32[]{:S(2)}, u32[]{:S(2)}) %collective-permute-start.4) | collective-permute-done | bytes 335904 | tf_op jit(solution)/shard_map/ppermute | solution.py:320
  26.7 1.2 pad_maximum_fusion.refs_0_
  27.9 2.2 %collective-permute-start.5 = (bf16[4,2,656,128]{3,2,1,0:T(8,128)(2,1)S(1)}, bf16[4,2,656,128]{3,2,1,0:T(8,128)(2,1)S(1)}, u32[]{:S(2)}, u32[]{:S(2)}) collective-permute-start(bf16[4,2,656,128]{3,2,1,0:T(8,128)(2,1)S(1)} %pad_maximum_fusion.refs_0_), channel_id=1, source_target_pairs={{0,32},{1,97},{32,64},{33,1},{64,96},{65,33},{96,0},{97,65},{2,34}... | collective-permute-start | bytes 4030472 | tf_op jit(solution)/shard_map/ppermute | solution.py:320
  30.1 0.0 collective-permute-done.10
  30.1 0.2 pad_maximum_fusion.1.refs_4_
  30.3 3.2 %collective-permute-start.11 = (bf16[4,2,656,128]{3,2,1,0:T(8,128)(2,1)S(1)}, bf16[4,2,656,128]{3,2,1,0:T(8,128)(2,1)}, u32[]{:S(2)}, u32[]{:S(2)}) collective-permute-start(bf16[4,2,656,128]{3,2,1,0:T(8,128)(2,1)S(1)} %pad_maximum_fusion.1.refs_4_), channel_id=1, source_target_pairs={{0,8},{1,25},{8,16},{9,1},{16,24},{17,9},{24,0},{25,17},{2,10},{3,... | collective-permute-start | bytes 4030472 | tf_op jit(solution)/shard_map/ppermute | solution.py:320
  33.5 11.7 %collective-permute-done.5.refs_1_ = bf16[4,2,656,128]{3,2,1,0:T(8,128)(2,1)S(1)} collective-permute-done((bf16[4,2,656,128]{3,2,1,0:T(8,128)(2,1)S(1)}, bf16[4,2,656,128]{3,2,1,0:T(8,128)(2,1)S(1)}, u32[]{:S(2)}, u32[]{:S(2)}) %collective-permute-start.5) | collective-permute-done | bytes 1343520 | tf_op jit(solution)/shard_map/ppermute | solution.py:320
  45.2 3.4 %collective-permute-start.6 = (bf16[4,2,656,128]{3,2,1,0:T(8,128)(2,1)S(1)}, bf16[4,2,656,128]{3,2,1,0:T(8,128)(2,1)}, u32[]{:S(2)}, u32[]{:S(2)}) collective-permute-start(bf16[4,2,656,128]{3,2,1,0:T(8,128)(2,1)S(1)} %collective-permute-done.5.refs_1_), channel_id=1, source_target_pairs={{0,32},{1,97},{32,64},{33,1},{64,96},{65,33},{96,0},{97,65},{2,34}... | collective-permute-start | bytes 4030472 | tf_op jit(solution)/shard_map/ppermute | solution.py:320
  48.5 0.0 collective-permute-done.11.refs_5_
  48.5 3.1 %collective-permute-start.12 = (bf16[4,2,656,128]{3,2,1,0:T(8,128)(2,1)}, bf16[4,2,656,128]{3,2,1,0:T(8,128)(2,1)}, u32[]{:S(2)}, u32[]{:S(2)}) collective-permute-start(bf16[4,2,656,128]{3,2,1,0:T(8,128)(2,1)} %collective-permute-done.11.refs_5_), channel_id=1, source_target_pairs={{0,8},{1,25},{8,16},{9,1},{16,24},{17,9},{24,0},{25,17},{2,10},{3,... | collective-permute-start | bytes 4030472 | tf_op jit(solution)/shard_map/ppermute | solution.py:320
  51.6 4.2 %collective-permute-start = (bf16[4,64,256]{2,1,0:T(8,128)(2,1)S(1)}, bf16[4,64,256]{2,1,0:T(8,128)(2,1)S(1)}, u32[]{:S(2)}, u32[]{:S(2)}) collective-permute-start(bf16[4,64,256]{2,1,0:T(8,128)(2,1)S(1)} %get-tuple-element.17), channel_id=1, source_target_pairs={{0,1},{1,2},{2,3},{3,4},{4,5},{5,6},{6,7},{8,9},{9,10},{10,11},{11... | collective-permute-start | bytes 393224 | tf_op jit(solution)/shard_map/ppermute | solution.py:353
  55.8 1.9 %collective-permute-start.1 = (bf16[4,64,256]{2,1,0:T(8,128)(2,1)S(1)}, bf16[4,64,256]{2,1,0:T(8,128)(2,1)S(1)}, u32[]{:S(2)}, u32[]{:S(2)}) collective-permute-start(bf16[4,64,256]{2,1,0:T(8,128)(2,1)S(1)} %get-tuple-element.16), channel_id=1, source_target_pairs={{1,0},{2,1},{3,2},{4,3},{5,4},{6,5},{7,6},{9,8},{10,9},{11,10},{12... | collective-permute-start | bytes 393224 | tf_op jit(solution)/shard_map/ppermute | solution.py:354
  57.7 0.1 collective-permute-start.14
  57.8 0.0 collective-permute-done.before_ref
  57.8 0.5 collective-permute-start.18
  58.3 4.2 %collective-permute-done.1.after_ref = bf16[4,64,256]{2,1,0:T(8,128)(2,1)S(1)} collective-permute-done((bf16[4,64,256]{2,1,0:T(8,128)(2,1)S(1)}, bf16[4,64,256]{2,1,0:T(8,128)(2,1)S(1)}, u32[]{:S(2)}, u32[]{:S(2)}) %collective-permute-start.1) | collective-permute-done | bytes 131104 | tf_op jit(solution)/shard_map/ppermute | solution.py:354
  62.5 0.0 collective-permute-start.15
  62.5 0.9 collective-permute-done.6.refs_2_
  63.4 3.5 %collective-permute-start.7 = (bf16[4,2,656,128]{3,2,1,0:T(8,128)(2,1)}, bf16[4,2,656,128]{3,2,1,0:T(8,128)(2,1)}, u32[]{:S(2)}, u32[]{:S(2)}) collective-permute-start(bf16[4,2,656,128]{3,2,1,0:T(8,128)(2,1)} %collective-permute-done.6.refs_2_), channel_id=1, source_target_pairs={{0,32},{1,97},{32,64},{33,1},{64,96},{65,33},{96,0},{97,65},{2,34}... | collective-permute-start | bytes 4030472 | tf_op jit(solution)/shard_map/ppermute | solution.py:320
  67.0 0.0 collective-permute-done.12.refs_6_
  67.0 3.0 %collective-permute-start.13 = (bf16[4,2,656,128]{3,2,1,0:T(8,128)(2,1)}, bf16[4,2,656,128]{3,2,1,0:T(8,128)(2,1)}, u32[]{:S(2)}, u32[]{:S(2)}) collective-permute-start(bf16[4,2,656,128]{3,2,1,0:T(8,128)(2,1)} %collective-permute-done.12.refs_6_), channel_id=1, source_target_pairs={{0,8},{1,25},{8,16},{9,1},{16,24},{17,9},{24,0},{25,17},{2,10},{3,... | collective-permute-start | bytes 4030472 | tf_op jit(solution)/shard_map/ppermute | solution.py:320
  70.0 0.0 copy-start.8
  70.0 0.0 copy-start.10
  70.0 0.0 collective-permute-done.14.refs_8_
  70.1 2.4 %collective-permute-start.19 = (bf16[4,2,656,128]{3,2,1,0:T(8,128)(2,1)}, bf16[4,2,656,128]{3,2,1,0:T(8,128)(2,1)}, u32[]{:S(2)}, u32[]{:S(2)}) collective-permute-start(bf16[4,2,656,128]{3,2,1,0:T(8,128)(2,1)} %collective-permute-done.11.refs_5_), channel_id=1, source_target_pairs={{0,1},{1,0},{2,3},{3,2},{4,5},{5,4},{6,7},{7,6},{8,9},{9,8},{10,11... | collective-permute-start | bytes 4030472 | tf_op jit(solution)/shard_map/ppermute | solution.py:349
  72.4 0.0 collective-permute-done.18.refs_12_
  72.4 0.1 collective-permute-start.16
  72.6 0.0 collective-permute-done.15.refs_9_
  72.6 0.5 collective-permute-start.20
  73.0 9.1 %collective-permute-done.7.refs_3_ = bf16[4,2,656,128]{3,2,1,0:T(8,128)(2,1)} collective-permute-done((bf16[4,2,656,128]{3,2,1,0:T(8,128)(2,1)}, bf16[4,2,656,128]{3,2,1,0:T(8,128)(2,1)}, u32[]{:S(2)}, u32[]{:S(2)}) %collective-permute-start.7) | collective-permute-done | bytes 1343520 | tf_op jit(solution)/shard_map/ppermute | solution.py:320
  82.2 7.4 %collective-permute-start.17 = (bf16[4,2,656,128]{3,2,1,0:T(8,128)(2,1)}, bf16[4,2,656,128]{3,2,1,0:T(8,128)(2,1)}, u32[]{:S(2)}, u32[]{:S(2)}) collective-permute-start(bf16[4,2,656,128]{3,2,1,0:T(8,128)(2,1)} %collective-permute-done.7.refs_3_), channel_id=1, source_target_pairs={{0,1},{1,0},{2,3},{3,2},{4,5},{5,4},{6,7},{7,6},{8,9},{9,8},{10,11... | collective-permute-start | bytes 4030472 | tf_op jit(solution)/shard_map/ppermute | solution.py:349
  89.6 0.0 collective-permute-done.13.refs_7_
  89.6 2.1 %collective-permute-start.21 = (bf16[4,2,656,128]{3,2,1,0:T(8,128)(2,1)}, bf16[4,2,656,128]{3,2,1,0:T(8,128)(2,1)}, u32[]{:S(2)}, u32[]{:S(2)}) collective-permute-start(bf16[4,2,656,128]{3,2,1,0:T(8,128)(2,1)} %collective-permute-done.13.refs_7_), channel_id=1, source_target_pairs={{0,1},{1,0},{2,3},{3,2},{4,5},{5,4},{6,7},{7,6},{8,9},{9,8},{10,11... | collective-permute-start | bytes 4030472 | tf_op jit(solution)/shard_map/ppermute | solution.py:349
  91.8 0.2 fusion
  92.0 0.8 broadcast_in_dim.4
  92.8 4.1 %all-to-all-start = ((bf16[4,6,64,128]{3,2,1,0:T(8,128)(2,1)}), bf16[4,6,64,128]{3,2,1,0:T(8,128)(2,1)}, u32[]{:S(2)}, u32[]{:S(2)}) async-start(bf16[4,6,64,128]{3,2,1,0:T(8,128)(2,1)} %broadcast_in_dim.4), calls=%async_computation | async-start | bytes 786432 | tf_op jit(solution)/shard_map/all_to_all | solution.py:360
  96.9 0.0 copy-start.9
  97.0 0.7 fusion.10
  107.7 0.7 dynamic_slice.32
  108.4 0.0 all-to-all-done
  108.4 1.1 constant_dynamic-slice_fusion.3
  109.4 0.8 pad_maximum_fusion.2
  110.2 4.3 %all-to-all-start.1 = ((bf16[4,6,64,128]{3,2,1,0:T(8,128)(2,1)}), bf16[4,6,64,128]{3,2,1,0:T(8,128)(2,1)}, u32[]{:S(2)}, u32[]{:S(2)}) async-start(bf16[4,6,64,128]{3,2,1,0:T(8,128)(2,1)} %pad_maximum_fusion.2), calls=%async_computation.1 | async-start | bytes 786432 | tf_op jit(solution)/shard_map/all_to_all | solution.py:363
  114.6 0.8 pad_add_fusion.scalars_ref
  115.4 7.2 %all-to-all-done.1.mate_ref = bf16[4,6,64,128]{3,2,1,0:T(8,128)(2,1)} async-done(((bf16[4,6,64,128]{3,2,1,0:T(8,128)(2,1)}), bf16[4,6,64,128]{3,2,1,0:T(8,128)(2,1)}, u32[]{:S(2)}, u32[]{:S(2)}) %all-to-all-start.1) | async-done | bytes 393248 | tf_op jit(solution)/shard_map/all_to_all | solution.py:363
  122.6 10.4 %filter_band.1 = (f32[16,64,256]{2,1,0:T(8,128)}, bf16[8192,128]{1,0:T(8,128)(2,1)S(1)}) custom-call(s32[4]{0:T(128)S(1)} %pad_add_fusion.scalars_ref, bf16[4,64,256]{2,1,0:T(8,128)(2,1)S(1)} %collective-permute-done.before_ref, bf16[16,64,256]{2,1,0:T(8,128)(2,1)S(1)} %bitcast.52, bf16[4,64,256]{2,1,0:T(8,128)(2,1)S(1)} %collective-permute-done.1.after_ref, ...), custom_call_target="tpu_custom_call" | custom-call | flops 2000000000 | bytes 6291456 | tf_op jit(solution)/shard_map/filter_band/pallas_call | solution.py:164
  133.0 1.4 copy-done
  134.3 0.0 collective-permute-done.19.refs_13_
  134.3 0.0 collective-permute-done.16.refs_10_
  134.3 0.0 collective-permute-done.20.refs_14_
  134.3 0.0 collective-permute-done.17.refs_11_
  134.3 0.0 collective-permute-done.21.refs_15_
  134.4 12.7 %classify.1 = f32[8,16]{1,0:T(8,128)} custom-call(s32[16]{0:T(128)S(1)} %copy-done.2, s32[9,16]{1,0:T(8,128)S(1)} %stack.61.place_ref, bf16[256,32,128]{2,1,0:T(8,128)(2,1)} %bitcast.49, bf16[4,2,656,128]{3,2,1,0:T(8,128)(2,1)S(1)} %pad_maximum_fusion.refs_0_, bf16[4,2,656,128]{3,2,1,0:T(8,128)(2,1)S(1)} %collective-permute-done.5.refs_1_, ...), custom_call_target="tpu_custom_call" | custom-call | flops 5500000256 | bytes 25165824 | tf_op jit(solution)/shard_map/classify/pallas_call | solution.py:291
  (26 shorter events, 0.2 us)
Async XLA Ops:
  2.8 9.0 %collective-permute-start.2 = (bf16[2,656,128]{2,1,0:T(8,128)(2,1)}, bf16[2,656,128]{2,1,0:T(8,128)(2,1)S(1)}, u32[]{:S(2)}, u32[]{:S(2)}) collective-permute-start(bf16[2,656,128]{2,1,0:T(8,128)(2,1)} %get-tuple-element.8), channel_id=1, source_target_pairs={{0,8},{1,25},{8,16},{9,1},{16,24},{17,9},{24,0},{25,17},{2,10},{3,... | collective-permute-start | bytes 1007624 | tf_op jit(solution)/shard_map/ppermute | solution.py:320
  7.4 7.7 %collective-permute-start.8 = (bf16[2,656,128]{2,1,0:T(8,128)(2,1)}, bf16[2,656,128]{2,1,0:T(8,128)(2,1)S(1)}, u32[]{:S(2)}, u32[]{:S(2)}) collective-permute-start(bf16[2,656,128]{2,1,0:T(8,128)(2,1)} %get-tuple-element.9), channel_id=1, source_target_pairs={{0,32},{1,97},{32,64},{33,1},{64,96},{65,33},{96,0},{97,65},{2,34}... | collective-permute-start | bytes 1007624 | tf_op jit(solution)/shard_map/ppermute | solution.py:320
  11.8 7.4 %collective-permute-start.3 = (bf16[2,656,128]{2,1,0:T(8,128)(2,1)S(1)}, bf16[2,656,128]{2,1,0:T(8,128)(2,1)S(1)}, u32[]{:S(2)}, u32[]{:S(2)}) collective-permute-start(bf16[2,656,128]{2,1,0:T(8,128)(2,1)S(1)} %collective-permute-done.2), channel_id=1, source_target_pairs={{0,8},{1,25},{8,16},{9,1},{16,24},{17,9},{24,0},{25,17},{2,10},{3,... | collective-permute-start | bytes 1007624 | tf_op jit(solution)/shard_map/ppermute | solution.py:320
  15.1 7.5 %collective-permute-start.9 = (bf16[2,656,128]{2,1,0:T(8,128)(2,1)S(1)}, bf16[2,656,128]{2,1,0:T(8,128)(2,1)S(1)}, u32[]{:S(2)}, u32[]{:S(2)}) collective-permute-start(bf16[2,656,128]{2,1,0:T(8,128)(2,1)S(1)} %collective-permute-done.8), channel_id=1, source_target_pairs={{0,32},{1,97},{32,64},{33,1},{64,96},{65,33},{96,0},{97,65},{2,34}... | collective-permute-start | bytes 1007624 | tf_op jit(solution)/shard_map/ppermute | solution.py:320
  19.2 7.5 %collective-permute-start.4 = (bf16[2,656,128]{2,1,0:T(8,128)(2,1)S(1)}, bf16[2,656,128]{2,1,0:T(8,128)(2,1)S(1)}, u32[]{:S(2)}, u32[]{:S(2)}) collective-permute-start(bf16[2,656,128]{2,1,0:T(8,128)(2,1)S(1)} %collective-permute-done.3), channel_id=1, source_target_pairs={{0,8},{1,25},{8,16},{9,1},{16,24},{17,9},{24,0},{25,17},{2,10},{3,... | collective-permute-start | bytes 1007624 | tf_op jit(solution)/shard_map/ppermute | solution.py:320
  22.6 7.5 %collective-permute-start.10 = (bf16[2,656,128]{2,1,0:T(8,128)(2,1)S(1)}, bf16[2,656,128]{2,1,0:T(8,128)(2,1)S(1)}, u32[]{:S(2)}, u32[]{:S(2)}) collective-permute-start(bf16[2,656,128]{2,1,0:T(8,128)(2,1)S(1)} %collective-permute-done.9), channel_id=1, source_target_pairs={{0,32},{1,97},{32,64},{33,1},{64,96},{65,33},{96,0},{97,65},{2,34}... | collective-permute-start | bytes 1007624 | tf_op jit(solution)/shard_map/ppermute | solution.py:320
  26.7 3.4 %copy-start.7 = (bf16[2,656,128]{2,1,0:T(8,128)(2,1)S(1)}, bf16[2,656,128]{2,1,0:T(8,128)(2,1)}, u32[]{:S(2)}) copy-start(bf16[2,656,128]{2,1,0:T(8,128)(2,1)} %get-tuple-element.9) | copy-start | bytes 1007620
  27.9 17.3 %collective-permute-start.5 = (bf16[4,2,656,128]{3,2,1,0:T(8,128)(2,1)S(1)}, bf16[4,2,656,128]{3,2,1,0:T(8,128)(2,1)S(1)}, u32[]{:S(2)}, u32[]{:S(2)}) collective-permute-start(bf16[4,2,656,128]{3,2,1,0:T(8,128)(2,1)S(1)} %pad_maximum_fusion.refs_0_), channel_id=1, source_target_pairs={{0,32},{1,97},{32,64},{33,1},{64,96},{65,33},{96,0},{97,65},{2,34}... | collective-permute-start | bytes 4030472 | tf_op jit(solution)/shard_map/ppermute | solution.py:320
  30.1 21.5 %copy-start.1 = (bf16[1,16,64,256]{3,2,1,0:T(8,128)(2,1)S(1)}, bf16[1,16,64,256]{3,2,1,0:T(8,128)(2,1)}, u32[]{:S(2)}) copy-start(bf16[1,16,64,256]{3,2,1,0:T(8,128)(2,1)} %param.9) | copy-start | bytes 1572868
  30.3 42.3 %copy-start.3 = (bf16[4,2,656,128]{3,2,1,0:T(8,128)(2,1)}, bf16[4,2,656,128]{3,2,1,0:T(8,128)(2,1)S(1)}, u32[]{:S(2)}) copy-start(bf16[4,2,656,128]{3,2,1,0:T(8,128)(2,1)S(1)} %pad_maximum_fusion.1.refs_4_) | copy-start | bytes 4030468
  30.3 18.2 %collective-permute-start.11 = (bf16[4,2,656,128]{3,2,1,0:T(8,128)(2,1)S(1)}, bf16[4,2,656,128]{3,2,1,0:T(8,128)(2,1)}, u32[]{:S(2)}, u32[]{:S(2)}) collective-permute-start(bf16[4,2,656,128]{3,2,1,0:T(8,128)(2,1)S(1)} %pad_maximum_fusion.1.refs_4_), channel_id=1, source_target_pairs={{0,8},{1,25},{8,16},{9,1},{16,24},{17,9},{24,0},{25,17},{2,10},{3,... | collective-permute-start | bytes 4030472 | tf_op jit(solution)/shard_map/ppermute | solution.py:320
  45.2 18.3 %collective-permute-start.6 = (bf16[4,2,656,128]{3,2,1,0:T(8,128)(2,1)S(1)}, bf16[4,2,656,128]{3,2,1,0:T(8,128)(2,1)}, u32[]{:S(2)}, u32[]{:S(2)}) collective-permute-start(bf16[4,2,656,128]{3,2,1,0:T(8,128)(2,1)S(1)} %collective-permute-done.5.refs_1_), channel_id=1, source_target_pairs={{0,32},{1,97},{32,64},{33,1},{64,96},{65,33},{96,0},{97,65},{2,34}... | collective-permute-start | bytes 4030472 | tf_op jit(solution)/shard_map/ppermute | solution.py:320
  48.5 18.4 %collective-permute-start.12 = (bf16[4,2,656,128]{3,2,1,0:T(8,128)(2,1)}, bf16[4,2,656,128]{3,2,1,0:T(8,128)(2,1)}, u32[]{:S(2)}, u32[]{:S(2)}) collective-permute-start(bf16[4,2,656,128]{3,2,1,0:T(8,128)(2,1)} %collective-permute-done.11.refs_5_), channel_id=1, source_target_pairs={{0,8},{1,25},{8,16},{9,1},{16,24},{17,9},{24,0},{25,17},{2,10},{3,... | collective-permute-start | bytes 4030472 | tf_op jit(solution)/shard_map/ppermute | solution.py:320
  51.6 6.2 %collective-permute-start = (bf16[4,64,256]{2,1,0:T(8,128)(2,1)S(1)}, bf16[4,64,256]{2,1,0:T(8,128)(2,1)S(1)}, u32[]{:S(2)}, u32[]{:S(2)}) collective-permute-start(bf16[4,64,256]{2,1,0:T(8,128)(2,1)S(1)} %get-tuple-element.17), channel_id=1, source_target_pairs={{0,1},{1,2},{2,3},{3,4},{4,5},{5,6},{6,7},{8,9},{9,10},{10,11},{11... | collective-permute-start | bytes 393224 | tf_op jit(solution)/shard_map/ppermute | solution.py:353
  55.8 6.7 %collective-permute-start.1 = (bf16[4,64,256]{2,1,0:T(8,128)(2,1)S(1)}, bf16[4,64,256]{2,1,0:T(8,128)(2,1)S(1)}, u32[]{:S(2)}, u32[]{:S(2)}) collective-permute-start(bf16[4,64,256]{2,1,0:T(8,128)(2,1)S(1)} %get-tuple-element.16), channel_id=1, source_target_pairs={{1,0},{2,1},{3,2},{4,3},{5,4},{6,5},{7,6},{9,8},{10,9},{11,10},{12... | collective-permute-start | bytes 393224 | tf_op jit(solution)/shard_map/ppermute | solution.py:354
  57.7 12.3 %collective-permute-start.14 = (bf16[4,2,656,128]{3,2,1,0:T(8,128)(2,1)S(1)}, bf16[4,2,656,128]{3,2,1,0:T(8,128)(2,1)S(1)}, u32[]{:S(2)}, u32[]{:S(2)}) collective-permute-start(bf16[4,2,656,128]{3,2,1,0:T(8,128)(2,1)S(1)} %pad_maximum_fusion.refs_0_), channel_id=1, source_target_pairs={{0,1},{1,0},{2,3},{3,2},{4,5},{5,4},{6,7},{7,6},{8,9},{9,8},{10,11... | collective-permute-start | bytes 4030472 | tf_op jit(solution)/shard_map/ppermute | solution.py:349
  57.8 14.6 %collective-permute-start.18 = (bf16[4,2,656,128]{3,2,1,0:T(8,128)(2,1)S(1)}, bf16[4,2,656,128]{3,2,1,0:T(8,128)(2,1)S(1)}, u32[]{:S(2)}, u32[]{:S(2)}) collective-permute-start(bf16[4,2,656,128]{3,2,1,0:T(8,128)(2,1)S(1)} %pad_maximum_fusion.1.refs_4_), channel_id=1, source_target_pairs={{0,1},{1,0},{2,3},{3,2},{4,5},{5,4},{6,7},{7,6},{8,9},{9,8},{10,11... | collective-permute-start | bytes 4030472 | tf_op jit(solution)/shard_map/ppermute | solution.py:349
  62.5 10.1 %collective-permute-start.15 = (bf16[4,2,656,128]{3,2,1,0:T(8,128)(2,1)S(1)}, bf16[4,2,656,128]{3,2,1,0:T(8,128)(2,1)S(1)}, u32[]{:S(2)}, u32[]{:S(2)}) collective-permute-start(bf16[4,2,656,128]{3,2,1,0:T(8,128)(2,1)S(1)} %collective-permute-done.5.refs_1_), channel_id=1, source_target_pairs={{0,1},{1,0},{2,3},{3,2},{4,5},{5,4},{6,7},{7,6},{8,9},{9,8},{10,11... | collective-permute-start | bytes 4030472 | tf_op jit(solution)/shard_map/ppermute | solution.py:349
  63.4 18.7 %collective-permute-start.7 = (bf16[4,2,656,128]{3,2,1,0:T(8,128)(2,1)}, bf16[4,2,656,128]{3,2,1,0:T(8,128)(2,1)}, u32[]{:S(2)}, u32[]{:S(2)}) collective-permute-start(bf16[4,2,656,128]{3,2,1,0:T(8,128)(2,1)} %collective-permute-done.6.refs_2_), channel_id=1, source_target_pairs={{0,32},{1,97},{32,64},{33,1},{64,96},{65,33},{96,0},{97,65},{2,34}... | collective-permute-start | bytes 4030472 | tf_op jit(solution)/shard_map/ppermute | solution.py:320
  67.0 22.6 %collective-permute-start.13 = (bf16[4,2,656,128]{3,2,1,0:T(8,128)(2,1)}, bf16[4,2,656,128]{3,2,1,0:T(8,128)(2,1)}, u32[]{:S(2)}, u32[]{:S(2)}) collective-permute-start(bf16[4,2,656,128]{3,2,1,0:T(8,128)(2,1)} %collective-permute-done.12.refs_6_), channel_id=1, source_target_pairs={{0,8},{1,25},{8,16},{9,1},{16,24},{17,9},{24,0},{25,17},{2,10},{3,... | collective-permute-start | bytes 4030472 | tf_op jit(solution)/shard_map/ppermute | solution.py:320
  70.0 26.9 %copy-start.8 = (s32[16]{0:T(128)S(1)}, s32[16]{0:T(128)}, u32[]{:S(2)}) copy-start(s32[16]{0:T(128)} %param.10) | copy-start | bytes 196
  70.0 37.7 %copy-start.10 = (s32[16]{0:T(128)S(1)}, s32[16]{0:T(128)}, u32[]{:S(2)}) copy-start(s32[16]{0:T(128)} %param.11) | copy-start | bytes 196
  70.0 3.0 %copy-start.4 = (bf16[4,2,656,128]{3,2,1,0:T(8,128)(2,1)}, bf16[4,2,656,128]{3,2,1,0:T(8,128)(2,1)S(1)}, u32[]{:S(2)}) copy-start(bf16[4,2,656,128]{3,2,1,0:T(8,128)(2,1)S(1)} %collective-permute-done.14.refs_8_) | copy-start | bytes 4030468
  70.1 64.3 %collective-permute-start.19 = (bf16[4,2,656,128]{3,2,1,0:T(8,128)(2,1)}, bf16[4,2,656,128]{3,2,1,0:T(8,128)(2,1)}, u32[]{:S(2)}, u32[]{:S(2)}) collective-permute-start(bf16[4,2,656,128]{3,2,1,0:T(8,128)(2,1)} %collective-permute-done.11.refs_5_), channel_id=1, source_target_pairs={{0,1},{1,0},{2,3},{3,2},{4,5},{5,4},{6,7},{7,6},{8,9},{9,8},{10,11... | collective-permute-start | bytes 4030472 | tf_op jit(solution)/shard_map/ppermute | solution.py:349
  72.4 9.7 %copy-start.5 = (bf16[4,2,656,128]{3,2,1,0:T(8,128)(2,1)}, bf16[4,2,656,128]{3,2,1,0:T(8,128)(2,1)S(1)}, u32[]{:S(2)}) copy-start(bf16[4,2,656,128]{3,2,1,0:T(8,128)(2,1)S(1)} %collective-permute-done.18.refs_12_) | copy-start | bytes 4030468
  72.4 61.9 %collective-permute-start.16 = (bf16[4,2,656,128]{3,2,1,0:T(8,128)(2,1)}, bf16[4,2,656,128]{3,2,1,0:T(8,128)(2,1)}, u32[]{:S(2)}, u32[]{:S(2)}) collective-permute-start(bf16[4,2,656,128]{3,2,1,0:T(8,128)(2,1)} %collective-permute-done.6.refs_2_), channel_id=1, source_target_pairs={{0,1},{1,0},{2,3},{3,2},{4,5},{5,4},{6,7},{7,6},{8,9},{9,8},{10,11... | collective-permute-start | bytes 4030472 | tf_op jit(solution)/shard_map/ppermute | solution.py:349
  72.6 17.0 %copy-start.6 = (bf16[4,2,656,128]{3,2,1,0:T(8,128)(2,1)}, bf16[4,2,656,128]{3,2,1,0:T(8,128)(2,1)S(1)}, u32[]{:S(2)}) copy-start(bf16[4,2,656,128]{3,2,1,0:T(8,128)(2,1)S(1)} %collective-permute-done.15.refs_9_) | copy-start | bytes 4030468
  72.6 61.8 %collective-permute-start.20 = (bf16[4,2,656,128]{3,2,1,0:T(8,128)(2,1)}, bf16[4,2,656,128]{3,2,1,0:T(8,128)(2,1)}, u32[]{:S(2)}, u32[]{:S(2)}) collective-permute-start(bf16[4,2,656,128]{3,2,1,0:T(8,128)(2,1)} %collective-permute-done.12.refs_6_), channel_id=1, source_target_pairs={{0,1},{1,0},{2,3},{3,2},{4,5},{5,4},{6,7},{7,6},{8,9},{9,8},{10,11... | collective-permute-start | bytes 4030472 | tf_op jit(solution)/shard_map/ppermute | solution.py:349
  82.2 52.1 %collective-permute-start.17 = (bf16[4,2,656,128]{3,2,1,0:T(8,128)(2,1)}, bf16[4,2,656,128]{3,2,1,0:T(8,128)(2,1)}, u32[]{:S(2)}, u32[]{:S(2)}) collective-permute-start(bf16[4,2,656,128]{3,2,1,0:T(8,128)(2,1)} %collective-permute-done.7.refs_3_), channel_id=1, source_target_pairs={{0,1},{1,0},{2,3},{3,2},{4,5},{5,4},{6,7},{7,6},{8,9},{9,8},{10,11... | collective-permute-start | bytes 4030472 | tf_op jit(solution)/shard_map/ppermute | solution.py:349
  89.6 44.7 %collective-permute-start.21 = (bf16[4,2,656,128]{3,2,1,0:T(8,128)(2,1)}, bf16[4,2,656,128]{3,2,1,0:T(8,128)(2,1)}, u32[]{:S(2)}, u32[]{:S(2)}) collective-permute-start(bf16[4,2,656,128]{3,2,1,0:T(8,128)(2,1)} %collective-permute-done.13.refs_7_), channel_id=1, source_target_pairs={{0,1},{1,0},{2,3},{3,2},{4,5},{5,4},{6,7},{7,6},{8,9},{9,8},{10,11... | collective-permute-start | bytes 4030472 | tf_op jit(solution)/shard_map/ppermute | solution.py:349
  92.8 15.6 %all-to-all-start = ((bf16[4,6,64,128]{3,2,1,0:T(8,128)(2,1)}), bf16[4,6,64,128]{3,2,1,0:T(8,128)(2,1)}, u32[]{:S(2)}, u32[]{:S(2)}) async-start(bf16[4,6,64,128]{3,2,1,0:T(8,128)(2,1)} %broadcast_in_dim.4), calls=%async_computation | async-start | bytes 786432 | tf_op jit(solution)/shard_map/all_to_all | solution.py:360
  96.9 17.6 %copy-start.9 = (s32[16,1]{0,1:T(1,128)S(1)}, s32[16,1]{0,1:T(1,128)}, u32[]{:S(2)}) copy-start(s32[16,1]{0,1:T(1,128)} %param.13) | copy-start | bytes 196
  110.2 12.4 %all-to-all-start.1 = ((bf16[4,6,64,128]{3,2,1,0:T(8,128)(2,1)}), bf16[4,6,64,128]{3,2,1,0:T(8,128)(2,1)}, u32[]{:S(2)}, u32[]{:S(2)}) async-start(bf16[4,6,64,128]{3,2,1,0:T(8,128)(2,1)} %pad_maximum_fusion.2), calls=%async_computation.1 | async-start | bytes 786432 | tf_op jit(solution)/shard_map/all_to_all | solution.py:363
  115.4 19.0 %copy-start.2 = (s32[16]{0:T(128)S(1)}, s32[16]{0:T(128)}, u32[]{:S(2)}) copy-start(s32[16]{0:T(128)} %starts_ref.1) | copy-start | bytes 196
  133.0 1.4 copy-start

commit v4 on v3

--- a/solution.py
+++ b/solution.py
@@ -22,6 +22,7 @@
 SHRINK_AT = EXPAND_AT + EXPAND_ROWS
 HEAD_AT = SHRINK_AT + SHRINK_ROWS
 PART_ROWS = HEAD_AT + HEAD_ROWS
+STRIP_ROWS = 128
 
 
 def gauss_taps():
@@ -30,7 +31,7 @@
     return [value / summed for value in weights_raw]
 
 
-def pack_kernel(core_ref, stem_ref, expand_ref, shrink_ref, head_ref, *refs):
+def pack_kernel(core_ref, stem_ref, expand_ref, shrink_ref, head_ref, own_ref, *refs):
     out_refs, wide_ref = refs[:2], refs[2]
     head = jnp.concatenate(
         [head_ref[:, :128].astype(F32), head_ref[:, 128:].astype(F32)], axis=0
@@ -49,13 +50,26 @@
         out_ref, q = out_refs[local // 2], local % 2
         out_ref[q, pl.ds(EXPAND_AT, 256), :] = expand_ref[:, pl.ds(128 * local, 128)]
         out_ref[q, pl.ds(HEAD_AT, 16), :] = head
-
-
-def pack_parts(core, stem, expand, shrink, head):
+    planes, rows = own_ref.shape[0], own_ref.shape[1]
+    lane = lax.broadcasted_iota(jnp.int32, (rows, 128), 1)
+    for i in range(HALO):
+        strip = own_ref[i].astype(F32)
+        for quarter in range(1, planes // HALO):
+            plane = pltpu.roll(own_ref[HALO * quarter + i].astype(F32), OV * quarter, 1)
+            strip = jnp.where(lane >= OV * quarter, plane, strip)
+        at = PART_ROWS + rows * (i % 2)
+        out_refs[0][i // 2, pl.ds(at, rows), :] = strip.astype(BF16)
+
+
+def pack_parts(core, stem, expand, shrink, head, own):
+    wide = pl.BlockSpec((2, PART_ROWS + STRIP_ROWS, 128), lambda i, c: (0, 0, 0))
     whole = pl.BlockSpec((2, PART_ROWS, 128), lambda i, c: (0, 0, 0))
     return pl.pallas_call(
         pack_kernel,
-        out_shape=(jax.ShapeDtypeStruct((2, PART_ROWS, 128), BF16),) * 2,
+        out_shape=(
+            jax.ShapeDtypeStruct((2, PART_ROWS + STRIP_ROWS, 128), BF16),
+            jax.ShapeDtypeStruct((2, PART_ROWS, 128), BF16),
+        ),
         grid_spec=pltpu.PrefetchScalarGridSpec(
             num_scalar_prefetch=1,
             grid=(1,),
@@ -64,44 +78,45 @@
                 pl.BlockSpec((256, 512), lambda i, c: (0, c[0])),
                 pl.BlockSpec((512, 256), lambda i, c: (c[0], 0)),
                 pl.BlockSpec((8, 256), lambda i, c: (0, 0)),
+                pl.BlockSpec(own.shape[:2] + (128,), lambda i, c: (0, 0, 0)),
             ],
-            out_specs=(whole, whole),
+            out_specs=(wide, whole),
             scratch_shapes=[pltpu.VMEM((512, 128), F32)],
         ),
         cost_estimate=pl.CostEstimate(flops=0, bytes_accessed=2 << 20, transcendentals=0),
         name="pack_parts",
-    )(core, stem, expand, shrink, head)
+    )(core, stem, expand, shrink, head, own)
 
 
 def band_kernel(
-    scalars_ref, before_ref, own_ref, after_ref, mate_ref, log_ref, table_ref,
-    joined_ref, rows_ref, smooth_ref, columns_ref,
+    scalars_ref, before_ref, own_ref, after_ref, mate_before_ref, mate_ref, mate_after_ref,
+    log_ref, table_ref, joined_ref, rows_ref, smooth_ref, columns_ref,
 ):
     taps = gauss_taps()
     planes, rows, width = own_ref.shape
-    offset, slab, slabs = scalars_ref[1], scalars_ref[2], scalars_ref[3]
-    total = planes + 2 * HALO
-    group = total // 4
+    offset, slab, slabs = scalars_ref[0], scalars_ref[1], scalars_ref[2]
 
     lane = lax.broadcasted_iota(jnp.int32, (rows, 128), 1)
     ramp = 0.25 + 0.5 * (lane.astype(F32) + 0.5) / OV
-    for i in range(group):
-        strip = pltpu.roll(mate_ref[0, i].astype(F32), offset, 0)
-        for quarter in range(4):
-            z = quarter * group + i
-            if z < HALO:
-                raw = before_ref[z]
-            elif z < HALO + planes:
-                raw = own_ref[z - HALO]
-            else:
-                raw = after_ref[z - HALO - planes]
-            raw = raw.astype(F32)
-            mate = strip if quarter == 0 else pltpu.roll(strip, 128 - 32 * quarter, 1)
-            first = raw[:, :128]
-            joined_ref[z, :, :128] = jnp.where(
-                lane < OV, ramp * first + (1.0 - ramp) * mate, first
-            )
-            joined_ref[z, :, 128:] = raw[:, 128:]
+    quarters = planes // HALO
+
+    def stitch(z, raw, strip, quarter):
+        raw = raw.astype(F32)
+        mate = strip if quarter == 0 else pltpu.roll(strip, 128 - OV * quarter, 1)
+        first = raw[:, :128]
+        joined_ref[z, :, :128] = jnp.where(lane < OV, ramp * first + (1.0 - ramp) * mate, first)
+        joined_ref[z, :, 128:] = raw[:, 128:]
+
+    def turned(ref, i):
+        return pltpu.roll(ref[i].astype(F32), offset, 0)
+
+    for i in range(HALO):
+        stitch(i, before_ref[i], turned(mate_before_ref, i), quarters - 1)
+        stitch(HALO + planes + i, after_ref[i], turned(mate_after_ref, i), 0)
+        strip = turned(mate_ref, i)
+        for quarter in range(quarters):
+            z = HALO * quarter + i
+            stitch(HALO + z, own_ref[z], strip, quarter)
 
     source = lax.broadcasted_iota(jnp.int32, (width, width), 0)
     target = lax.broadcasted_iota(jnp.int32, (width, width), 1)
@@ -157,7 +172,7 @@
     table_ref[...] = columns_ref[...].astype(BF16)
 
 
-def filter_band(scalars, before, own, after, mates):
+def filter_band(scalars, before, own, after, mate_before, mate, mate_after):
     planes, rows, width = own.shape
     count = (planes // 4) * (rows // 8)
     whole3 = lambda i, s: (0, 0, 0)
@@ -174,8 +189,8 @@
                 pl.BlockSpec((HALO, rows, width), whole3),
                 pl.BlockSpec((planes, rows, width), whole3),
                 pl.BlockSpec((HALO, rows, width), whole3),
-                pl.BlockSpec((1,) + mates.shape[1:], lambda i, s: (s[0], 0, 0, 0)),
-            ],
+            ]
+            + [pl.BlockSpec(mate.shape, whole3)] * 3,
             out_specs=(
                 pl.BlockSpec((planes, rows, width), whole3),
                 pl.BlockSpec((width * count, 128), lambda i, s: (0, 0)),
@@ -192,7 +207,7 @@
             flops=2_000_000_000, bytes_accessed=6 << 20, transcendentals=0
         ),
         name="filter_band",
-    )(scalars, before, own, after, mates)
+    )(scalars, before, own, after, mate_before, mate, mate_after)
 
 
 def classify_kernel(starts_ref, place_ref, table_ref, *refs):
@@ -311,20 +326,17 @@
     return scores.T
 
 
-def ring(value, axis):
-    size = lax.axis_size(axis)
+def trade(value, axis, first):
     pairs = []
-    for i in range(size):
-        pairs.append((2 * i, 2 * ((i + 1) % size)))
-        pairs.append((2 * i + 1, 2 * ((i - 1) % size) + 1))
+    for i in range(4):
+        for core in range(2):
+            pairs.append((2 * i + core, 2 * (i ^ (1 if first == (core == 0) else 3)) + core))
     return lax.ppermute(value, (axis, "core"), pairs)
 
 
-def around(value, axis):
-    values = [value]
-    for _ in range(lax.axis_size(axis) - 1):
-        values.append(ring(values[-1], axis))
-    return values
+def chosen(me, other, core):
+    apart = me ^ other
+    return jnp.where(apart == 2, 3, jnp.where(apart == 0, 0, jnp.where((apart == 1) == (core == 0), 1, 2)))
 
 
 def body(
@@ -340,46 +352,64 @@
 
     first, second = pack_parts(
         jnp.reshape(core_me, (1,)).astype(jnp.int32),
-        stem_weight[0], expand_weight[0, 0], shrink_weight[0, 0], head_weight[0].T,
+        stem_weight[0], expand_weight[0, 0], shrink_weight[0, 0], head_weight[0].T, own,
     )
-    stream_a = around(jnp.stack(around(first, "post")), "line")
-    stream_b = around(jnp.stack(around(second, "line")), "post")
-    swap = [(0, 1), (1, 0)]
-    weights = stream_a + stream_b
-    weights = weights + [lax.ppermute(value, "core", swap) for value in weights]
+
+    def near(value, axis):
+        return [value, trade(value, axis, True), trade(value, axis, False)]
+
+    def far(values, axis):
+        return values + [trade(values[1], axis, False)]
+
+    stream_a, stream_b = near(first, "post"), near(second, "line")
+    own, _ = lax.optimization_barrier((own, first))
+    stream_a, stream_b = far(stream_a, "post"), far(stream_b, "line")
+
+    routes = classifier[:, 0]
+    places = []
+    for core in (core_me, 1 - core_me):
+        by_line = chosen(line_me, routes // posts, core)
+        by_post = chosen(post_me, routes % posts, core)
+        places += [by_line, by_post, by_post, by_line]
+    place = jnp.stack(places + [jnp.broadcast_to(core_me, routes.shape)]).astype(jnp.int32)
+    scalars = jnp.stack([offsets[tile_me], slab_me, jnp.int32(slabs)])
 
     up = [(i, i + 1) for i in range(slabs - 1)]
     down = [(j, i) for i, j in up]
     before = lax.ppermute(own[planes - HALO :], slab_axes, up)
     after = lax.ppermute(own[:HALO], slab_axes, down)
 
-    group = (planes + 2 * HALO) // 4
-    strip = jnp.concatenate([before[:, :, :OV], own[:, :, :OV], after[:, :, :OV]], axis=0)
-    strip = jnp.concatenate([strip[q * group : (q + 1) * group] for q in range(4)], axis=2)
-    sent = jnp.broadcast_to(strip[None], (posts,) + strip.shape)
-    met = lax.all_to_all(sent, "post", split_axis=0, concat_axis=0, tiled=True)
-    wanted = [partner[line * posts + post_me] % posts for line in range(lines)]
-    sent = jnp.stack([lax.dynamic_index_in_dim(met, w, 0, keepdims=False) for w in wanted])
+    met = jnp.stack([value[:, PART_ROWS:] for value in stream_a])
+    sent = []
+    for line in range(lines):
+        back = chosen(post_me, partner[line * posts + post_me] % posts, core_me)
+        sent.append(lax.dynamic_index_in_dim(met, back, 0, keepdims=False))
+    sent = jnp.stack(sent)
+    all_a = jnp.stack([value[:, :PART_ROWS] for value in stream_a])
+    all_b = jnp.stack(stream_b)
+    all_a, place, scalars = lax.optimization_barrier((all_a, place, scalars))
+    stream_a, stream_b = near(all_a, "line"), near(all_b, "post")
     mates = lax.all_to_all(sent, "line", split_axis=0, concat_axis=0, tiled=True)
-
-    scalars = jnp.stack(
-        [partner[tile_me] // posts, offsets[tile_me], slab_me, jnp.int32(slabs)]
+    mate = lax.dynamic_index_in_dim(mates, partner[tile_me] // posts, 0, keepdims=False)
+    mate = mate.reshape(HALO, rows, 128)
+    (stream_a[1], stream_b[1]), mate = lax.optimization_barrier(
+        ((stream_a[1], stream_b[1]), mate)
     )
-    log_response, table = filter_band(scalars, before, own, after, mates)
+    stream_a, stream_b = far(stream_a, "line"), far(stream_b, "post")
+
+    mate_before = lax.ppermute(mate, slab_axes, up)
+    mate_after = lax.ppermute(mate, slab_axes, down)
+    log_response, table = filter_band(
+        scalars, before, own, after, mate_before, mate, mate_after
+    )
     table = table.reshape(width, -1, 128)
-
-    routes = classifier[:, 0]
-    turn = 1 - 2 * core_me
-    by_line = (turn * (line_me - routes // posts)) % lines
-    by_post = (turn * (post_me - routes % posts)) % posts
-    other_line, other_post = (lines - by_line) % lines, (posts - by_post) % posts
-    place = jnp.stack(
-        [
-            by_line, by_post, by_post, by_line,
-            other_line, other_post, other_post, other_line,
-            jnp.broadcast_to(core_me, routes.shape),
-        ]
-    ).astype(jnp.int32)
+    ends, table = lax.optimization_barrier(((stream_a[-1], stream_b[-1]), table))
+    stream_a[-1], stream_b[-1] = ends
+
+    swap = [(0, 1), (1, 0)]
+    weights = stream_a + stream_b
+    weights = weights + [lax.ppermute(value, "core", swap) for value in weights]
+
     logits = classify(starts, place, table, weights)
     return (log_response[None], logits)
 

time: 149 us -> 116 us (0.78)
  starting transfers between devices: 64.5 us -> 45.8 us
  waiting for transfers between devices: 38.5 us -> 22.7 us
  local copies, waits for them, and re-layouts: 4.8 us -> 7.59 us
    ppermute x12 -> x14, waiting for transfers between devices: 27.1 us -> 5.11 us  [the longest x12 5.1 us: trade(): return lax.ppermute(value, (axis, 'core'), pairs)]
    ppermute x12 -> x14, starting transfers between devices: 37 us -> 19.4 us  [the longest x12 13.8 us: trade(): return lax.ppermute(value, (axis, 'core'), pairs)]
    ppermute x1, starting transfers between devices: 1.92 us -> 10.6 us  [body(): after = lax.ppermute(own[:HALO], slab_axes, down)]
    ppermute x8, waiting for transfers between devices: 0.02 us -> 6.62 us  [body(): weights = weights + [lax.ppermute(value, 'core', swap) for value in weights]]
    ppermute x1, waiting for transfers between devices: 4.16 us -> 0.01 us  [body(): after = lax.ppermute(own[:HALO], slab_axes, down)]
    all_to_all x1 -> x0, starting transfers between devices: 4.1 us -> none  [body(): met = lax.all_to_all(sent, 'post', split_axis=0, concat_axis=0, tiled=True)]
    ppermute x8, starting transfers between devices: 13.1 us -> 9.33 us  [body(): weights = weights + [lax.ppermute(value, 'core', swap) for value in weights]]
    all_to_all x1, waiting for transfers between devices: 7.21 us -> 11 us  [body(): lax.all_to_all(sent, 'line', split_axis=0, concat_axis=0, tiled=True)]
  transfers between devices with their start and end apart: 24 -> 25, of which waited for: 8 -> 4; matrix products, arithmetic and copies ran while one was open for 4% -> 7% of each run, Pallas kernels for 7% -> 8%
where the time goes in v4:
time: 116 us; the launch traced here: 115 us
  starting transfers between devices  45.8 us (39%)
  Pallas kernels  24.5 us (21%)
  waiting for transfers between devices  22.7 us (20%)
  between operations  11.3 us (10%)
  local copies, waits for them, and re-layouts  7.59 us (7%)
  other arithmetic  2.91 us (3%)
    ppermute x12, starting transfers between devices, trade(): return lax.ppermute(value, (axis, 'core'), pairs)  13.8 us
    pallas_call x1, Pallas kernels, classify(): pl.pallas_call(classify_kernel, out_shape=jax.ShapeDtypeStruct((8, count)...  12.8 us
    all_to_all x1, waiting for transfers between devices, body(): lax.all_to_all(sent, 'line', split_axis=0, concat_axis=0, tiled=True)  11 us
    ppermute x1, starting transfers between devices, body(): after = lax.ppermute(own[:HALO], slab_axes, down)  10.6 us
    pallas_call x1, Pallas kernels, filter_band(): pl.pallas_call(band_kernel, out_shape=(jax.ShapeDtypeStruct((planes, rows...  9.43 us
    ppermute x8, starting transfers between devices, body(): weights = weights + [lax.ppermute(value, 'core', swap) for value in weights]  9.33 us
    ppermute x8, waiting for transfers between devices, body(): weights = weights + [lax.ppermute(value, 'core', swap) for value in weights]  6.62 us
    ppermute x12, waiting for transfers between devices, trade(): return lax.ppermute(value, (axis, 'core'), pairs)  5.1 us
  transfers between devices with their start and end apart: 25, of which 4 were waited for; matrix products, arithmetic and copies ran while one was open for 7% of the time, Pallas kernels for 8%

profile of v4, /device:TPU:1, one launch (start us, length us, event | category | flops | bytes accessed | tf_op | source)
XLA Modules:
  0.0 114.8 jit_solution(17882551492438103289)
XLA Ops:
  0.7 2.3 %pack_parts.1 = (bf16[2,784,128]{2,1,0:T(8,128)(2,1)}, bf16[2,656,128]{2,1,0:T(8,128)(2,1)}) custom-call(s32[1]{0:T(128)} %bitcast.core_ref, bf16[512,256]{1,0:T(8,128)(2,1)} %bitcast.70, bf16[256,1024]{1,0:T(8,128)(2,1)} %bitcast.64, bf16[1024,256]{1,0:T(8,128)(2,1)} %bitcast.65, bf16[8,256]{1,0:T(8,128)(2,1)} %bitcast.71, bf16[16,64,256]{2,1,0:T(8,128)(2,1)} %bitcast.58), custom_call_target="tpu_custom_call" | custom-call | bytes 2097152 | tf_op jit(solution)/shard_map/pack_parts/pallas_call | solution.py:67
  3.0 2.1 %collective-permute-start.7 = (bf16[2,656,128]{2,1,0:T(8,128)(2,1)}, bf16[2,656,128]{2,1,0:T(8,128)(2,1)S(1)}, u32[]{:S(2)}, u32[]{:S(2)}) collective-permute-start(bf16[2,656,128]{2,1,0:T(8,128)(2,1)} %get-tuple-element.20), channel_id=1, source_target_pairs={{0,96},{1,33},{32,64},{33,1},{64,32},{65,97},{96,0},{97,65},{2,98}... | collective-permute-start | bytes 1007624 | tf_op jit(solution)/shard_map/ppermute | solution.py:334
  5.1 1.9 %collective-permute-start.6 = (bf16[2,656,128]{2,1,0:T(8,128)(2,1)}, bf16[2,656,128]{2,1,0:T(8,128)(2,1)S(1)}, u32[]{:S(2)}, u32[]{:S(2)}) collective-permute-start(bf16[2,656,128]{2,1,0:T(8,128)(2,1)} %get-tuple-element.20), channel_id=1, source_target_pairs={{0,32},{1,97},{32,0},{33,65},{64,96},{65,33},{96,64},{97,1},{2,34}... | collective-permute-start | bytes 1007624 | tf_op jit(solution)/shard_map/ppermute | solution.py:334
  7.0 1.6 %collective-permute-start.1 = (bf16[2,784,128]{2,1,0:T(8,128)(2,1)}, bf16[2,784,128]{2,1,0:T(8,128)(2,1)S(1)}, u32[]{:S(2)}, u32[]{:S(2)}) collective-permute-start(bf16[2,784,128]{2,1,0:T(8,128)(2,1)} %get-tuple-element.16), channel_id=1, source_target_pairs={{0,24},{1,9},{8,16},{9,1},{16,8},{17,25},{24,0},{25,17},{2,26},{3,... | collective-permute-start | bytes 1204232 | tf_op jit(solution)/shard_map/ppermute | solution.py:334
  8.6 2.2 %collective-permute-start = (bf16[2,784,128]{2,1,0:T(8,128)(2,1)}, bf16[2,784,128]{2,1,0:T(8,128)(2,1)S(1)}, u32[]{:S(2)}, u32[]{:S(2)}) collective-permute-start(bf16[2,784,128]{2,1,0:T(8,128)(2,1)} %get-tuple-element.16), channel_id=1, source_target_pairs={{0,8},{1,25},{8,0},{9,17},{16,24},{17,9},{24,16},{25,1},{2,10},{3,... | collective-permute-start | bytes 1204232 | tf_op jit(solution)/shard_map/ppermute | solution.py:334
  10.9 0.9 slice_bitcast_fusion.7
  11.7 1.0 slice_bitcast_fusion.3
  12.8 0.7 fusion.5
  21.1 0.7 dynamic_slice.35
  21.8 0.7 pad_add_fusion.scalars_ref
  22.5 0.0 collective-permute-done.6
  22.5 0.4 collective-permute-start.8
  23.0 0.0 collective-permute-done
  23.0 0.7 collective-permute-start.2
  23.7 0.0 collective-permute-done.1
  23.7 0.0 copy-start.11
  23.8 0.0 collective-permute-done.7
  23.8 5.1 %collective-permute-done.8 = bf16[2,656,128]{2,1,0:T(8,128)(2,1)S(1)} collective-permute-done((bf16[2,656,128]{2,1,0:T(8,128)(2,1)S(1)}, bf16[2,656,128]{2,1,0:T(8,128)(2,1)S(1)}, u32[]{:S(2)}, u32[]{:S(2)}) %collective-permute-start.8) | collective-permute-done | bytes 335904 | tf_op jit(solution)/shard_map/ppermute | solution.py:334
  28.9 1.2 %pad_maximum_fusion.1.refs_4_ = bf16[4,2,656,128]{3,2,1,0:T(8,128)(2,1)} fusion(bf16[1,2,656,128]{3,2,1,0:T(8,128)(2,1)S(1)} %bitcast.69, bf16[1,2,656,128]{3,2,1,0:T(8,128)(2,1)S(1)} %bitcast.67, bf16[1,2,656,128]{3,2,1,0:T(8,128)(2,1)S(1)} %bitcast.68, bf16[1,2,656,128]{3,2,1,0:T(8,128)(2,1)S(1)} %bitcast.66), kind=kLoop, calls=%fused_computation.1 | loop fusion | flops 2015232 | bytes 2686976 | tf_op jit(solution)/shard_map/stack | solution.py:389
  30.1 0.4 collective-permute-start.9
  30.6 0.0 collective-permute-done.2
  30.6 0.2 pad_maximum_fusion.refs_0_
  30.8 0.0 copy-start.1
  30.8 0.9 collective-permute-start.5
  31.6 0.8 slice_bitcast_fusion.5
  32.5 0.8 slice_bitcast_fusion.6
  33.4 0.7 pad_maximum_fusion.3
  34.2 3.4 %all-to-all-start = ((bf16[4,2,128,128]{3,2,1,0:T(8,128)(2,1)}), bf16[4,2,128,128]{3,2,1,0:T(8,128)(2,1)S(1)}, u32[]{:S(2)}, u32[]{:S(2)}) async-start(bf16[4,2,128,128]{3,2,1,0:T(8,128)(2,1)} %pad_maximum_fusion.3), calls=%async_computation | async-start | bytes 524288 | tf_op jit(solution)/shard_map/all_to_all | solution.py:392
  40.0 0.4 collective-permute-start.15
  40.4 11.0 %all-to-all-done = bf16[4,2,128,128]{3,2,1,0:T(8,128)(2,1)S(1)} async-done(((bf16[4,2,128,128]{3,2,1,0:T(8,128)(2,1)}), bf16[4,2,128,128]{3,2,1,0:T(8,128)(2,1)S(1)}, u32[]{:S(2)}, u32[]{:S(2)}) %all-to-all-start) | async-done | bytes 262176 | tf_op jit(solution)/shard_map/all_to_all | solution.py:392
  51.4 0.0 collective-permute-done.9.refs_5_
  51.4 0.0 collective-permute-done.5.refs_1_
  51.4 0.1 collective-permute-start.12
  51.5 10.6 %collective-permute-start.4 = (bf16[4,64,256]{2,1,0:T(8,128)(2,1)S(1)}, bf16[4,64,256]{2,1,0:T(8,128)(2,1)S(1)}, u32[]{:S(2)}, u32[]{:S(2)}) collective-permute-start(bf16[4,64,256]{2,1,0:T(8,128)(2,1)S(1)} %get-tuple-element.34), channel_id=1, source_target_pairs={{1,0},{2,1},{3,2},{4,3},{5,4},{6,5},{7,6},{9,8},{10,9},{11,10},{12... | collective-permute-start | bytes 393224 | tf_op jit(solution)/shard_map/ppermute | solution.py:380
  62.2 0.0 copy-start.2
  62.2 3.0 %collective-permute-start.3 = (bf16[4,64,256]{2,1,0:T(8,128)(2,1)S(1)}, bf16[4,64,256]{2,1,0:T(8,128)(2,1)S(1)}, u32[]{:S(2)}, u32[]{:S(2)}) collective-permute-start(bf16[4,64,256]{2,1,0:T(8,128)(2,1)S(1)} %get-tuple-element.35), channel_id=1, source_target_pairs={{0,1},{1,2},{2,3},{3,4},{4,5},{5,6},{6,7},{8,9},{9,10},{10,11},{11... | collective-permute-start | bytes 393224 | tf_op jit(solution)/shard_map/ppermute | solution.py:379
  65.2 1.9 %collective-permute-start.11 = (bf16[4,64,128]{2,1,0:T(8,128)(2,1)S(1)}, bf16[4,64,128]{2,1,0:T(8,128)(2,1)S(1)}, u32[]{:S(2)}, u32[]{:S(2)}) collective-permute-start(bf16[4,64,128]{2,1,0:T(8,128)(2,1)S(1)} %bitcast.61), channel_id=1, source_target_pairs={{1,0},{2,1},{3,2},{4,3},{5,4},{6,5},{7,6},{9,8},{10,9},{11,10},{12... | collective-permute-start | bytes 196616 | tf_op jit(solution)/shard_map/ppermute | solution.py:401
  67.1 0.0 collective-permute-done.4.after_ref
  67.1 3.6 %collective-permute-start.10 = (bf16[4,64,128]{2,1,0:T(8,128)(2,1)S(1)}, bf16[4,64,128]{2,1,0:T(8,128)(2,1)S(1)}, u32[]{:S(2)}, u32[]{:S(2)}) collective-permute-start(bf16[4,64,128]{2,1,0:T(8,128)(2,1)S(1)} %bitcast.62), channel_id=1, source_target_pairs={{0,1},{1,2},{2,3},{3,4},{4,5},{5,6},{6,7},{8,9},{9,10},{10,11},{11... | collective-permute-start | bytes 196616 | tf_op jit(solution)/shard_map/ppermute | solution.py:400
  70.8 0.0 collective-permute-done.3.before_ref
  70.8 1.9 %collective-permute-start.13 = (bf16[4,2,656,128]{3,2,1,0:T(8,128)(2,1)}, bf16[4,2,656,128]{3,2,1,0:T(8,128)(2,1)S(1)}, u32[]{:S(2)}, u32[]{:S(2)}) collective-permute-start(bf16[4,2,656,128]{3,2,1,0:T(8,128)(2,1)} %collective-permute-done.9.refs_5_), channel_id=1, source_target_pairs={{0,24},{1,9},{8,16},{9,1},{16,8},{17,25},{24,0},{25,17},{2,26},{3,... | collective-permute-start | bytes 4030472 | tf_op jit(solution)/shard_map/ppermute | solution.py:334
  72.7 0.0 collective-permute-done.15.refs_6_
  72.7 0.0 collective-permute-start.20
  72.8 0.0 collective-permute-done.11.mate_after_ref
  72.8 1.0 collective-permute-start.14
  73.8 2.7 %collective-permute-start.16 = (bf16[4,2,656,128]{3,2,1,0:T(8,128)(2,1)S(1)}, bf16[4,2,656,128]{3,2,1,0:T(8,128)(2,1)S(1)}, u32[]{:S(2)}, u32[]{:S(2)}) collective-permute-start(bf16[4,2,656,128]{3,2,1,0:T(8,128)(2,1)S(1)} %pad_maximum_fusion.refs_0_), channel_id=1, source_target_pairs={{0,1},{1,0},{2,3},{3,2},{4,5},{5,4},{6,7},{7,6},{8,9},{9,8},{10,11... | collective-permute-start | bytes 4030472 | tf_op jit(solution)/shard_map/ppermute | solution.py:411
  76.5 0.0 collective-permute-done.12.refs_3_
  76.5 2.5 %collective-permute-start.22 = (bf16[4,2,656,128]{3,2,1,0:T(8,128)(2,1)}, bf16[4,2,656,128]{3,2,1,0:T(8,128)(2,1)S(1)}, u32[]{:S(2)}, u32[]{:S(2)}) collective-permute-start(bf16[4,2,656,128]{3,2,1,0:T(8,128)(2,1)} %collective-permute-done.15.refs_6_), channel_id=1, source_target_pairs={{0,1},{1,0},{2,3},{3,2},{4,5},{5,4},{6,7},{7,6},{8,9},{9,8},{10,11... | collective-permute-start | bytes 4030472 | tf_op jit(solution)/shard_map/ppermute | solution.py:411
  79.0 9.4 %filter_band.1 = (f32[16,64,256]{2,1,0:T(8,128)}, bf16[8192,128]{1,0:T(8,128)(2,1)S(1)}) custom-call(s32[3]{0:T(128)S(1)} %pad_add_fusion.scalars_ref, bf16[4,64,256]{2,1,0:T(8,128)(2,1)S(1)} %collective-permute-done.3.before_ref, bf16[16,64,256]{2,1,0:T(8,128)(2,1)S(1)} %bitcast.60, bf16[4,64,256]{2,1,0:T(8,128)(2,1)S(1)} %collective-permute-done.4.after_ref, ...), custom_call_target="tpu_custom_call" | custom-call | flops 2000000000 | bytes 6291456 | tf_op jit(solution)/shard_map/filter_band/pallas_call | solution.py:179
  88.5 1.3 %copy-done = bf16[8192,128]{1,0:T(8,128)(2,1)} copy-done((bf16[8192,128]{1,0:T(8,128)(2,1)}, bf16[8192,128]{1,0:T(8,128)(2,1)S(1)}, u32[]{:S(2)}) %copy-start) | copy-done | bytes 2097176
  89.8 0.0 collective-permute-done.13.refs_7_
  89.8 0.0 collective-permute-start.17
  89.8 0.5 collective-permute-start.21
  90.3 3.1 %collective-permute-start.18 = (bf16[4,2,656,128]{3,2,1,0:T(8,128)(2,1)S(1)}, bf16[4,2,656,128]{3,2,1,0:T(8,128)(2,1)S(1)}, u32[]{:S(2)}, u32[]{:S(2)}) collective-permute-start(bf16[4,2,656,128]{3,2,1,0:T(8,128)(2,1)S(1)} %collective-permute-done.14.refs_2_), channel_id=1, source_target_pairs={{0,1},{1,0},{2,3},{3,2},{4,5},{5,4},{6,7},{7,6},{8,9},{9,8},{10,11... | collective-permute-start | bytes 4030472 | tf_op jit(solution)/shard_map/ppermute | solution.py:411
  93.4 0.0 collective-permute-done.16.refs_8_
  93.4 0.1 collective-permute-start.19
  93.5 0.0 collective-permute-done.22.refs_14_
  93.5 0.4 collective-permute-start.23
  93.9 4.7 %collective-permute-done.18.refs_10_ = bf16[4,2,656,128]{3,2,1,0:T(8,128)(2,1)S(1)} collective-permute-done((bf16[4,2,656,128]{3,2,1,0:T(8,128)(2,1)S(1)}, bf16[4,2,656,128]{3,2,1,0:T(8,128)(2,1)S(1)}, u32[]{:S(2)}, u32[]{:S(2)}) %collective-permute-start.18) | collective-permute-done | bytes 1343520 | tf_op jit(solution)/shard_map/ppermute | solution.py:411
  98.6 0.0 collective-permute-done.17.refs_9_
  98.7 1.9 %collective-permute-done.19.refs_11_ = bf16[4,2,656,128]{3,2,1,0:T(8,128)(2,1)S(1)} collective-permute-done((bf16[4,2,656,128]{3,2,1,0:T(8,128)(2,1)S(1)}, bf16[4,2,656,128]{3,2,1,0:T(8,128)(2,1)S(1)}, u32[]{:S(2)}, u32[]{:S(2)}) %collective-permute-start.19) | collective-permute-done | bytes 1343520 | tf_op jit(solution)/shard_map/ppermute | solution.py:411
  100.6 1.1 copy-done.10
  101.7 0.0 collective-permute-done.23.refs_15_
  101.8 12.8 %classify.1 = f32[8,16]{1,0:T(8,128)} custom-call(s32[16]{0:T(128)S(1)} %copy-done.2, s32[9,16]{1,0:T(8,128)S(1)} %stack.74.place_ref, bf16[256,32,128]{2,1,0:T(8,128)(2,1)} %bitcast.57, bf16[4,2,656,128]{3,2,1,0:T(8,128)(2,1)S(1)} %pad_maximum_fusion.refs_0_, bf16[4,2,656,128]{3,2,1,0:T(8,128)(2,1)S(1)} %collective-permute-done.5.refs_1_, ...), custom_call_target="tpu_custom_call" | custom-call | flops 5500000256 | bytes 25165824 | tf_op jit(solution)/shard_map/classify/pallas_call | solution.py:306
  (45 shorter events, 0.3 us)
Async XLA Ops:
  0.6 12.1 %copy-start.15 = (s32[16,1]{0,1:T(1,128)S(1)}, s32[16,1]{0,1:T(1,128)}, u32[]{:S(2)}) copy-start(s32[16,1]{0,1:T(1,128)} %param.13) | copy-start | bytes 196
  0.6 12.2 %copy-start.14 = (s32[16]{0:T(128)S(1)}, s32[16]{0:T(128)}, u32[]{:S(2)}) copy-start(s32[16]{0:T(128)} %param.10) | copy-start | bytes 196
  0.7 20.5 %copy-start.16 = (s32[16]{0:T(128)S(1)}, s32[16]{0:T(128)}, u32[]{:S(2)}) copy-start(s32[16]{0:T(128)} %param.11) | copy-start | bytes 196
  3.0 25.9 %copy-start.13 = (bf16[2,656,128]{2,1,0:T(8,128)(2,1)S(1)}, bf16[2,656,128]{2,1,0:T(8,128)(2,1)}, u32[]{:S(2)}) copy-start(bf16[2,656,128]{2,1,0:T(8,128)(2,1)} %get-tuple-element.20) | copy-start | bytes 1007620
  3.0 20.8 %collective-permute-start.7 = (bf16[2,656,128]{2,1,0:T(8,128)(2,1)}, bf16[2,656,128]{2,1,0:T(8,128)(2,1)S(1)}, u32[]{:S(2)}, u32[]{:S(2)}) collective-permute-start(bf16[2,656,128]{2,1,0:T(8,128)(2,1)} %get-tuple-element.20), channel_id=1, source_target_pairs={{0,96},{1,33},{32,64},{33,1},{64,32},{65,97},{96,0},{97,65},{2,98}... | collective-permute-start | bytes 1007624 | tf_op jit(solution)/shard_map/ppermute | solution.py:334
  5.1 17.5 %collective-permute-start.6 = (bf16[2,656,128]{2,1,0:T(8,128)(2,1)}, bf16[2,656,128]{2,1,0:T(8,128)(2,1)S(1)}, u32[]{:S(2)}, u32[]{:S(2)}) collective-permute-start(bf16[2,656,128]{2,1,0:T(8,128)(2,1)} %get-tuple-element.20), channel_id=1, source_target_pairs={{0,32},{1,97},{32,0},{33,65},{64,96},{65,33},{96,64},{97,1},{2,34}... | collective-permute-start | bytes 1007624 | tf_op jit(solution)/shard_map/ppermute | solution.py:334
  7.0 16.8 %collective-permute-start.1 = (bf16[2,784,128]{2,1,0:T(8,128)(2,1)}, bf16[2,784,128]{2,1,0:T(8,128)(2,1)S(1)}, u32[]{:S(2)}, u32[]{:S(2)}) collective-permute-start(bf16[2,784,128]{2,1,0:T(8,128)(2,1)} %get-tuple-element.16), channel_id=1, source_target_pairs={{0,24},{1,9},{8,16},{9,1},{16,8},{17,25},{24,0},{25,17},{2,26},{3,... | collective-permute-start | bytes 1204232 | tf_op jit(solution)/shard_map/ppermute | solution.py:334
  8.6 14.3 %collective-permute-start = (bf16[2,784,128]{2,1,0:T(8,128)(2,1)}, bf16[2,784,128]{2,1,0:T(8,128)(2,1)S(1)}, u32[]{:S(2)}, u32[]{:S(2)}) collective-permute-start(bf16[2,784,128]{2,1,0:T(8,128)(2,1)} %get-tuple-element.16), channel_id=1, source_target_pairs={{0,8},{1,25},{8,0},{9,17},{16,24},{17,9},{24,16},{25,1},{2,10},{3,... | collective-permute-start | bytes 1204232 | tf_op jit(solution)/shard_map/ppermute | solution.py:334
  22.5 6.3 %collective-permute-start.8 = (bf16[2,656,128]{2,1,0:T(8,128)(2,1)S(1)}, bf16[2,656,128]{2,1,0:T(8,128)(2,1)S(1)}, u32[]{:S(2)}, u32[]{:S(2)}) collective-permute-start(bf16[2,656,128]{2,1,0:T(8,128)(2,1)S(1)} %collective-permute-done.6), channel_id=1, source_target_pairs={{0,96},{1,33},{32,64},{33,1},{64,32},{65,97},{96,0},{97,65},{2,98}... | collective-permute-start | bytes 1007624 | tf_op jit(solution)/shard_map/ppermute | solution.py:334
  23.0 7.2 %copy-start.12 = (bf16[2,784,128]{2,1,0:T(8,128)(2,1)}, bf16[2,784,128]{2,1,0:T(8,128)(2,1)S(1)}, u32[]{:S(2)}) copy-start(bf16[2,784,128]{2,1,0:T(8,128)(2,1)S(1)} %collective-permute-done) | copy-start | bytes 1204228
  23.0 7.6 %collective-permute-start.2 = (bf16[2,784,128]{2,1,0:T(8,128)(2,1)S(1)}, bf16[2,784,128]{2,1,0:T(8,128)(2,1)S(1)}, u32[]{:S(2)}, u32[]{:S(2)}) collective-permute-start(bf16[2,784,128]{2,1,0:T(8,128)(2,1)S(1)} %collective-permute-done), channel_id=1, source_target_pairs={{0,24},{1,9},{8,16},{9,1},{16,8},{17,25},{24,0},{25,17},{2,26},{3,... | collective-permute-start | bytes 1204232 | tf_op jit(solution)/shard_map/ppermute | solution.py:334
  23.7 6.4 %copy-start.11 = (bf16[2,784,128]{2,1,0:T(8,128)(2,1)}, bf16[2,784,128]{2,1,0:T(8,128)(2,1)S(1)}, u32[]{:S(2)}) copy-start(bf16[2,784,128]{2,1,0:T(8,128)(2,1)S(1)} %collective-permute-done.1) | copy-start | bytes 1204228
  30.1 21.3 %collective-permute-start.9 = (bf16[4,2,656,128]{3,2,1,0:T(8,128)(2,1)}, bf16[4,2,656,128]{3,2,1,0:T(8,128)(2,1)}, u32[]{:S(2)}, u32[]{:S(2)}) collective-permute-start(bf16[4,2,656,128]{3,2,1,0:T(8,128)(2,1)} %pad_maximum_fusion.1.refs_4_), channel_id=1, source_target_pairs={{0,8},{1,25},{8,0},{9,17},{16,24},{17,9},{24,16},{25,1},{2,10},{3,... | collective-permute-start | bytes 4030472 | tf_op jit(solution)/shard_map/ppermute | solution.py:334
  30.8 20.7 %copy-start.1 = (bf16[1,16,64,256]{3,2,1,0:T(8,128)(2,1)S(1)}, bf16[1,16,64,256]{3,2,1,0:T(8,128)(2,1)}, u32[]{:S(2)}) copy-start(bf16[1,16,64,256]{3,2,1,0:T(8,128)(2,1)} %param.9) | copy-start | bytes 1572868
  30.8 20.6 %collective-permute-start.5 = (bf16[4,2,656,128]{3,2,1,0:T(8,128)(2,1)S(1)}, bf16[4,2,656,128]{3,2,1,0:T(8,128)(2,1)S(1)}, u32[]{:S(2)}, u32[]{:S(2)}) collective-permute-start(bf16[4,2,656,128]{3,2,1,0:T(8,128)(2,1)S(1)} %pad_maximum_fusion.refs_0_), channel_id=1, source_target_pairs={{0,32},{1,97},{32,0},{33,65},{64,96},{65,33},{96,64},{97,1},{2,34}... | collective-permute-start | bytes 4030472 | tf_op jit(solution)/shard_map/ppermute | solution.py:334
  34.2 17.2 %all-to-all-start = ((bf16[4,2,128,128]{3,2,1,0:T(8,128)(2,1)}), bf16[4,2,128,128]{3,2,1,0:T(8,128)(2,1)S(1)}, u32[]{:S(2)}, u32[]{:S(2)}) async-start(bf16[4,2,128,128]{3,2,1,0:T(8,128)(2,1)} %pad_maximum_fusion.3), calls=%async_computation | async-start | bytes 524288 | tf_op jit(solution)/shard_map/all_to_all | solution.py:392
  40.0 32.7 %collective-permute-start.15 = (bf16[4,2,656,128]{3,2,1,0:T(8,128)(2,1)}, bf16[4,2,656,128]{3,2,1,0:T(8,128)(2,1)}, u32[]{:S(2)}, u32[]{:S(2)}) collective-permute-start(bf16[4,2,656,128]{3,2,1,0:T(8,128)(2,1)} %pad_maximum_fusion.1.refs_4_), channel_id=1, source_target_pairs={{0,24},{1,9},{8,16},{9,1},{16,8},{17,25},{24,0},{25,17},{2,26},{3,... | collective-permute-start | bytes 4030472 | tf_op jit(solution)/shard_map/ppermute | solution.py:334
  51.4 25.1 %collective-permute-start.12 = (bf16[4,2,656,128]{3,2,1,0:T(8,128)(2,1)S(1)}, bf16[4,2,656,128]{3,2,1,0:T(8,128)(2,1)S(1)}, u32[]{:S(2)}, u32[]{:S(2)}) collective-permute-start(bf16[4,2,656,128]{3,2,1,0:T(8,128)(2,1)S(1)} %collective-permute-done.5.refs_1_), channel_id=1, source_target_pairs={{0,96},{1,33},{32,64},{33,1},{64,32},{65,97},{96,0},{97,65},{2,98}... | collective-permute-start | bytes 4030472 | tf_op jit(solution)/shard_map/ppermute | solution.py:334
  51.5 15.6 %collective-permute-start.4 = (bf16[4,64,256]{2,1,0:T(8,128)(2,1)S(1)}, bf16[4,64,256]{2,1,0:T(8,128)(2,1)S(1)}, u32[]{:S(2)}, u32[]{:S(2)}) collective-permute-start(bf16[4,64,256]{2,1,0:T(8,128)(2,1)S(1)} %get-tuple-element.34), channel_id=1, source_target_pairs={{1,0},{2,1},{3,2},{4,3},{5,4},{6,5},{7,6},{9,8},{10,9},{11,10},{12... | collective-permute-start | bytes 393224 | tf_op jit(solution)/shard_map/ppermute | solution.py:380
  62.2 39.6 %copy-start.2 = (s32[16]{0:T(128)S(1)}, s32[16]{0:T(128)}, u32[]{:S(2)}) copy-start(s32[16]{0:T(128)} %starts_ref.1) | copy-start | bytes 196
  62.2 8.6 %collective-permute-start.3 = (bf16[4,64,256]{2,1,0:T(8,128)(2,1)S(1)}, bf16[4,64,256]{2,1,0:T(8,128)(2,1)S(1)}, u32[]{:S(2)}, u32[]{:S(2)}) collective-permute-start(bf16[4,64,256]{2,1,0:T(8,128)(2,1)S(1)} %get-tuple-element.35), channel_id=1, source_target_pairs={{0,1},{1,2},{2,3},{3,4},{4,5},{5,6},{6,7},{8,9},{9,10},{10,11},{11... | collective-permute-start | bytes 393224 | tf_op jit(solution)/shard_map/ppermute | solution.py:379
  65.2 7.5 %collective-permute-start.11 = (bf16[4,64,128]{2,1,0:T(8,128)(2,1)S(1)}, bf16[4,64,128]{2,1,0:T(8,128)(2,1)S(1)}, u32[]{:S(2)}, u32[]{:S(2)}) collective-permute-start(bf16[4,64,128]{2,1,0:T(8,128)(2,1)S(1)} %bitcast.61), channel_id=1, source_target_pairs={{1,0},{2,1},{3,2},{4,3},{5,4},{6,5},{7,6},{9,8},{10,9},{11,10},{12... | collective-permute-start | bytes 196616 | tf_op jit(solution)/shard_map/ppermute | solution.py:401
  67.1 6.6 %collective-permute-start.10 = (bf16[4,64,128]{2,1,0:T(8,128)(2,1)S(1)}, bf16[4,64,128]{2,1,0:T(8,128)(2,1)S(1)}, u32[]{:S(2)}, u32[]{:S(2)}) collective-permute-start(bf16[4,64,128]{2,1,0:T(8,128)(2,1)S(1)} %bitcast.62), channel_id=1, source_target_pairs={{0,1},{1,2},{2,3},{3,4},{4,5},{5,6},{6,7},{8,9},{9,10},{10,11},{11... | collective-permute-start | bytes 196616 | tf_op jit(solution)/shard_map/ppermute | solution.py:400
  70.8 19.0 %collective-permute-start.13 = (bf16[4,2,656,128]{3,2,1,0:T(8,128)(2,1)}, bf16[4,2,656,128]{3,2,1,0:T(8,128)(2,1)S(1)}, u32[]{:S(2)}, u32[]{:S(2)}) collective-permute-start(bf16[4,2,656,128]{3,2,1,0:T(8,128)(2,1)} %collective-permute-done.9.refs_5_), channel_id=1, source_target_pairs={{0,24},{1,9},{8,16},{9,1},{16,8},{17,25},{24,0},{25,17},{2,26},{3,... | collective-permute-start | bytes 4030472 | tf_op jit(solution)/shard_map/ppermute | solution.py:334
  72.7 17.1 %collective-permute-start.20 = (bf16[4,2,656,128]{3,2,1,0:T(8,128)(2,1)}, bf16[4,2,656,128]{3,2,1,0:T(8,128)(2,1)S(1)}, u32[]{:S(2)}, u32[]{:S(2)}) collective-permute-start(bf16[4,2,656,128]{3,2,1,0:T(8,128)(2,1)} %pad_maximum_fusion.1.refs_4_), channel_id=1, source_target_pairs={{0,1},{1,0},{2,3},{3,2},{4,5},{5,4},{6,7},{7,6},{8,9},{9,8},{10,11... | collective-permute-start | bytes 4030472 | tf_op jit(solution)/shard_map/ppermute | solution.py:411
  72.8 17.6 %collective-permute-start.14 = (bf16[4,2,656,128]{3,2,1,0:T(8,128)(2,1)S(1)}, bf16[4,2,656,128]{3,2,1,0:T(8,128)(2,1)S(1)}, u32[]{:S(2)}, u32[]{:S(2)}) collective-permute-start(bf16[4,2,656,128]{3,2,1,0:T(8,128)(2,1)S(1)} %pad_maximum_fusion.refs_0_), channel_id=1, source_target_pairs={{0,96},{1,33},{32,64},{33,1},{64,32},{65,97},{96,0},{97,65},{2,98}... | collective-permute-start | bytes 4030472 | tf_op jit(solution)/shard_map/ppermute | solution.py:334
  73.8 19.6 %collective-permute-start.16 = (bf16[4,2,656,128]{3,2,1,0:T(8,128)(2,1)S(1)}, bf16[4,2,656,128]{3,2,1,0:T(8,128)(2,1)S(1)}, u32[]{:S(2)}, u32[]{:S(2)}) collective-permute-start(bf16[4,2,656,128]{3,2,1,0:T(8,128)(2,1)S(1)} %pad_maximum_fusion.refs_0_), channel_id=1, source_target_pairs={{0,1},{1,0},{2,3},{3,2},{4,5},{5,4},{6,7},{7,6},{8,9},{9,8},{10,11... | collective-permute-start | bytes 4030472 | tf_op jit(solution)/shard_map/ppermute | solution.py:411
  76.5 17.0 %collective-permute-start.22 = (bf16[4,2,656,128]{3,2,1,0:T(8,128)(2,1)}, bf16[4,2,656,128]{3,2,1,0:T(8,128)(2,1)S(1)}, u32[]{:S(2)}, u32[]{:S(2)}) collective-permute-start(bf16[4,2,656,128]{3,2,1,0:T(8,128)(2,1)} %collective-permute-done.15.refs_6_), channel_id=1, source_target_pairs={{0,1},{1,0},{2,3},{3,2},{4,5},{5,4},{6,7},{7,6},{8,9},{9,8},{10,11... | collective-permute-start | bytes 4030472 | tf_op jit(solution)/shard_map/ppermute | solution.py:411
  88.5 1.3 %copy-start = (bf16[8192,128]{1,0:T(8,128)(2,1)}, bf16[8192,128]{1,0:T(8,128)(2,1)S(1)}, u32[]{:S(2)}) copy-start(bf16[8192,128]{1,0:T(8,128)(2,1)S(1)} %get-tuple-element.26) | copy-start | bytes 6291460
  89.8 11.9 %copy-start.3 = (bf16[4,2,656,128]{3,2,1,0:T(8,128)(2,1)}, bf16[4,2,656,128]{3,2,1,0:T(8,128)(2,1)S(1)}, u32[]{:S(2)}) copy-start(bf16[4,2,656,128]{3,2,1,0:T(8,128)(2,1)S(1)} %collective-permute-done.13.refs_7_) | copy-start | bytes 4030468
  89.8 8.9 %collective-permute-start.17 = (bf16[4,2,656,128]{3,2,1,0:T(8,128)(2,1)S(1)}, bf16[4,2,656,128]{3,2,1,0:T(8,128)(2,1)S(1)}, u32[]{:S(2)}, u32[]{:S(2)}) collective-permute-start(bf16[4,2,656,128]{3,2,1,0:T(8,128)(2,1)S(1)} %collective-permute-done.5.refs_1_), channel_id=1, source_target_pairs={{0,1},{1,0},{2,3},{3,2},{4,5},{5,4},{6,7},{7,6},{8,9},{9,8},{10,11... | collective-permute-start | bytes 4030472 | tf_op jit(solution)/shard_map/ppermute | solution.py:411
  89.8 11.9 %copy-start.4 = (bf16[4,2,656,128]{3,2,1,0:T(8,128)(2,1)}, bf16[4,2,656,128]{3,2,1,0:T(8,128)(2,1)S(1)}, u32[]{:S(2)}) copy-start(bf16[4,2,656,128]{3,2,1,0:T(8,128)(2,1)S(1)} %collective-permute-done.20.refs_12_) | copy-start | bytes 4030468
  89.8 8.8 %collective-permute-start.21 = (bf16[4,2,656,128]{3,2,1,0:T(8,128)(2,1)}, bf16[4,2,656,128]{3,2,1,0:T(8,128)(2,1)S(1)}, u32[]{:S(2)}, u32[]{:S(2)}) collective-permute-start(bf16[4,2,656,128]{3,2,1,0:T(8,128)(2,1)} %collective-permute-done.9.refs_5_), channel_id=1, source_target_pairs={{0,1},{1,0},{2,3},{3,2},{4,5},{5,4},{6,7},{7,6},{8,9},{9,8},{10,11... | collective-permute-start | bytes 4030472 | tf_op jit(solution)/shard_map/ppermute | solution.py:411
  90.3 8.3 %collective-permute-start.18 = (bf16[4,2,656,128]{3,2,1,0:T(8,128)(2,1)S(1)}, bf16[4,2,656,128]{3,2,1,0:T(8,128)(2,1)S(1)}, u32[]{:S(2)}, u32[]{:S(2)}) collective-permute-start(bf16[4,2,656,128]{3,2,1,0:T(8,128)(2,1)S(1)} %collective-permute-done.14.refs_2_), channel_id=1, source_target_pairs={{0,1},{1,0},{2,3},{3,2},{4,5},{5,4},{6,7},{7,6},{8,9},{9,8},{10,11... | collective-permute-start | bytes 4030472 | tf_op jit(solution)/shard_map/ppermute | solution.py:411
  93.4 8.3 %copy-start.5 = (bf16[4,2,656,128]{3,2,1,0:T(8,128)(2,1)}, bf16[4,2,656,128]{3,2,1,0:T(8,128)(2,1)S(1)}, u32[]{:S(2)}) copy-start(bf16[4,2,656,128]{3,2,1,0:T(8,128)(2,1)S(1)} %collective-permute-done.16.refs_8_) | copy-start | bytes 4030468
  93.4 7.1 %collective-permute-start.19 = (bf16[4,2,656,128]{3,2,1,0:T(8,128)(2,1)S(1)}, bf16[4,2,656,128]{3,2,1,0:T(8,128)(2,1)S(1)}, u32[]{:S(2)}, u32[]{:S(2)}) collective-permute-start(bf16[4,2,656,128]{3,2,1,0:T(8,128)(2,1)S(1)} %collective-permute-done.12.refs_3_), channel_id=1, source_target_pairs={{0,1},{1,0},{2,3},{3,2},{4,5},{5,4},{6,7},{7,6},{8,9},{9,8},{10,11... | collective-permute-start | bytes 4030472 | tf_op jit(solution)/shard_map/ppermute | solution.py:411
  93.5 8.2 %copy-start.6 = (bf16[4,2,656,128]{3,2,1,0:T(8,128)(2,1)}, bf16[4,2,656,128]{3,2,1,0:T(8,128)(2,1)S(1)}, u32[]{:S(2)}) copy-start(bf16[4,2,656,128]{3,2,1,0:T(8,128)(2,1)S(1)} %collective-permute-done.22.refs_14_) | copy-start | bytes 4030468
  93.5 8.2 %collective-permute-start.23 = (bf16[4,2,656,128]{3,2,1,0:T(8,128)(2,1)S(1)}, bf16[4,2,656,128]{3,2,1,0:T(8,128)(2,1)}, u32[]{:S(2)}, u32[]{:S(2)}) collective-permute-start(bf16[4,2,656,128]{3,2,1,0:T(8,128)(2,1)S(1)} %collective-permute-done.13.refs_7_), channel_id=1, source_target_pairs={{0,1},{1,0},{2,3},{3,2},{4,5},{5,4},{6,7},{7,6},{8,9},{9,8},{10,11... | collective-permute-start | bytes 4030472 | tf_op jit(solution)/shard_map/ppermute | solution.py:411
  98.6 3.1 %copy-start.9 = (bf16[4,2,656,128]{3,2,1,0:T(8,128)(2,1)}, bf16[4,2,656,128]{3,2,1,0:T(8,128)(2,1)S(1)}, u32[]{:S(2)}) copy-start(bf16[4,2,656,128]{3,2,1,0:T(8,128)(2,1)S(1)} %collective-permute-done.18.refs_10_) | copy-start | bytes 4030468
  98.6 3.1 %copy-start.7 = (bf16[4,2,656,128]{3,2,1,0:T(8,128)(2,1)}, bf16[4,2,656,128]{3,2,1,0:T(8,128)(2,1)S(1)}, u32[]{:S(2)}) copy-start(bf16[4,2,656,128]{3,2,1,0:T(8,128)(2,1)S(1)} %collective-permute-done.17.refs_9_) | copy-start | bytes 4030468
  98.7 3.1 %copy-start.8 = (bf16[4,2,656,128]{3,2,1,0:T(8,128)(2,1)}, bf16[4,2,656,128]{3,2,1,0:T(8,128)(2,1)S(1)}, u32[]{:S(2)}) copy-start(bf16[4,2,656,128]{3,2,1,0:T(8,128)(2,1)S(1)} %collective-permute-done.21.refs_13_) | copy-start | bytes 4030468
  100.6 1.1 copy-start.10

commit v5 on v4

--- a/solution.py
+++ b/solution.py
@@ -223,13 +223,15 @@
         )
 
     def start(i, carry):
-        for piece in range(4):
-            chosen, k = place_ref[2 * piece, i], place_ref[2 * piece + 1, i]
+        for piece in range(2):
+            chosen_one = place_ref[2 * piece, i]
+            k, other_k = place_ref[2 * piece + 1, i], place_ref[2 * piece + 5, i]
             for source in range(4):
 
-                @pl.when(chosen == source)
+                @pl.when(chosen_one == source)
                 def _():
                     copy(source, k, i, piece).start()
+                    copy((0, 2, 1, 3)[source], other_k, i, piece + 2).start()
 
         return carry
 
@@ -258,37 +260,34 @@
             ]
             return jnp.concatenate(halves, axis=1)
 
-        hidden = [None] * TOGETHER
-        for half in range(2):
-            for k in each:
-                begin = starts_ref[first + k]
-                patches = jnp.concatenate(
-                    [
-                        jnp.concatenate(
-                            [table_ref[begin + 8 * c + 4 * half + 2 * j] for j in range(2)], axis=1
-                        )
-                        for c in range(8)
-                    ],
-                    axis=0,
-                )
-                stem = joined_lanes(k, range(4 * half, 4 * half + 4), 0, 64)
-                term = jnp.dot(patches, stem, preferred_element_type=F32)
-                hidden[k] = term if half == 0 else hidden[k] + term
-        total = [hidden[k].astype(BF16).astype(F32) for k in each]
+        hidden = []
+        for k in each:
+            begin = starts_ref[first + k]
+            patches = jnp.concatenate(
+                [
+                    jnp.concatenate(
+                        [table_ref[begin + 8 * c + 2 * j] for j in range(4)], axis=1
+                    )
+                    for c in range(8)
+                ],
+                axis=0,
+            )
+            stem = joined_lanes(k, range(8), 0, 64)
+            hidden.append(jnp.dot(patches, stem, preferred_element_type=F32))
+        wides = [hidden[k].astype(BF16).astype(F32) for k in each]
         normed = []
         for k in each:
-            power = jnp.mean(total[k] * total[k], axis=-1, keepdims=True)
-            normed.append((total[k] * lax.rsqrt(power + 1e-05)).astype(BF16))
-        for pair in range(4):
-            parts = (2 * pair, 2 * pair + 1)
-            up = []
-            for k in each:
-                expand = jnp.concatenate([rows_of(k, p, EXPAND_AT, 256) for p in parts], axis=1)
-                wide = jnp.dot(normed[k], expand, preferred_element_type=F32)
-                up.append(jnp.maximum(wide, 0.0).astype(BF16))
-            for k in each:
-                shrink = joined_lanes(k, parts, SHRINK_AT, 128)
-                total[k] = total[k] + jnp.dot(up[k], shrink, preferred_element_type=F32)
+            power = jnp.mean(wides[k] * wides[k], axis=-1, keepdims=True)
+            normed.append((wides[k] * lax.rsqrt(power + 1e-05)).astype(BF16))
+        ups = []
+        for k in each:
+            expand = jnp.concatenate([rows_of(k, p, EXPAND_AT, 256) for p in range(8)], axis=1)
+            wide = jnp.dot(normed[k], expand, preferred_element_type=F32)
+            ups.append([jnp.maximum(wide, 0.0).astype(BF16)])
+        total = []
+        for k in each:
+            shrink = joined_lanes(k, range(8), SHRINK_AT, 128)
+            total.append(wides[k] + jnp.dot(jnp.concatenate(ups[k], axis=1), shrink, preferred_element_type=F32))
         for k in each:
             last = total[k].astype(BF16).astype(F32)
             pooled = jnp.sum(last, axis=0, keepdims=True) * (1.0 / last.shape[0])
@@ -392,8 +391,8 @@
     mates = lax.all_to_all(sent, "line", split_axis=0, concat_axis=0, tiled=True)
     mate = lax.dynamic_index_in_dim(mates, partner[tile_me] // posts, 0, keepdims=False)
     mate = mate.reshape(HALO, rows, 128)
-    (stream_a[1], stream_b[1]), mate = lax.optimization_barrier(
-        ((stream_a[1], stream_b[1]), mate)
+    (stream_a[1], stream_b[1]), mate, before, after = lax.optimization_barrier(
+        ((stream_a[1], stream_b[1]), mate, before, after)
     )
     stream_a, stream_b = far(stream_a, "line"), far(stream_b, "post")
 

time: 116 us -> 113 us (0.974)
  waiting for transfers between devices: 22.7 us -> 14.8 us
  starting transfers between devices: 45.8 us -> 49.9 us
  local copies, waits for them, and re-layouts: 7.59 us -> 9.15 us
    all_to_all x1, waiting for transfers between devices: 11 us -> 0.01 us  [body(): lax.all_to_all(sent, 'line', split_axis=0, concat_axis=0, tiled=True)]
    ppermute x1, starting transfers between devices: 1.92 us -> 7.83 us  [body(): mate_after = lax.ppermute(mate, slab_axes, down)]
    ppermute x1, starting transfers between devices: 10.6 us -> 6.22 us  [body(): after = lax.ppermute(own[:HALO], slab_axes, down)]
    ppermute x12, waiting for transfers between devices: 5.1 us -> 8.19 us  [trade(): return lax.ppermute(value, (axis, 'core'), pairs)]
    ppermute x8, starting transfers between devices: 9.33 us -> 11 us  [body(): weights = weights + [lax.ppermute(value, 'core', swap) for value in weights]]
  transfers between devices with their start and end apart: 25 -> 25, of which waited for: 4 -> 4; matrix products, arithmetic and copies ran while one was open for 7% -> 9% of each run, Pallas kernels for 8% -> 8%
where the time goes in v5:
time: 113 us; the launch traced here: 112 us
  starting transfers between devices  49.9 us (44%)
  Pallas kernels  24.1 us (21%)
  waiting for transfers between devices  14.8 us (13%)
  between operations  11.2 us (10%)
  local copies, waits for them, and re-layouts  9.15 us (8%)
  other arithmetic  2.91 us (3%)
    ppermute x12, starting transfers between devices, trade(): return lax.ppermute(value, (axis, 'core'), pairs)  14.7 us
    pallas_call x1, Pallas kernels, classify(): pl.pallas_call(classify_kernel, out_shape=jax.ShapeDtypeStruct((8, count)...  12.3 us
    ppermute x8, starting transfers between devices, body(): weights = weights + [lax.ppermute(value, 'core', swap) for value in weights]  11 us
    pallas_call x1, Pallas kernels, filter_band(): pl.pallas_call(band_kernel, out_shape=(jax.ShapeDtypeStruct((planes, rows...  9.43 us
    ppermute x12, waiting for transfers between devices, trade(): return lax.ppermute(value, (axis, 'core'), pairs)  8.19 us
    ppermute x1, starting transfers between devices, body(): mate_after = lax.ppermute(mate, slab_axes, down)  7.83 us
    ppermute x8, waiting for transfers between devices, body(): weights = weights + [lax.ppermute(value, 'core', swap) for value in weights]  6.62 us
    ppermute x1, starting transfers between devices, body(): after = lax.ppermute(own[:HALO], slab_axes, down)  6.22 us
  transfers between devices with their start and end apart: 25, of which 4 were waited for; matrix products, arithmetic and copies ran while one was open for 9% of the time, Pallas kernels for 8%

profile of v5, /device:TPU:1, one launch (start us, length us, event | category | flops | bytes accessed | tf_op | source)
XLA Modules:
  0.0 112.0 jit_solution(11705539734515704853)
XLA Ops:
  0.7 2.3 %pack_parts.1 = (bf16[2,784,128]{2,1,0:T(8,128)(2,1)}, bf16[2,656,128]{2,1,0:T(8,128)(2,1)}) custom-call(s32[1]{0:T(128)} %bitcast.core_ref, bf16[512,256]{1,0:T(8,128)(2,1)} %bitcast.70, bf16[256,1024]{1,0:T(8,128)(2,1)} %bitcast.64, bf16[1024,256]{1,0:T(8,128)(2,1)} %bitcast.65, bf16[8,256]{1,0:T(8,128)(2,1)} %bitcast.71, bf16[16,64,256]{2,1,0:T(8,128)(2,1)} %bitcast.58), custom_call_target="tpu_custom_call" | custom-call | bytes 2097152 | tf_op jit(solution)/shard_map/pack_parts/pallas_call | solution.py:67
  3.0 2.1 %collective-permute-start.5 = (bf16[2,656,128]{2,1,0:T(8,128)(2,1)}, bf16[2,656,128]{2,1,0:T(8,128)(2,1)S(1)}, u32[]{:S(2)}, u32[]{:S(2)}) collective-permute-start(bf16[2,656,128]{2,1,0:T(8,128)(2,1)} %get-tuple-element.21), channel_id=1, source_target_pairs={{0,96},{1,33},{32,64},{33,1},{64,32},{65,97},{96,0},{97,65},{2,98}... | collective-permute-start | bytes 1007624 | tf_op jit(solution)/shard_map/ppermute | solution.py:333
  5.1 1.9 %collective-permute-start.4 = (bf16[2,656,128]{2,1,0:T(8,128)(2,1)}, bf16[2,656,128]{2,1,0:T(8,128)(2,1)S(1)}, u32[]{:S(2)}, u32[]{:S(2)}) collective-permute-start(bf16[2,656,128]{2,1,0:T(8,128)(2,1)} %get-tuple-element.21), channel_id=1, source_target_pairs={{0,32},{1,97},{32,0},{33,65},{64,96},{65,33},{96,64},{97,1},{2,34}... | collective-permute-start | bytes 1007624 | tf_op jit(solution)/shard_map/ppermute | solution.py:333
  7.0 1.6 %collective-permute-start.1 = (bf16[2,784,128]{2,1,0:T(8,128)(2,1)}, bf16[2,784,128]{2,1,0:T(8,128)(2,1)S(1)}, u32[]{:S(2)}, u32[]{:S(2)}) collective-permute-start(bf16[2,784,128]{2,1,0:T(8,128)(2,1)} %get-tuple-element.18), channel_id=1, source_target_pairs={{0,24},{1,9},{8,16},{9,1},{16,8},{17,25},{24,0},{25,17},{2,26},{3,... | collective-permute-start | bytes 1204232 | tf_op jit(solution)/shard_map/ppermute | solution.py:333
  8.6 2.2 %collective-permute-start = (bf16[2,784,128]{2,1,0:T(8,128)(2,1)}, bf16[2,784,128]{2,1,0:T(8,128)(2,1)S(1)}, u32[]{:S(2)}, u32[]{:S(2)}) collective-permute-start(bf16[2,784,128]{2,1,0:T(8,128)(2,1)} %get-tuple-element.18), channel_id=1, source_target_pairs={{0,8},{1,25},{8,0},{9,17},{16,24},{17,9},{24,16},{25,1},{2,10},{3,... | collective-permute-start | bytes 1204232 | tf_op jit(solution)/shard_map/ppermute | solution.py:333
  10.9 0.9 slice_bitcast_fusion.7
  11.7 1.0 slice_bitcast_fusion.3
  12.8 0.7 fusion.5
  21.1 0.7 dynamic_slice.35
  21.8 0.7 pad_add_fusion.scalars_ref
  22.5 0.0 collective-permute-done.4
  22.5 0.4 collective-permute-start.6
  23.0 0.0 collective-permute-done
  23.0 0.7 collective-permute-start.2
  23.7 0.0 collective-permute-done.1
  23.7 0.0 copy-start.11
  23.8 0.0 collective-permute-done.5
  23.8 5.1 %collective-permute-done.6 = bf16[2,656,128]{2,1,0:T(8,128)(2,1)S(1)} collective-permute-done((bf16[2,656,128]{2,1,0:T(8,128)(2,1)S(1)}, bf16[2,656,128]{2,1,0:T(8,128)(2,1)S(1)}, u32[]{:S(2)}, u32[]{:S(2)}) %collective-permute-start.6) | collective-permute-done | bytes 335904 | tf_op jit(solution)/shard_map/ppermute | solution.py:333
  28.9 1.2 %pad_maximum_fusion.1.refs_4_ = bf16[4,2,656,128]{3,2,1,0:T(8,128)(2,1)} fusion(bf16[1,2,656,128]{3,2,1,0:T(8,128)(2,1)S(1)} %bitcast.69, bf16[1,2,656,128]{3,2,1,0:T(8,128)(2,1)S(1)} %bitcast.67, bf16[1,2,656,128]{3,2,1,0:T(8,128)(2,1)S(1)} %bitcast.68, bf16[1,2,656,128]{3,2,1,0:T(8,128)(2,1)S(1)} %bitcast.66), kind=kLoop, calls=%fused_computation.1 | loop fusion | flops 2015232 | bytes 2686976 | tf_op jit(solution)/shard_map/stack | solution.py:388
  30.1 0.4 collective-permute-start.7
  30.6 0.0 collective-permute-done.2
  30.6 0.2 pad_maximum_fusion.refs_0_
  30.8 0.0 copy-start.1
  30.8 0.9 collective-permute-start.3
  31.6 0.8 slice_bitcast_fusion.5
  32.5 0.8 slice_bitcast_fusion.6
  33.4 0.7 pad_maximum_fusion.3
  34.2 4.0 %all-to-all-start = ((bf16[4,2,128,128]{3,2,1,0:T(8,128)(2,1)}), bf16[4,2,128,128]{3,2,1,0:T(8,128)(2,1)}, u32[]{:S(2)}, u32[]{:S(2)}) async-start(bf16[4,2,128,128]{3,2,1,0:T(8,128)(2,1)} %pad_maximum_fusion.3), calls=%async_computation | async-start | bytes 524288 | tf_op jit(solution)/shard_map/all_to_all | solution.py:391
  38.2 0.7 fusion.4
  39.0 6.2 %collective-permute-start.9 = (bf16[4,64,256]{2,1,0:T(8,128)(2,1)}, bf16[4,64,256]{2,1,0:T(8,128)(2,1)S(1)}, u32[]{:S(2)}, u32[]{:S(2)}) collective-permute-start(bf16[4,64,256]{2,1,0:T(8,128)(2,1)} %get-tuple-element.38), channel_id=1, source_target_pairs={{1,0},{2,1},{3,2},{4,3},{5,4},{6,5},{7,6},{9,8},{10,9},{11,10},{12... | collective-permute-start | bytes 393224 | tf_op jit(solution)/shard_map/ppermute | solution.py:379
  45.2 3.0 %collective-permute-start.8 = (bf16[4,64,256]{2,1,0:T(8,128)(2,1)}, bf16[4,64,256]{2,1,0:T(8,128)(2,1)S(1)}, u32[]{:S(2)}, u32[]{:S(2)}) collective-permute-start(bf16[4,64,256]{2,1,0:T(8,128)(2,1)} %get-tuple-element.39), channel_id=1, source_target_pairs={{0,1},{1,2},{2,3},{3,4},{4,5},{5,6},{6,7},{8,9},{9,10},{10,11},{11... | collective-permute-start | bytes 393224 | tf_op jit(solution)/shard_map/ppermute | solution.py:378
  50.7 0.7 collective-permute-start.15
  51.4 0.0 all-to-all-done
  51.4 0.8 constant_dynamic-slice_fusion
  52.2 0.0 collective-permute-done.9.after_ref
  52.2 0.0 collective-permute-done.8.before_ref
  52.3 0.0 collective-permute-done.7.refs_5_
  52.3 0.0 collective-permute-done.3.refs_1_
  52.3 0.0 copy-start.2
  52.3 1.8 %collective-permute-start.12 = (bf16[4,2,656,128]{3,2,1,0:T(8,128)(2,1)S(1)}, bf16[4,2,656,128]{3,2,1,0:T(8,128)(2,1)S(1)}, u32[]{:S(2)}, u32[]{:S(2)}) collective-permute-start(bf16[4,2,656,128]{3,2,1,0:T(8,128)(2,1)S(1)} %collective-permute-done.3.refs_1_), channel_id=1, source_target_pairs={{0,96},{1,33},{32,64},{33,1},{64,32},{65,97},{96,0},{97,65},{2,98}... | collective-permute-start | bytes 4030472 | tf_op jit(solution)/shard_map/ppermute | solution.py:333
  54.1 7.8 %collective-permute-start.11 = (bf16[4,64,128]{2,1,0:T(8,128)(2,1)S(1)}, bf16[4,64,128]{2,1,0:T(8,128)(2,1)S(1)}, u32[]{:S(2)}, u32[]{:S(2)}) collective-permute-start(bf16[4,64,128]{2,1,0:T(8,128)(2,1)S(1)} %bitcast.61), channel_id=1, source_target_pairs={{1,0},{2,1},{3,2},{4,3},{5,4},{6,5},{7,6},{9,8},{10,9},{11,10},{12... | collective-permute-start | bytes 196616 | tf_op jit(solution)/shard_map/ppermute | solution.py:400
  61.9 3.0 %collective-permute-start.10 = (bf16[4,64,128]{2,1,0:T(8,128)(2,1)S(1)}, bf16[4,64,128]{2,1,0:T(8,128)(2,1)S(1)}, u32[]{:S(2)}, u32[]{:S(2)}) collective-permute-start(bf16[4,64,128]{2,1,0:T(8,128)(2,1)S(1)} %bitcast.62), channel_id=1, source_target_pairs={{0,1},{1,2},{2,3},{3,4},{4,5},{5,6},{6,7},{8,9},{9,10},{10,11},{11... | collective-permute-start | bytes 196616 | tf_op jit(solution)/shard_map/ppermute | solution.py:399
  65.0 0.1 collective-permute-start.13
  65.1 3.1 %collective-permute-done.15.refs_6_ = bf16[4,2,656,128]{3,2,1,0:T(8,128)(2,1)} collective-permute-done((bf16[4,2,656,128]{3,2,1,0:T(8,128)(2,1)}, bf16[4,2,656,128]{3,2,1,0:T(8,128)(2,1)}, u32[]{:S(2)}, u32[]{:S(2)}) %collective-permute-start.15) | collective-permute-done | bytes 1343520 | tf_op jit(solution)/shard_map/ppermute | solution.py:333
  68.2 1.5 %collective-permute-start.20 = (bf16[4,2,656,128]{3,2,1,0:T(8,128)(2,1)}, bf16[4,2,656,128]{3,2,1,0:T(8,128)(2,1)S(1)}, u32[]{:S(2)}, u32[]{:S(2)}) collective-permute-start(bf16[4,2,656,128]{3,2,1,0:T(8,128)(2,1)} %pad_maximum_fusion.1.refs_4_), channel_id=1, source_target_pairs={{0,1},{1,0},{2,3},{3,2},{4,5},{5,4},{6,7},{7,6},{8,9},{9,8},{10,11... | collective-permute-start | bytes 4030472 | tf_op jit(solution)/shard_map/ppermute | solution.py:410
  69.6 0.0 collective-permute-done.11.mate_after_ref
  69.6 1.7 %collective-permute-start.14 = (bf16[4,2,656,128]{3,2,1,0:T(8,128)(2,1)S(1)}, bf16[4,2,656,128]{3,2,1,0:T(8,128)(2,1)S(1)}, u32[]{:S(2)}, u32[]{:S(2)}) collective-permute-start(bf16[4,2,656,128]{3,2,1,0:T(8,128)(2,1)S(1)} %pad_maximum_fusion.refs_0_), channel_id=1, source_target_pairs={{0,96},{1,33},{32,64},{33,1},{64,32},{65,97},{96,0},{97,65},{2,98}... | collective-permute-start | bytes 4030472 | tf_op jit(solution)/shard_map/ppermute | solution.py:333
  71.3 1.5 %collective-permute-start.16 = (bf16[4,2,656,128]{3,2,1,0:T(8,128)(2,1)S(1)}, bf16[4,2,656,128]{3,2,1,0:T(8,128)(2,1)S(1)}, u32[]{:S(2)}, u32[]{:S(2)}) collective-permute-start(bf16[4,2,656,128]{3,2,1,0:T(8,128)(2,1)S(1)} %pad_maximum_fusion.refs_0_), channel_id=1, source_target_pairs={{0,1},{1,0},{2,3},{3,2},{4,5},{5,4},{6,7},{7,6},{8,9},{9,8},{10,11... | collective-permute-start | bytes 4030472 | tf_op jit(solution)/shard_map/ppermute | solution.py:410
  72.8 4.0 %collective-permute-start.22 = (bf16[4,2,656,128]{3,2,1,0:T(8,128)(2,1)}, bf16[4,2,656,128]{3,2,1,0:T(8,128)(2,1)S(1)}, u32[]{:S(2)}, u32[]{:S(2)}) collective-permute-start(bf16[4,2,656,128]{3,2,1,0:T(8,128)(2,1)} %collective-permute-done.15.refs_6_), channel_id=1, source_target_pairs={{0,1},{1,0},{2,3},{3,2},{4,5},{5,4},{6,7},{7,6},{8,9},{9,8},{10,11... | collective-permute-start | bytes 4030472 | tf_op jit(solution)/shard_map/ppermute | solution.py:410
  76.8 9.4 %filter_band.1 = (f32[16,64,256]{2,1,0:T(8,128)}, bf16[8192,128]{1,0:T(8,128)(2,1)S(1)}) custom-call(s32[3]{0:T(128)S(1)} %pad_add_fusion.scalars_ref, bf16[4,64,256]{2,1,0:T(8,128)(2,1)S(1)} %collective-permute-done.8.before_ref, bf16[16,64,256]{2,1,0:T(8,128)(2,1)S(1)} %bitcast.60, bf16[4,64,256]{2,1,0:T(8,128)(2,1)S(1)} %collective-permute-done.9.after_ref, ...), custom_call_target="tpu_custom_call" | custom-call | flops 2000000000 | bytes 6291456 | tf_op jit(solution)/shard_map/filter_band/pallas_call | solution.py:179
  86.2 1.3 %copy-done = bf16[8192,128]{1,0:T(8,128)(2,1)} copy-done((bf16[8192,128]{1,0:T(8,128)(2,1)}, bf16[8192,128]{1,0:T(8,128)(2,1)S(1)}, u32[]{:S(2)}) %copy-start) | copy-done | bytes 2097176
  87.6 0.0 collective-permute-done.13.refs_7_
  87.6 0.0 collective-permute-start.17
  87.6 0.5 collective-permute-start.21
  88.1 3.1 %collective-permute-start.18 = (bf16[4,2,656,128]{3,2,1,0:T(8,128)(2,1)S(1)}, bf16[4,2,656,128]{3,2,1,0:T(8,128)(2,1)S(1)}, u32[]{:S(2)}, u32[]{:S(2)}) collective-permute-start(bf16[4,2,656,128]{3,2,1,0:T(8,128)(2,1)S(1)} %collective-permute-done.14.refs_2_), channel_id=1, source_target_pairs={{0,1},{1,0},{2,3},{3,2},{4,5},{5,4},{6,7},{7,6},{8,9},{9,8},{10,11... | collective-permute-start | bytes 4030472 | tf_op jit(solution)/shard_map/ppermute | solution.py:410
  91.2 0.0 collective-permute-done.16.refs_8_
  91.2 0.1 collective-permute-start.19
  91.3 0.4 collective-permute-start.23
  91.7 4.7 %collective-permute-done.18.refs_10_ = bf16[4,2,656,128]{3,2,1,0:T(8,128)(2,1)S(1)} collective-permute-done((bf16[4,2,656,128]{3,2,1,0:T(8,128)(2,1)S(1)}, bf16[4,2,656,128]{3,2,1,0:T(8,128)(2,1)S(1)}, u32[]{:S(2)}, u32[]{:S(2)}) %collective-permute-start.18) | collective-permute-done | bytes 1343520 | tf_op jit(solution)/shard_map/ppermute | solution.py:410
  96.4 0.0 collective-permute-done.17.refs_9_
  96.4 1.9 %collective-permute-done.19.refs_11_ = bf16[4,2,656,128]{3,2,1,0:T(8,128)(2,1)S(1)} collective-permute-done((bf16[4,2,656,128]{3,2,1,0:T(8,128)(2,1)S(1)}, bf16[4,2,656,128]{3,2,1,0:T(8,128)(2,1)S(1)}, u32[]{:S(2)}, u32[]{:S(2)}) %collective-permute-start.19) | collective-permute-done | bytes 1343520 | tf_op jit(solution)/shard_map/ppermute | solution.py:410
  98.3 1.1 %copy-done.10 = bf16[4,2,656,128]{3,2,1,0:T(8,128)(2,1)} copy-done((bf16[4,2,656,128]{3,2,1,0:T(8,128)(2,1)}, bf16[4,2,656,128]{3,2,1,0:T(8,128)(2,1)S(1)}, u32[]{:S(2)}) %copy-start.10) | copy-done | bytes 1343512
  99.5 0.0 collective-permute-done.23.refs_15_
  99.5 12.3 %classify.1 = f32[8,16]{1,0:T(8,128)} custom-call(s32[16]{0:T(128)S(1)} %copy-done.2, s32[9,16]{1,0:T(8,128)S(1)} %stack.74.place_ref, bf16[256,32,128]{2,1,0:T(8,128)(2,1)} %bitcast.57, bf16[4,2,656,128]{3,2,1,0:T(8,128)(2,1)S(1)} %pad_maximum_fusion.refs_0_, bf16[4,2,656,128]{3,2,1,0:T(8,128)(2,1)S(1)} %collective-permute-done.3.refs_1_, ...), custom_call_target="tpu_custom_call" | custom-call | flops 5500000256 | bytes 25165824 | tf_op jit(solution)/shard_map/classify/pallas_call | solution.py:305
  (45 shorter events, 0.3 us)
Async XLA Ops:
  0.6 12.1 %copy-start.15 = (s32[16,1]{0,1:T(1,128)S(1)}, s32[16,1]{0,1:T(1,128)}, u32[]{:S(2)}) copy-start(s32[16,1]{0,1:T(1,128)} %param.13) | copy-start | bytes 196
  0.6 12.2 %copy-start.14 = (s32[16]{0:T(128)S(1)}, s32[16]{0:T(128)}, u32[]{:S(2)}) copy-start(s32[16]{0:T(128)} %param.10) | copy-start | bytes 196
  0.7 20.5 %copy-start.16 = (s32[16]{0:T(128)S(1)}, s32[16]{0:T(128)}, u32[]{:S(2)}) copy-start(s32[16]{0:T(128)} %param.11) | copy-start | bytes 196
  3.0 25.9 %copy-start.13 = (bf16[2,656,128]{2,1,0:T(8,128)(2,1)S(1)}, bf16[2,656,128]{2,1,0:T(8,128)(2,1)}, u32[]{:S(2)}) copy-start(bf16[2,656,128]{2,1,0:T(8,128)(2,1)} %get-tuple-element.21) | copy-start | bytes 1007620
  3.0 20.8 %collective-permute-start.5 = (bf16[2,656,128]{2,1,0:T(8,128)(2,1)}, bf16[2,656,128]{2,1,0:T(8,128)(2,1)S(1)}, u32[]{:S(2)}, u32[]{:S(2)}) collective-permute-start(bf16[2,656,128]{2,1,0:T(8,128)(2,1)} %get-tuple-element.21), channel_id=1, source_target_pairs={{0,96},{1,33},{32,64},{33,1},{64,32},{65,97},{96,0},{97,65},{2,98}... | collective-permute-start | bytes 1007624 | tf_op jit(solution)/shard_map/ppermute | solution.py:333
  5.1 17.5 %collective-permute-start.4 = (bf16[2,656,128]{2,1,0:T(8,128)(2,1)}, bf16[2,656,128]{2,1,0:T(8,128)(2,1)S(1)}, u32[]{:S(2)}, u32[]{:S(2)}) collective-permute-start(bf16[2,656,128]{2,1,0:T(8,128)(2,1)} %get-tuple-element.21), channel_id=1, source_target_pairs={{0,32},{1,97},{32,0},{33,65},{64,96},{65,33},{96,64},{97,1},{2,34}... | collective-permute-start | bytes 1007624 | tf_op jit(solution)/shard_map/ppermute | solution.py:333
  7.0 16.8 %collective-permute-start.1 = (bf16[2,784,128]{2,1,0:T(8,128)(2,1)}, bf16[2,784,128]{2,1,0:T(8,128)(2,1)S(1)}, u32[]{:S(2)}, u32[]{:S(2)}) collective-permute-start(bf16[2,784,128]{2,1,0:T(8,128)(2,1)} %get-tuple-element.18), channel_id=1, source_target_pairs={{0,24},{1,9},{8,16},{9,1},{16,8},{17,25},{24,0},{25,17},{2,26},{3,... | collective-permute-start | bytes 1204232 | tf_op jit(solution)/shard_map/ppermute | solution.py:333
  8.6 14.3 %collective-permute-start = (bf16[2,784,128]{2,1,0:T(8,128)(2,1)}, bf16[2,784,128]{2,1,0:T(8,128)(2,1)S(1)}, u32[]{:S(2)}, u32[]{:S(2)}) collective-permute-start(bf16[2,784,128]{2,1,0:T(8,128)(2,1)} %get-tuple-element.18), channel_id=1, source_target_pairs={{0,8},{1,25},{8,0},{9,17},{16,24},{17,9},{24,16},{25,1},{2,10},{3,... | collective-permute-start | bytes 1204232 | tf_op jit(solution)/shard_map/ppermute | solution.py:333
  22.5 6.3 %collective-permute-start.6 = (bf16[2,656,128]{2,1,0:T(8,128)(2,1)S(1)}, bf16[2,656,128]{2,1,0:T(8,128)(2,1)S(1)}, u32[]{:S(2)}, u32[]{:S(2)}) collective-permute-start(bf16[2,656,128]{2,1,0:T(8,128)(2,1)S(1)} %collective-permute-done.4), channel_id=1, source_target_pairs={{0,96},{1,33},{32,64},{33,1},{64,32},{65,97},{96,0},{97,65},{2,98}... | collective-permute-start | bytes 1007624 | tf_op jit(solution)/shard_map/ppermute | solution.py:333
  23.0 7.2 %copy-start.12 = (bf16[2,784,128]{2,1,0:T(8,128)(2,1)}, bf16[2,784,128]{2,1,0:T(8,128)(2,1)S(1)}, u32[]{:S(2)}) copy-start(bf16[2,784,128]{2,1,0:T(8,128)(2,1)S(1)} %collective-permute-done) | copy-start | bytes 1204228
  23.0 7.6 %collective-permute-start.2 = (bf16[2,784,128]{2,1,0:T(8,128)(2,1)S(1)}, bf16[2,784,128]{2,1,0:T(8,128)(2,1)S(1)}, u32[]{:S(2)}, u32[]{:S(2)}) collective-permute-start(bf16[2,784,128]{2,1,0:T(8,128)(2,1)S(1)} %collective-permute-done), channel_id=1, source_target_pairs={{0,24},{1,9},{8,16},{9,1},{16,8},{17,25},{24,0},{25,17},{2,26},{3,... | collective-permute-start | bytes 1204232 | tf_op jit(solution)/shard_map/ppermute | solution.py:333
  23.7 6.4 %copy-start.11 = (bf16[2,784,128]{2,1,0:T(8,128)(2,1)}, bf16[2,784,128]{2,1,0:T(8,128)(2,1)S(1)}, u32[]{:S(2)}) copy-start(bf16[2,784,128]{2,1,0:T(8,128)(2,1)S(1)} %collective-permute-done.1) | copy-start | bytes 1204228
  30.1 22.1 %collective-permute-start.7 = (bf16[4,2,656,128]{3,2,1,0:T(8,128)(2,1)}, bf16[4,2,656,128]{3,2,1,0:T(8,128)(2,1)}, u32[]{:S(2)}, u32[]{:S(2)}) collective-permute-start(bf16[4,2,656,128]{3,2,1,0:T(8,128)(2,1)} %pad_maximum_fusion.1.refs_4_), channel_id=1, source_target_pairs={{0,8},{1,25},{8,0},{9,17},{16,24},{17,9},{24,16},{25,1},{2,10},{3,... | collective-permute-start | bytes 4030472 | tf_op jit(solution)/shard_map/ppermute | solution.py:333
  30.8 7.4 %copy-start.1 = (bf16[1,16,64,256]{3,2,1,0:T(8,128)(2,1)S(1)}, bf16[1,16,64,256]{3,2,1,0:T(8,128)(2,1)}, u32[]{:S(2)}) copy-start(bf16[1,16,64,256]{3,2,1,0:T(8,128)(2,1)} %param.9) | copy-start | bytes 1572868
  30.8 21.5 %collective-permute-start.3 = (bf16[4,2,656,128]{3,2,1,0:T(8,128)(2,1)S(1)}, bf16[4,2,656,128]{3,2,1,0:T(8,128)(2,1)S(1)}, u32[]{:S(2)}, u32[]{:S(2)}) collective-permute-start(bf16[4,2,656,128]{3,2,1,0:T(8,128)(2,1)S(1)} %pad_maximum_fusion.refs_0_), channel_id=1, source_target_pairs={{0,32},{1,97},{32,0},{33,65},{64,96},{65,33},{96,64},{97,1},{2,34}... | collective-permute-start | bytes 4030472 | tf_op jit(solution)/shard_map/ppermute | solution.py:333
  34.2 17.2 %all-to-all-start = ((bf16[4,2,128,128]{3,2,1,0:T(8,128)(2,1)}), bf16[4,2,128,128]{3,2,1,0:T(8,128)(2,1)}, u32[]{:S(2)}, u32[]{:S(2)}) async-start(bf16[4,2,128,128]{3,2,1,0:T(8,128)(2,1)} %pad_maximum_fusion.3), calls=%async_computation | async-start | bytes 524288 | tf_op jit(solution)/shard_map/all_to_all | solution.py:391
  39.0 13.3 %collective-permute-start.9 = (bf16[4,64,256]{2,1,0:T(8,128)(2,1)}, bf16[4,64,256]{2,1,0:T(8,128)(2,1)S(1)}, u32[]{:S(2)}, u32[]{:S(2)}) collective-permute-start(bf16[4,64,256]{2,1,0:T(8,128)(2,1)} %get-tuple-element.38), channel_id=1, source_target_pairs={{1,0},{2,1},{3,2},{4,3},{5,4},{6,5},{7,6},{9,8},{10,9},{11,10},{12... | collective-permute-start | bytes 393224 | tf_op jit(solution)/shard_map/ppermute | solution.py:379
  45.2 7.1 %collective-permute-start.8 = (bf16[4,64,256]{2,1,0:T(8,128)(2,1)}, bf16[4,64,256]{2,1,0:T(8,128)(2,1)S(1)}, u32[]{:S(2)}, u32[]{:S(2)}) collective-permute-start(bf16[4,64,256]{2,1,0:T(8,128)(2,1)} %get-tuple-element.39), channel_id=1, source_target_pairs={{0,1},{1,2},{2,3},{3,4},{4,5},{5,6},{6,7},{8,9},{9,10},{10,11},{11... | collective-permute-start | bytes 393224 | tf_op jit(solution)/shard_map/ppermute | solution.py:378
  50.7 17.5 %collective-permute-start.15 = (bf16[4,2,656,128]{3,2,1,0:T(8,128)(2,1)}, bf16[4,2,656,128]{3,2,1,0:T(8,128)(2,1)}, u32[]{:S(2)}, u32[]{:S(2)}) collective-permute-start(bf16[4,2,656,128]{3,2,1,0:T(8,128)(2,1)} %pad_maximum_fusion.1.refs_4_), channel_id=1, source_target_pairs={{0,24},{1,9},{8,16},{9,1},{16,8},{17,25},{24,0},{25,17},{2,26},{3,... | collective-permute-start | bytes 4030472 | tf_op jit(solution)/shard_map/ppermute | solution.py:333
  52.3 47.3 %copy-start.2 = (s32[16]{0:T(128)S(1)}, s32[16]{0:T(128)}, u32[]{:S(2)}) copy-start(s32[16]{0:T(128)} %starts_ref.1) | copy-start | bytes 196
  52.3 20.5 %collective-permute-start.12 = (bf16[4,2,656,128]{3,2,1,0:T(8,128)(2,1)S(1)}, bf16[4,2,656,128]{3,2,1,0:T(8,128)(2,1)S(1)}, u32[]{:S(2)}, u32[]{:S(2)}) collective-permute-start(bf16[4,2,656,128]{3,2,1,0:T(8,128)(2,1)S(1)} %collective-permute-done.3.refs_1_), channel_id=1, source_target_pairs={{0,96},{1,33},{32,64},{33,1},{64,32},{65,97},{96,0},{97,65},{2,98}... | collective-permute-start | bytes 4030472 | tf_op jit(solution)/shard_map/ppermute | solution.py:333
  54.1 15.5 %collective-permute-start.11 = (bf16[4,64,128]{2,1,0:T(8,128)(2,1)S(1)}, bf16[4,64,128]{2,1,0:T(8,128)(2,1)S(1)}, u32[]{:S(2)}, u32[]{:S(2)}) collective-permute-start(bf16[4,64,128]{2,1,0:T(8,128)(2,1)S(1)} %bitcast.61), channel_id=1, source_target_pairs={{1,0},{2,1},{3,2},{4,3},{5,4},{6,5},{7,6},{9,8},{10,9},{11,10},{12... | collective-permute-start | bytes 196616 | tf_op jit(solution)/shard_map/ppermute | solution.py:400
  61.9 9.4 %collective-permute-start.10 = (bf16[4,64,128]{2,1,0:T(8,128)(2,1)S(1)}, bf16[4,64,128]{2,1,0:T(8,128)(2,1)S(1)}, u32[]{:S(2)}, u32[]{:S(2)}) collective-permute-start(bf16[4,64,128]{2,1,0:T(8,128)(2,1)S(1)} %bitcast.62), channel_id=1, source_target_pairs={{0,1},{1,2},{2,3},{3,4},{4,5},{5,6},{6,7},{8,9},{9,10},{10,11},{11... | collective-permute-start | bytes 196616 | tf_op jit(solution)/shard_map/ppermute | solution.py:399
  65.0 22.6 %collective-permute-start.13 = (bf16[4,2,656,128]{3,2,1,0:T(8,128)(2,1)}, bf16[4,2,656,128]{3,2,1,0:T(8,128)(2,1)S(1)}, u32[]{:S(2)}, u32[]{:S(2)}) collective-permute-start(bf16[4,2,656,128]{3,2,1,0:T(8,128)(2,1)} %collective-permute-done.7.refs_5_), channel_id=1, source_target_pairs={{0,24},{1,9},{8,16},{9,1},{16,8},{17,25},{24,0},{25,17},{2,26},{3,... | collective-permute-start | bytes 4030472 | tf_op jit(solution)/shard_map/ppermute | solution.py:333
  68.2 19.4 %collective-permute-start.20 = (bf16[4,2,656,128]{3,2,1,0:T(8,128)(2,1)}, bf16[4,2,656,128]{3,2,1,0:T(8,128)(2,1)S(1)}, u32[]{:S(2)}, u32[]{:S(2)}) collective-permute-start(bf16[4,2,656,128]{3,2,1,0:T(8,128)(2,1)} %pad_maximum_fusion.1.refs_4_), channel_id=1, source_target_pairs={{0,1},{1,0},{2,3},{3,2},{4,5},{5,4},{6,7},{7,6},{8,9},{9,8},{10,11... | collective-permute-start | bytes 4030472 | tf_op jit(solution)/shard_map/ppermute | solution.py:410
  69.6 18.5 %collective-permute-start.14 = (bf16[4,2,656,128]{3,2,1,0:T(8,128)(2,1)S(1)}, bf16[4,2,656,128]{3,2,1,0:T(8,128)(2,1)S(1)}, u32[]{:S(2)}, u32[]{:S(2)}) collective-permute-start(bf16[4,2,656,128]{3,2,1,0:T(8,128)(2,1)S(1)} %pad_maximum_fusion.refs_0_), channel_id=1, source_target_pairs={{0,96},{1,33},{32,64},{33,1},{64,32},{65,97},{96,0},{97,65},{2,98}... | collective-permute-start | bytes 4030472 | tf_op jit(solution)/shard_map/ppermute | solution.py:333
  71.3 19.9 %collective-permute-start.16 = (bf16[4,2,656,128]{3,2,1,0:T(8,128)(2,1)S(1)}, bf16[4,2,656,128]{3,2,1,0:T(8,128)(2,1)S(1)}, u32[]{:S(2)}, u32[]{:S(2)}) collective-permute-start(bf16[4,2,656,128]{3,2,1,0:T(8,128)(2,1)S(1)} %pad_maximum_fusion.refs_0_), channel_id=1, source_target_pairs={{0,1},{1,0},{2,3},{3,2},{4,5},{5,4},{6,7},{7,6},{8,9},{9,8},{10,11... | collective-permute-start | bytes 4030472 | tf_op jit(solution)/shard_map/ppermute | solution.py:410
  72.8 18.5 %collective-permute-start.22 = (bf16[4,2,656,128]{3,2,1,0:T(8,128)(2,1)}, bf16[4,2,656,128]{3,2,1,0:T(8,128)(2,1)S(1)}, u32[]{:S(2)}, u32[]{:S(2)}) collective-permute-start(bf16[4,2,656,128]{3,2,1,0:T(8,128)(2,1)} %collective-permute-done.15.refs_6_), channel_id=1, source_target_pairs={{0,1},{1,0},{2,3},{3,2},{4,5},{5,4},{6,7},{7,6},{8,9},{9,8},{10,11... | collective-permute-start | bytes 4030472 | tf_op jit(solution)/shard_map/ppermute | solution.py:410
  86.2 1.3 %copy-start = (bf16[8192,128]{1,0:T(8,128)(2,1)}, bf16[8192,128]{1,0:T(8,128)(2,1)S(1)}, u32[]{:S(2)}) copy-start(bf16[8192,128]{1,0:T(8,128)(2,1)S(1)} %get-tuple-element.30) | copy-start | bytes 6291460
  87.6 11.9 %copy-start.3 = (bf16[4,2,656,128]{3,2,1,0:T(8,128)(2,1)}, bf16[4,2,656,128]{3,2,1,0:T(8,128)(2,1)S(1)}, u32[]{:S(2)}) copy-start(bf16[4,2,656,128]{3,2,1,0:T(8,128)(2,1)S(1)} %collective-permute-done.13.refs_7_) | copy-start | bytes 4030468
  87.6 8.9 %collective-permute-start.17 = (bf16[4,2,656,128]{3,2,1,0:T(8,128)(2,1)S(1)}, bf16[4,2,656,128]{3,2,1,0:T(8,128)(2,1)S(1)}, u32[]{:S(2)}, u32[]{:S(2)}) collective-permute-start(bf16[4,2,656,128]{3,2,1,0:T(8,128)(2,1)S(1)} %collective-permute-done.3.refs_1_), channel_id=1, source_target_pairs={{0,1},{1,0},{2,3},{3,2},{4,5},{5,4},{6,7},{7,6},{8,9},{9,8},{10,11... | collective-permute-start | bytes 4030472 | tf_op jit(solution)/shard_map/ppermute | solution.py:410
  87.6 11.9 %copy-start.4 = (bf16[4,2,656,128]{3,2,1,0:T(8,128)(2,1)}, bf16[4,2,656,128]{3,2,1,0:T(8,128)(2,1)S(1)}, u32[]{:S(2)}) copy-start(bf16[4,2,656,128]{3,2,1,0:T(8,128)(2,1)S(1)} %collective-permute-done.20.refs_12_) | copy-start | bytes 4030468
  87.6 8.8 %collective-permute-start.21 = (bf16[4,2,656,128]{3,2,1,0:T(8,128)(2,1)}, bf16[4,2,656,128]{3,2,1,0:T(8,128)(2,1)S(1)}, u32[]{:S(2)}, u32[]{:S(2)}) collective-permute-start(bf16[4,2,656,128]{3,2,1,0:T(8,128)(2,1)} %collective-permute-done.7.refs_5_), channel_id=1, source_target_pairs={{0,1},{1,0},{2,3},{3,2},{4,5},{5,4},{6,7},{7,6},{8,9},{9,8},{10,11... | collective-permute-start | bytes 4030472 | tf_op jit(solution)/shard_map/ppermute | solution.py:410
  88.1 8.3 %collective-permute-start.18 = (bf16[4,2,656,128]{3,2,1,0:T(8,128)(2,1)S(1)}, bf16[4,2,656,128]{3,2,1,0:T(8,128)(2,1)S(1)}, u32[]{:S(2)}, u32[]{:S(2)}) collective-permute-start(bf16[4,2,656,128]{3,2,1,0:T(8,128)(2,1)S(1)} %collective-permute-done.14.refs_2_), channel_id=1, source_target_pairs={{0,1},{1,0},{2,3},{3,2},{4,5},{5,4},{6,7},{7,6},{8,9},{9,8},{10,11... | collective-permute-start | bytes 4030472 | tf_op jit(solution)/shard_map/ppermute | solution.py:410
  91.2 8.3 %copy-start.5 = (bf16[4,2,656,128]{3,2,1,0:T(8,128)(2,1)}, bf16[4,2,656,128]{3,2,1,0:T(8,128)(2,1)S(1)}, u32[]{:S(2)}) copy-start(bf16[4,2,656,128]{3,2,1,0:T(8,128)(2,1)S(1)} %collective-permute-done.16.refs_8_) | copy-start | bytes 4030468
  91.2 7.1 %collective-permute-start.19 = (bf16[4,2,656,128]{3,2,1,0:T(8,128)(2,1)S(1)}, bf16[4,2,656,128]{3,2,1,0:T(8,128)(2,1)S(1)}, u32[]{:S(2)}, u32[]{:S(2)}) collective-permute-start(bf16[4,2,656,128]{3,2,1,0:T(8,128)(2,1)S(1)} %collective-permute-done.12.refs_3_), channel_id=1, source_target_pairs={{0,1},{1,0},{2,3},{3,2},{4,5},{5,4},{6,7},{7,6},{8,9},{9,8},{10,11... | collective-permute-start | bytes 4030472 | tf_op jit(solution)/shard_map/ppermute | solution.py:410
  91.3 8.2 %copy-start.6 = (bf16[4,2,656,128]{3,2,1,0:T(8,128)(2,1)}, bf16[4,2,656,128]{3,2,1,0:T(8,128)(2,1)S(1)}, u32[]{:S(2)}) copy-start(bf16[4,2,656,128]{3,2,1,0:T(8,128)(2,1)S(1)} %collective-permute-done.22.refs_14_) | copy-start | bytes 4030468
  91.3 8.2 %collective-permute-start.23 = (bf16[4,2,656,128]{3,2,1,0:T(8,128)(2,1)S(1)}, bf16[4,2,656,128]{3,2,1,0:T(8,128)(2,1)}, u32[]{:S(2)}, u32[]{:S(2)}) collective-permute-start(bf16[4,2,656,128]{3,2,1,0:T(8,128)(2,1)S(1)} %collective-permute-done.13.refs_7_), channel_id=1, source_target_pairs={{0,1},{1,0},{2,3},{3,2},{4,5},{5,4},{6,7},{7,6},{8,9},{9,8},{10,11... | collective-permute-start | bytes 4030472 | tf_op jit(solution)/shard_map/ppermute | solution.py:410
  96.4 3.1 %copy-start.9 = (bf16[4,2,656,128]{3,2,1,0:T(8,128)(2,1)}, bf16[4,2,656,128]{3,2,1,0:T(8,128)(2,1)S(1)}, u32[]{:S(2)}) copy-start(bf16[4,2,656,128]{3,2,1,0:T(8,128)(2,1)S(1)} %collective-permute-done.18.refs_10_) | copy-start | bytes 4030468
  96.4 3.1 %copy-start.7 = (bf16[4,2,656,128]{3,2,1,0:T(8,128)(2,1)}, bf16[4,2,656,128]{3,2,1,0:T(8,128)(2,1)S(1)}, u32[]{:S(2)}) copy-start(bf16[4,2,656,128]{3,2,1,0:T(8,128)(2,1)S(1)} %collective-permute-done.17.refs_9_) | copy-start | bytes 4030468
  96.4 3.1 %copy-start.8 = (bf16[4,2,656,128]{3,2,1,0:T(8,128)(2,1)}, bf16[4,2,656,128]{3,2,1,0:T(8,128)(2,1)S(1)}, u32[]{:S(2)}) copy-start(bf16[4,2,656,128]{3,2,1,0:T(8,128)(2,1)S(1)} %collective-permute-done.21.refs_13_) | copy-start | bytes 4030468
  98.3 1.1 %copy-start.10 = (bf16[4,2,656,128]{3,2,1,0:T(8,128)(2,1)}, bf16[4,2,656,128]{3,2,1,0:T(8,128)(2,1)S(1)}, u32[]{:S(2)}) copy-start(bf16[4,2,656,128]{3,2,1,0:T(8,128)(2,1)S(1)} %collective-permute-done.19.refs_11_) | copy-start | bytes 4030468

commit v6 on v5

--- a/solution.py
+++ b/solution.py
@@ -355,7 +355,8 @@
     )
 
     def near(value, axis):
-        return [value, trade(value, axis, True), trade(value, axis, False)]
+        second_trade = trade(value, axis, False)
+        return [value, trade(value, axis, True), second_trade]
 
     def far(values, axis):
         return values + [trade(values[1], axis, False)]

time: 113 us -> 113 us (level)
  no operation moved by 1% of the time
where the time goes in v6:
time: 113 us; the launch traced here: 112 us
  starting transfers between devices  49.9 us (44%)
  Pallas kernels  24.1 us (21%)
  waiting for transfers between devices  14.8 us (13%)
  between operations  11.2 us (10%)
  local copies, waits for them, and re-layouts  9.15 us (8%)
  other arithmetic  2.91 us (3%)
    ppermute x12, starting transfers between devices, trade(): return lax.ppermute(value, (axis, 'core'), pairs)  14.7 us
    pallas_call x1, Pallas kernels, classify(): pl.pallas_call(classify_kernel, out_shape=jax.ShapeDtypeStruct((8, count)...  12.4 us
    ppermute x8, starting transfers between devices, body(): weights = weights + [lax.ppermute(value, 'core', swap) for value in weights]  11 us
    pallas_call x1, Pallas kernels, filter_band(): pl.pallas_call(band_kernel, out_shape=(jax.ShapeDtypeStruct((planes, rows...  9.43 us
    ppermute x12, waiting for transfers between devices, trade(): return lax.ppermute(value, (axis, 'core'), pairs)  8.19 us
    ppermute x1, starting transfers between devices, body(): mate_after = lax.ppermute(mate, slab_axes, down)  7.83 us
    ppermute x8, waiting for transfers between devices, body(): weights = weights + [lax.ppermute(value, 'core', swap) for value in weights]  6.62 us
    ppermute x1, starting transfers between devices, body(): after = lax.ppermute(own[:HALO], slab_axes, down)  6.22 us
  transfers between devices with their start and end apart: 25, of which 4 were waited for; matrix products, arithmetic and copies ran while one was open for 9% of the time, Pallas kernels for 8%

profile of v6, /device:TPU:1, one launch (start us, length us, event | category | flops | bytes accessed | tf_op | source)
XLA Modules:
  0.0 112.1 jit_solution(11705539734515704853)
XLA Ops:
  0.7 2.3 %pack_parts.1 = (bf16[2,784,128]{2,1,0:T(8,128)(2,1)}, bf16[2,656,128]{2,1,0:T(8,128)(2,1)}) custom-call(s32[1]{0:T(128)} %bitcast.core_ref, bf16[512,256]{1,0:T(8,128)(2,1)} %bitcast.70, bf16[256,1024]{1,0:T(8,128)(2,1)} %bitcast.64, bf16[1024,256]{1,0:T(8,128)(2,1)} %bitcast.65, bf16[8,256]{1,0:T(8,128)(2,1)} %bitcast.71, bf16[16,64,256]{2,1,0:T(8,128)(2,1)} %bitcast.58), custom_call_target="tpu_custom_call" | custom-call | bytes 2097152 | tf_op jit(solution)/shard_map/pack_parts/pallas_call | solution.py:67
  3.0 2.1 %collective-permute-start.5 = (bf16[2,656,128]{2,1,0:T(8,128)(2,1)}, bf16[2,656,128]{2,1,0:T(8,128)(2,1)S(1)}, u32[]{:S(2)}, u32[]{:S(2)}) collective-permute-start(bf16[2,656,128]{2,1,0:T(8,128)(2,1)} %get-tuple-element.21), channel_id=1, source_target_pairs={{0,96},{1,33},{32,64},{33,1},{64,32},{65,97},{96,0},{97,65},{2,98}... | collective-permute-start | bytes 1007624 | tf_op jit(solution)/shard_map/ppermute | solution.py:333
  5.1 1.9 %collective-permute-start.4 = (bf16[2,656,128]{2,1,0:T(8,128)(2,1)}, bf16[2,656,128]{2,1,0:T(8,128)(2,1)S(1)}, u32[]{:S(2)}, u32[]{:S(2)}) collective-permute-start(bf16[2,656,128]{2,1,0:T(8,128)(2,1)} %get-tuple-element.21), channel_id=1, source_target_pairs={{0,32},{1,97},{32,0},{33,65},{64,96},{65,33},{96,64},{97,1},{2,34}... | collective-permute-start | bytes 1007624 | tf_op jit(solution)/shard_map/ppermute | solution.py:333
  7.0 1.6 %collective-permute-start.1 = (bf16[2,784,128]{2,1,0:T(8,128)(2,1)}, bf16[2,784,128]{2,1,0:T(8,128)(2,1)S(1)}, u32[]{:S(2)}, u32[]{:S(2)}) collective-permute-start(bf16[2,784,128]{2,1,0:T(8,128)(2,1)} %get-tuple-element.18), channel_id=1, source_target_pairs={{0,24},{1,9},{8,16},{9,1},{16,8},{17,25},{24,0},{25,17},{2,26},{3,... | collective-permute-start | bytes 1204232 | tf_op jit(solution)/shard_map/ppermute | solution.py:333
  8.6 2.2 %collective-permute-start = (bf16[2,784,128]{2,1,0:T(8,128)(2,1)}, bf16[2,784,128]{2,1,0:T(8,128)(2,1)S(1)}, u32[]{:S(2)}, u32[]{:S(2)}) collective-permute-start(bf16[2,784,128]{2,1,0:T(8,128)(2,1)} %get-tuple-element.18), channel_id=1, source_target_pairs={{0,8},{1,25},{8,0},{9,17},{16,24},{17,9},{24,16},{25,1},{2,10},{3,... | collective-permute-start | bytes 1204232 | tf_op jit(solution)/shard_map/ppermute | solution.py:333
  10.9 0.9 slice_bitcast_fusion.7
  11.7 1.0 slice_bitcast_fusion.3
  12.8 0.7 fusion.5
  21.1 0.7 dynamic_slice.35
  21.8 0.7 pad_add_fusion.scalars_ref
  22.5 0.0 collective-permute-done.4
  22.5 0.4 collective-permute-start.6
  23.0 0.0 collective-permute-done
  23.0 0.7 collective-permute-start.2
  23.7 0.0 collective-permute-done.1
  23.7 0.0 copy-start.11
  23.8 5.1 %collective-permute-done.6 = bf16[2,656,128]{2,1,0:T(8,128)(2,1)S(1)} collective-permute-done((bf16[2,656,128]{2,1,0:T(8,128)(2,1)S(1)}, bf16[2,656,128]{2,1,0:T(8,128)(2,1)S(1)}, u32[]{:S(2)}, u32[]{:S(2)}) %collective-permute-start.6) | collective-permute-done | bytes 335904 | tf_op jit(solution)/shard_map/ppermute | solution.py:333
  28.9 1.2 %pad_maximum_fusion.1.refs_4_ = bf16[4,2,656,128]{3,2,1,0:T(8,128)(2,1)} fusion(bf16[1,2,656,128]{3,2,1,0:T(8,128)(2,1)S(1)} %bitcast.69, bf16[1,2,656,128]{3,2,1,0:T(8,128)(2,1)S(1)} %bitcast.67, bf16[1,2,656,128]{3,2,1,0:T(8,128)(2,1)S(1)} %bitcast.68, bf16[1,2,656,128]{3,2,1,0:T(8,128)(2,1)S(1)} %bitcast.66), kind=kLoop, calls=%fused_computation.1 | loop fusion | flops 2015232 | bytes 2686976 | tf_op jit(solution)/shard_map/stack | solution.py:389
  30.1 0.4 collective-permute-start.7
  30.6 0.0 collective-permute-done.2
  30.6 0.2 pad_maximum_fusion.refs_0_
  30.8 0.0 copy-start.1
  30.8 0.9 collective-permute-start.3
  31.6 0.8 slice_bitcast_fusion.5
  32.5 0.8 slice_bitcast_fusion.6
  33.4 0.7 pad_maximum_fusion.3
  34.2 4.0 %all-to-all-start = ((bf16[4,2,128,128]{3,2,1,0:T(8,128)(2,1)}), bf16[4,2,128,128]{3,2,1,0:T(8,128)(2,1)}, u32[]{:S(2)}, u32[]{:S(2)}) async-start(bf16[4,2,128,128]{3,2,1,0:T(8,128)(2,1)} %pad_maximum_fusion.3), calls=%async_computation | async-start | bytes 524288 | tf_op jit(solution)/shard_map/all_to_all | solution.py:392
  38.2 0.7 fusion.4
  39.0 6.2 %collective-permute-start.9 = (bf16[4,64,256]{2,1,0:T(8,128)(2,1)}, bf16[4,64,256]{2,1,0:T(8,128)(2,1)S(1)}, u32[]{:S(2)}, u32[]{:S(2)}) collective-permute-start(bf16[4,64,256]{2,1,0:T(8,128)(2,1)} %get-tuple-element.38), channel_id=1, source_target_pairs={{1,0},{2,1},{3,2},{4,3},{5,4},{6,5},{7,6},{9,8},{10,9},{11,10},{12... | collective-permute-start | bytes 393224 | tf_op jit(solution)/shard_map/ppermute | solution.py:380
  45.2 3.0 %collective-permute-start.8 = (bf16[4,64,256]{2,1,0:T(8,128)(2,1)}, bf16[4,64,256]{2,1,0:T(8,128)(2,1)S(1)}, u32[]{:S(2)}, u32[]{:S(2)}) collective-permute-start(bf16[4,64,256]{2,1,0:T(8,128)(2,1)} %get-tuple-element.39), channel_id=1, source_target_pairs={{0,1},{1,2},{2,3},{3,4},{4,5},{5,6},{6,7},{8,9},{9,10},{10,11},{11... | collective-permute-start | bytes 393224 | tf_op jit(solution)/shard_map/ppermute | solution.py:379
  50.7 0.7 collective-permute-start.15
  51.4 0.0 all-to-all-done
  51.4 0.8 constant_dynamic-slice_fusion
  52.2 0.0 collective-permute-done.9.after_ref
  52.2 0.0 collective-permute-done.8.before_ref
  52.3 0.0 collective-permute-done.3.refs_1_
  52.3 0.0 copy-start.2
  52.3 1.8 %collective-permute-start.12 = (bf16[4,2,656,128]{3,2,1,0:T(8,128)(2,1)S(1)}, bf16[4,2,656,128]{3,2,1,0:T(8,128)(2,1)S(1)}, u32[]{:S(2)}, u32[]{:S(2)}) collective-permute-start(bf16[4,2,656,128]{3,2,1,0:T(8,128)(2,1)S(1)} %collective-permute-done.3.refs_1_), channel_id=1, source_target_pairs={{0,96},{1,33},{32,64},{33,1},{64,32},{65,97},{96,0},{97,65},{2,98}... | collective-permute-start | bytes 4030472 | tf_op jit(solution)/shard_map/ppermute | solution.py:333
  54.1 7.8 %collective-permute-start.11 = (bf16[4,64,128]{2,1,0:T(8,128)(2,1)S(1)}, bf16[4,64,128]{2,1,0:T(8,128)(2,1)S(1)}, u32[]{:S(2)}, u32[]{:S(2)}) collective-permute-start(bf16[4,64,128]{2,1,0:T(8,128)(2,1)S(1)} %bitcast.61), channel_id=1, source_target_pairs={{1,0},{2,1},{3,2},{4,3},{5,4},{6,5},{7,6},{9,8},{10,9},{11,10},{12... | collective-permute-start | bytes 196616 | tf_op jit(solution)/shard_map/ppermute | solution.py:401
  61.9 3.0 %collective-permute-start.10 = (bf16[4,64,128]{2,1,0:T(8,128)(2,1)S(1)}, bf16[4,64,128]{2,1,0:T(8,128)(2,1)S(1)}, u32[]{:S(2)}, u32[]{:S(2)}) collective-permute-start(bf16[4,64,128]{2,1,0:T(8,128)(2,1)S(1)} %bitcast.62), channel_id=1, source_target_pairs={{0,1},{1,2},{2,3},{3,4},{4,5},{5,6},{6,7},{8,9},{9,10},{10,11},{11... | collective-permute-start | bytes 196616 | tf_op jit(solution)/shard_map/ppermute | solution.py:400
  65.0 0.1 collective-permute-start.13
  65.1 3.1 %collective-permute-done.15.refs_6_ = bf16[4,2,656,128]{3,2,1,0:T(8,128)(2,1)} collective-permute-done((bf16[4,2,656,128]{3,2,1,0:T(8,128)(2,1)}, bf16[4,2,656,128]{3,2,1,0:T(8,128)(2,1)}, u32[]{:S(2)}, u32[]{:S(2)}) %collective-permute-start.15) | collective-permute-done | bytes 1343520 | tf_op jit(solution)/shard_map/ppermute | solution.py:333
  68.2 1.5 %collective-permute-start.20 = (bf16[4,2,656,128]{3,2,1,0:T(8,128)(2,1)}, bf16[4,2,656,128]{3,2,1,0:T(8,128)(2,1)S(1)}, u32[]{:S(2)}, u32[]{:S(2)}) collective-permute-start(bf16[4,2,656,128]{3,2,1,0:T(8,128)(2,1)} %pad_maximum_fusion.1.refs_4_), channel_id=1, source_target_pairs={{0,1},{1,0},{2,3},{3,2},{4,5},{5,4},{6,7},{7,6},{8,9},{9,8},{10,11... | collective-permute-start | bytes 4030472 | tf_op jit(solution)/shard_map/ppermute | solution.py:411
  69.6 0.0 collective-permute-done.11.mate_after_ref
  69.6 1.7 %collective-permute-start.14 = (bf16[4,2,656,128]{3,2,1,0:T(8,128)(2,1)S(1)}, bf16[4,2,656,128]{3,2,1,0:T(8,128)(2,1)S(1)}, u32[]{:S(2)}, u32[]{:S(2)}) collective-permute-start(bf16[4,2,656,128]{3,2,1,0:T(8,128)(2,1)S(1)} %pad_maximum_fusion.refs_0_), channel_id=1, source_target_pairs={{0,96},{1,33},{32,64},{33,1},{64,32},{65,97},{96,0},{97,65},{2,98}... | collective-permute-start | bytes 4030472 | tf_op jit(solution)/shard_map/ppermute | solution.py:333
  71.3 0.0 collective-permute-done.10.mate_before_ref
  71.3 1.5 %collective-permute-start.16 = (bf16[4,2,656,128]{3,2,1,0:T(8,128)(2,1)S(1)}, bf16[4,2,656,128]{3,2,1,0:T(8,128)(2,1)S(1)}, u32[]{:S(2)}, u32[]{:S(2)}) collective-permute-start(bf16[4,2,656,128]{3,2,1,0:T(8,128)(2,1)S(1)} %pad_maximum_fusion.refs_0_), channel_id=1, source_target_pairs={{0,1},{1,0},{2,3},{3,2},{4,5},{5,4},{6,7},{7,6},{8,9},{9,8},{10,11... | collective-permute-start | bytes 4030472 | tf_op jit(solution)/shard_map/ppermute | solution.py:411
  72.8 4.0 %collective-permute-start.22 = (bf16[4,2,656,128]{3,2,1,0:T(8,128)(2,1)}, bf16[4,2,656,128]{3,2,1,0:T(8,128)(2,1)S(1)}, u32[]{:S(2)}, u32[]{:S(2)}) collective-permute-start(bf16[4,2,656,128]{3,2,1,0:T(8,128)(2,1)} %collective-permute-done.15.refs_6_), channel_id=1, source_target_pairs={{0,1},{1,0},{2,3},{3,2},{4,5},{5,4},{6,7},{7,6},{8,9},{9,8},{10,11... | collective-permute-start | bytes 4030472 | tf_op jit(solution)/shard_map/ppermute | solution.py:411
  76.8 9.4 %filter_band.1 = (f32[16,64,256]{2,1,0:T(8,128)}, bf16[8192,128]{1,0:T(8,128)(2,1)S(1)}) custom-call(s32[3]{0:T(128)S(1)} %pad_add_fusion.scalars_ref, bf16[4,64,256]{2,1,0:T(8,128)(2,1)S(1)} %collective-permute-done.8.before_ref, bf16[16,64,256]{2,1,0:T(8,128)(2,1)S(1)} %bitcast.60, bf16[4,64,256]{2,1,0:T(8,128)(2,1)S(1)} %collective-permute-done.9.after_ref, ...), custom_call_target="tpu_custom_call" | custom-call | flops 2000000000 | bytes 6291456 | tf_op jit(solution)/shard_map/filter_band/pallas_call | solution.py:179
  86.2 1.3 %copy-done = bf16[8192,128]{1,0:T(8,128)(2,1)} copy-done((bf16[8192,128]{1,0:T(8,128)(2,1)}, bf16[8192,128]{1,0:T(8,128)(2,1)S(1)}, u32[]{:S(2)}) %copy-start) | copy-done | bytes 2097176
  87.6 0.0 collective-permute-done.13.refs_7_
  87.6 0.0 collective-permute-start.17
  87.6 0.5 collective-permute-start.21
  88.1 3.1 %collective-permute-start.18 = (bf16[4,2,656,128]{3,2,1,0:T(8,128)(2,1)S(1)}, bf16[4,2,656,128]{3,2,1,0:T(8,128)(2,1)S(1)}, u32[]{:S(2)}, u32[]{:S(2)}) collective-permute-start(bf16[4,2,656,128]{3,2,1,0:T(8,128)(2,1)S(1)} %collective-permute-done.14.refs_2_), channel_id=1, source_target_pairs={{0,1},{1,0},{2,3},{3,2},{4,5},{5,4},{6,7},{7,6},{8,9},{9,8},{10,11... | collective-permute-start | bytes 4030472 | tf_op jit(solution)/shard_map/ppermute | solution.py:411
  91.2 0.0 collective-permute-done.16.refs_8_
  91.2 0.1 collective-permute-start.19
  91.3 0.4 collective-permute-start.23
  91.7 4.7 %collective-permute-done.18.refs_10_ = bf16[4,2,656,128]{3,2,1,0:T(8,128)(2,1)S(1)} collective-permute-done((bf16[4,2,656,128]{3,2,1,0:T(8,128)(2,1)S(1)}, bf16[4,2,656,128]{3,2,1,0:T(8,128)(2,1)S(1)}, u32[]{:S(2)}, u32[]{:S(2)}) %collective-permute-start.18) | collective-permute-done | bytes 1343520 | tf_op jit(solution)/shard_map/ppermute | solution.py:411
  96.4 0.0 collective-permute-done.17.refs_9_
  96.4 0.0 collective-permute-done.21.refs_13_
  96.4 1.9 %collective-permute-done.19.refs_11_ = bf16[4,2,656,128]{3,2,1,0:T(8,128)(2,1)S(1)} collective-permute-done((bf16[4,2,656,128]{3,2,1,0:T(8,128)(2,1)S(1)}, bf16[4,2,656,128]{3,2,1,0:T(8,128)(2,1)S(1)}, u32[]{:S(2)}, u32[]{:S(2)}) %collective-permute-start.19) | collective-permute-done | bytes 1343520 | tf_op jit(solution)/shard_map/ppermute | solution.py:411
  98.3 1.1 %copy-done.10 = bf16[4,2,656,128]{3,2,1,0:T(8,128)(2,1)} copy-done((bf16[4,2,656,128]{3,2,1,0:T(8,128)(2,1)}, bf16[4,2,656,128]{3,2,1,0:T(8,128)(2,1)S(1)}, u32[]{:S(2)}) %copy-start.10) | copy-done | bytes 1343512
  99.5 0.0 collective-permute-done.23.refs_15_
  99.5 12.4 %classify.1 = f32[8,16]{1,0:T(8,128)} custom-call(s32[16]{0:T(128)S(1)} %copy-done.2, s32[9,16]{1,0:T(8,128)S(1)} %stack.74.place_ref, bf16[256,32,128]{2,1,0:T(8,128)(2,1)} %bitcast.57, bf16[4,2,656,128]{3,2,1,0:T(8,128)(2,1)S(1)} %pad_maximum_fusion.refs_0_, bf16[4,2,656,128]{3,2,1,0:T(8,128)(2,1)S(1)} %collective-permute-done.3.refs_1_, ...), custom_call_target="tpu_custom_call" | custom-call | flops 5500000256 | bytes 25165824 | tf_op jit(solution)/shard_map/classify/pallas_call | solution.py:305
  (45 shorter events, 0.3 us)
Async XLA Ops:
  0.6 12.1 %copy-start.15 = (s32[16,1]{0,1:T(1,128)S(1)}, s32[16,1]{0,1:T(1,128)}, u32[]{:S(2)}) copy-start(s32[16,1]{0,1:T(1,128)} %param.13) | copy-start | bytes 196
  0.6 12.2 %copy-start.14 = (s32[16]{0:T(128)S(1)}, s32[16]{0:T(128)}, u32[]{:S(2)}) copy-start(s32[16]{0:T(128)} %param.10) | copy-start | bytes 196
  0.7 20.5 %copy-start.16 = (s32[16]{0:T(128)S(1)}, s32[16]{0:T(128)}, u32[]{:S(2)}) copy-start(s32[16]{0:T(128)} %param.11) | copy-start | bytes 196
  3.0 25.9 %copy-start.13 = (bf16[2,656,128]{2,1,0:T(8,128)(2,1)S(1)}, bf16[2,656,128]{2,1,0:T(8,128)(2,1)}, u32[]{:S(2)}) copy-start(bf16[2,656,128]{2,1,0:T(8,128)(2,1)} %get-tuple-element.21) | copy-start | bytes 1007620
  3.0 20.8 %collective-permute-start.5 = (bf16[2,656,128]{2,1,0:T(8,128)(2,1)}, bf16[2,656,128]{2,1,0:T(8,128)(2,1)S(1)}, u32[]{:S(2)}, u32[]{:S(2)}) collective-permute-start(bf16[2,656,128]{2,1,0:T(8,128)(2,1)} %get-tuple-element.21), channel_id=1, source_target_pairs={{0,96},{1,33},{32,64},{33,1},{64,32},{65,97},{96,0},{97,65},{2,98}... | collective-permute-start | bytes 1007624 | tf_op jit(solution)/shard_map/ppermute | solution.py:333
  5.1 17.5 %collective-permute-start.4 = (bf16[2,656,128]{2,1,0:T(8,128)(2,1)}, bf16[2,656,128]{2,1,0:T(8,128)(2,1)S(1)}, u32[]{:S(2)}, u32[]{:S(2)}) collective-permute-start(bf16[2,656,128]{2,1,0:T(8,128)(2,1)} %get-tuple-element.21), channel_id=1, source_target_pairs={{0,32},{1,97},{32,0},{33,65},{64,96},{65,33},{96,64},{97,1},{2,34}... | collective-permute-start | bytes 1007624 | tf_op jit(solution)/shard_map/ppermute | solution.py:333
  7.0 16.8 %collective-permute-start.1 = (bf16[2,784,128]{2,1,0:T(8,128)(2,1)}, bf16[2,784,128]{2,1,0:T(8,128)(2,1)S(1)}, u32[]{:S(2)}, u32[]{:S(2)}) collective-permute-start(bf16[2,784,128]{2,1,0:T(8,128)(2,1)} %get-tuple-element.18), channel_id=1, source_target_pairs={{0,24},{1,9},{8,16},{9,1},{16,8},{17,25},{24,0},{25,17},{2,26},{3,... | collective-permute-start | bytes 1204232 | tf_op jit(solution)/shard_map/ppermute | solution.py:333
  8.6 14.3 %collective-permute-start = (bf16[2,784,128]{2,1,0:T(8,128)(2,1)}, bf16[2,784,128]{2,1,0:T(8,128)(2,1)S(1)}, u32[]{:S(2)}, u32[]{:S(2)}) collective-permute-start(bf16[2,784,128]{2,1,0:T(8,128)(2,1)} %get-tuple-element.18), channel_id=1, source_target_pairs={{0,8},{1,25},{8,0},{9,17},{16,24},{17,9},{24,16},{25,1},{2,10},{3,... | collective-permute-start | bytes 1204232 | tf_op jit(solution)/shard_map/ppermute | solution.py:333
  22.5 6.3 %collective-permute-start.6 = (bf16[2,656,128]{2,1,0:T(8,128)(2,1)S(1)}, bf16[2,656,128]{2,1,0:T(8,128)(2,1)S(1)}, u32[]{:S(2)}, u32[]{:S(2)}) collective-permute-start(bf16[2,656,128]{2,1,0:T(8,128)(2,1)S(1)} %collective-permute-done.4), channel_id=1, source_target_pairs={{0,96},{1,33},{32,64},{33,1},{64,32},{65,97},{96,0},{97,65},{2,98}... | collective-permute-start | bytes 1007624 | tf_op jit(solution)/shard_map/ppermute | solution.py:333
  23.0 7.2 %copy-start.12 = (bf16[2,784,128]{2,1,0:T(8,128)(2,1)}, bf16[2,784,128]{2,1,0:T(8,128)(2,1)S(1)}, u32[]{:S(2)}) copy-start(bf16[2,784,128]{2,1,0:T(8,128)(2,1)S(1)} %collective-permute-done) | copy-start | bytes 1204228
  23.0 7.6 %collective-permute-start.2 = (bf16[2,784,128]{2,1,0:T(8,128)(2,1)S(1)}, bf16[2,784,128]{2,1,0:T(8,128)(2,1)S(1)}, u32[]{:S(2)}, u32[]{:S(2)}) collective-permute-start(bf16[2,784,128]{2,1,0:T(8,128)(2,1)S(1)} %collective-permute-done), channel_id=1, source_target_pairs={{0,24},{1,9},{8,16},{9,1},{16,8},{17,25},{24,0},{25,17},{2,26},{3,... | collective-permute-start | bytes 1204232 | tf_op jit(solution)/shard_map/ppermute | solution.py:333
  23.7 6.4 %copy-start.11 = (bf16[2,784,128]{2,1,0:T(8,128)(2,1)}, bf16[2,784,128]{2,1,0:T(8,128)(2,1)S(1)}, u32[]{:S(2)}) copy-start(bf16[2,784,128]{2,1,0:T(8,128)(2,1)S(1)} %collective-permute-done.1) | copy-start | bytes 1204228
  30.1 22.1 %collective-permute-start.7 = (bf16[4,2,656,128]{3,2,1,0:T(8,128)(2,1)}, bf16[4,2,656,128]{3,2,1,0:T(8,128)(2,1)}, u32[]{:S(2)}, u32[]{:S(2)}) collective-permute-start(bf16[4,2,656,128]{3,2,1,0:T(8,128)(2,1)} %pad_maximum_fusion.1.refs_4_), channel_id=1, source_target_pairs={{0,8},{1,25},{8,0},{9,17},{16,24},{17,9},{24,16},{25,1},{2,10},{3,... | collective-permute-start | bytes 4030472 | tf_op jit(solution)/shard_map/ppermute | solution.py:333
  30.8 7.4 %copy-start.1 = (bf16[1,16,64,256]{3,2,1,0:T(8,128)(2,1)S(1)}, bf16[1,16,64,256]{3,2,1,0:T(8,128)(2,1)}, u32[]{:S(2)}) copy-start(bf16[1,16,64,256]{3,2,1,0:T(8,128)(2,1)} %param.9) | copy-start | bytes 1572868
  30.8 21.5 %collective-permute-start.3 = (bf16[4,2,656,128]{3,2,1,0:T(8,128)(2,1)S(1)}, bf16[4,2,656,128]{3,2,1,0:T(8,128)(2,1)S(1)}, u32[]{:S(2)}, u32[]{:S(2)}) collective-permute-start(bf16[4,2,656,128]{3,2,1,0:T(8,128)(2,1)S(1)} %pad_maximum_fusion.refs_0_), channel_id=1, source_target_pairs={{0,32},{1,97},{32,0},{33,65},{64,96},{65,33},{96,64},{97,1},{2,34}... | collective-permute-start | bytes 4030472 | tf_op jit(solution)/shard_map/ppermute | solution.py:333
  34.2 17.2 %all-to-all-start = ((bf16[4,2,128,128]{3,2,1,0:T(8,128)(2,1)}), bf16[4,2,128,128]{3,2,1,0:T(8,128)(2,1)}, u32[]{:S(2)}, u32[]{:S(2)}) async-start(bf16[4,2,128,128]{3,2,1,0:T(8,128)(2,1)} %pad_maximum_fusion.3), calls=%async_computation | async-start | bytes 524288 | tf_op jit(solution)/shard_map/all_to_all | solution.py:392
  39.0 13.3 %collective-permute-start.9 = (bf16[4,64,256]{2,1,0:T(8,128)(2,1)}, bf16[4,64,256]{2,1,0:T(8,128)(2,1)S(1)}, u32[]{:S(2)}, u32[]{:S(2)}) collective-permute-start(bf16[4,64,256]{2,1,0:T(8,128)(2,1)} %get-tuple-element.38), channel_id=1, source_target_pairs={{1,0},{2,1},{3,2},{4,3},{5,4},{6,5},{7,6},{9,8},{10,9},{11,10},{12... | collective-permute-start | bytes 393224 | tf_op jit(solution)/shard_map/ppermute | solution.py:380
  45.2 7.1 %collective-permute-start.8 = (bf16[4,64,256]{2,1,0:T(8,128)(2,1)}, bf16[4,64,256]{2,1,0:T(8,128)(2,1)S(1)}, u32[]{:S(2)}, u32[]{:S(2)}) collective-permute-start(bf16[4,64,256]{2,1,0:T(8,128)(2,1)} %get-tuple-element.39), channel_id=1, source_target_pairs={{0,1},{1,2},{2,3},{3,4},{4,5},{5,6},{6,7},{8,9},{9,10},{10,11},{11... | collective-permute-start | bytes 393224 | tf_op jit(solution)/shard_map/ppermute | solution.py:379
  50.7 17.5 %collective-permute-start.15 = (bf16[4,2,656,128]{3,2,1,0:T(8,128)(2,1)}, bf16[4,2,656,128]{3,2,1,0:T(8,128)(2,1)}, u32[]{:S(2)}, u32[]{:S(2)}) collective-permute-start(bf16[4,2,656,128]{3,2,1,0:T(8,128)(2,1)} %pad_maximum_fusion.1.refs_4_), channel_id=1, source_target_pairs={{0,24},{1,9},{8,16},{9,1},{16,8},{17,25},{24,0},{25,17},{2,26},{3,... | collective-permute-start | bytes 4030472 | tf_op jit(solution)/shard_map/ppermute | solution.py:333
  52.3 47.3 %copy-start.2 = (s32[16]{0:T(128)S(1)}, s32[16]{0:T(128)}, u32[]{:S(2)}) copy-start(s32[16]{0:T(128)} %starts_ref.1) | copy-start | bytes 196
  52.3 20.5 %collective-permute-start.12 = (bf16[4,2,656,128]{3,2,1,0:T(8,128)(2,1)S(1)}, bf16[4,2,656,128]{3,2,1,0:T(8,128)(2,1)S(1)}, u32[]{:S(2)}, u32[]{:S(2)}) collective-permute-start(bf16[4,2,656,128]{3,2,1,0:T(8,128)(2,1)S(1)} %collective-permute-done.3.refs_1_), channel_id=1, source_target_pairs={{0,96},{1,33},{32,64},{33,1},{64,32},{65,97},{96,0},{97,65},{2,98}... | collective-permute-start | bytes 4030472 | tf_op jit(solution)/shard_map/ppermute | solution.py:333
  54.1 15.5 %collective-permute-start.11 = (bf16[4,64,128]{2,1,0:T(8,128)(2,1)S(1)}, bf16[4,64,128]{2,1,0:T(8,128)(2,1)S(1)}, u32[]{:S(2)}, u32[]{:S(2)}) collective-permute-start(bf16[4,64,128]{2,1,0:T(8,128)(2,1)S(1)} %bitcast.61), channel_id=1, source_target_pairs={{1,0},{2,1},{3,2},{4,3},{5,4},{6,5},{7,6},{9,8},{10,9},{11,10},{12... | collective-permute-start | bytes 196616 | tf_op jit(solution)/shard_map/ppermute | solution.py:401
  61.9 9.4 %collective-permute-start.10 = (bf16[4,64,128]{2,1,0:T(8,128)(2,1)S(1)}, bf16[4,64,128]{2,1,0:T(8,128)(2,1)S(1)}, u32[]{:S(2)}, u32[]{:S(2)}) collective-permute-start(bf16[4,64,128]{2,1,0:T(8,128)(2,1)S(1)} %bitcast.62), channel_id=1, source_target_pairs={{0,1},{1,2},{2,3},{3,4},{4,5},{5,6},{6,7},{8,9},{9,10},{10,11},{11... | collective-permute-start | bytes 196616 | tf_op jit(solution)/shard_map/ppermute | solution.py:400
  65.0 22.6 %collective-permute-start.13 = (bf16[4,2,656,128]{3,2,1,0:T(8,128)(2,1)}, bf16[4,2,656,128]{3,2,1,0:T(8,128)(2,1)S(1)}, u32[]{:S(2)}, u32[]{:S(2)}) collective-permute-start(bf16[4,2,656,128]{3,2,1,0:T(8,128)(2,1)} %collective-permute-done.7.refs_5_), channel_id=1, source_target_pairs={{0,24},{1,9},{8,16},{9,1},{16,8},{17,25},{24,0},{25,17},{2,26},{3,... | collective-permute-start | bytes 4030472 | tf_op jit(solution)/shard_map/ppermute | solution.py:333
  68.2 19.4 %collective-permute-start.20 = (bf16[4,2,656,128]{3,2,1,0:T(8,128)(2,1)}, bf16[4,2,656,128]{3,2,1,0:T(8,128)(2,1)S(1)}, u32[]{:S(2)}, u32[]{:S(2)}) collective-permute-start(bf16[4,2,656,128]{3,2,1,0:T(8,128)(2,1)} %pad_maximum_fusion.1.refs_4_), channel_id=1, source_target_pairs={{0,1},{1,0},{2,3},{3,2},{4,5},{5,4},{6,7},{7,6},{8,9},{9,8},{10,11... | collective-permute-start | bytes 4030472 | tf_op jit(solution)/shard_map/ppermute | solution.py:411
  69.6 18.5 %collective-permute-start.14 = (bf16[4,2,656,128]{3,2,1,0:T(8,128)(2,1)S(1)}, bf16[4,2,656,128]{3,2,1,0:T(8,128)(2,1)S(1)}, u32[]{:S(2)}, u32[]{:S(2)}) collective-permute-start(bf16[4,2,656,128]{3,2,1,0:T(8,128)(2,1)S(1)} %pad_maximum_fusion.refs_0_), channel_id=1, source_target_pairs={{0,96},{1,33},{32,64},{33,1},{64,32},{65,97},{96,0},{97,65},{2,98}... | collective-permute-start | bytes 4030472 | tf_op jit(solution)/shard_map/ppermute | solution.py:333
  71.3 19.9 %collective-permute-start.16 = (bf16[4,2,656,128]{3,2,1,0:T(8,128)(2,1)S(1)}, bf16[4,2,656,128]{3,2,1,0:T(8,128)(2,1)S(1)}, u32[]{:S(2)}, u32[]{:S(2)}) collective-permute-start(bf16[4,2,656,128]{3,2,1,0:T(8,128)(2,1)S(1)} %pad_maximum_fusion.refs_0_), channel_id=1, source_target_pairs={{0,1},{1,0},{2,3},{3,2},{4,5},{5,4},{6,7},{7,6},{8,9},{9,8},{10,11... | collective-permute-start | bytes 4030472 | tf_op jit(solution)/shard_map/ppermute | solution.py:411
  72.8 18.5 %collective-permute-start.22 = (bf16[4,2,656,128]{3,2,1,0:T(8,128)(2,1)}, bf16[4,2,656,128]{3,2,1,0:T(8,128)(2,1)S(1)}, u32[]{:S(2)}, u32[]{:S(2)}) collective-permute-start(bf16[4,2,656,128]{3,2,1,0:T(8,128)(2,1)} %collective-permute-done.15.refs_6_), channel_id=1, source_target_pairs={{0,1},{1,0},{2,3},{3,2},{4,5},{5,4},{6,7},{7,6},{8,9},{9,8},{10,11... | collective-permute-start | bytes 4030472 | tf_op jit(solution)/shard_map/ppermute | solution.py:411
  86.2 1.3 %copy-start = (bf16[8192,128]{1,0:T(8,128)(2,1)}, bf16[8192,128]{1,0:T(8,128)(2,1)S(1)}, u32[]{:S(2)}) copy-start(bf16[8192,128]{1,0:T(8,128)(2,1)S(1)} %get-tuple-element.30) | copy-start | bytes 6291460
  87.6 11.9 %copy-start.3 = (bf16[4,2,656,128]{3,2,1,0:T(8,128)(2,1)}, bf16[4,2,656,128]{3,2,1,0:T(8,128)(2,1)S(1)}, u32[]{:S(2)}) copy-start(bf16[4,2,656,128]{3,2,1,0:T(8,128)(2,1)S(1)} %collective-permute-done.13.refs_7_) | copy-start | bytes 4030468
  87.6 8.9 %collective-permute-start.17 = (bf16[4,2,656,128]{3,2,1,0:T(8,128)(2,1)S(1)}, bf16[4,2,656,128]{3,2,1,0:T(8,128)(2,1)S(1)}, u32[]{:S(2)}, u32[]{:S(2)}) collective-permute-start(bf16[4,2,656,128]{3,2,1,0:T(8,128)(2,1)S(1)} %collective-permute-done.3.refs_1_), channel_id=1, source_target_pairs={{0,1},{1,0},{2,3},{3,2},{4,5},{5,4},{6,7},{7,6},{8,9},{9,8},{10,11... | collective-permute-start | bytes 4030472 | tf_op jit(solution)/shard_map/ppermute | solution.py:411
  87.6 11.9 %copy-start.4 = (bf16[4,2,656,128]{3,2,1,0:T(8,128)(2,1)}, bf16[4,2,656,128]{3,2,1,0:T(8,128)(2,1)S(1)}, u32[]{:S(2)}) copy-start(bf16[4,2,656,128]{3,2,1,0:T(8,128)(2,1)S(1)} %collective-permute-done.20.refs_12_) | copy-start | bytes 4030468
  87.6 8.8 %collective-permute-start.21 = (bf16[4,2,656,128]{3,2,1,0:T(8,128)(2,1)}, bf16[4,2,656,128]{3,2,1,0:T(8,128)(2,1)S(1)}, u32[]{:S(2)}, u32[]{:S(2)}) collective-permute-start(bf16[4,2,656,128]{3,2,1,0:T(8,128)(2,1)} %collective-permute-done.7.refs_5_), channel_id=1, source_target_pairs={{0,1},{1,0},{2,3},{3,2},{4,5},{5,4},{6,7},{7,6},{8,9},{9,8},{10,11... | collective-permute-start | bytes 4030472 | tf_op jit(solution)/shard_map/ppermute | solution.py:411
  88.1 8.3 %collective-permute-start.18 = (bf16[4,2,656,128]{3,2,1,0:T(8,128)(2,1)S(1)}, bf16[4,2,656,128]{3,2,1,0:T(8,128)(2,1)S(1)}, u32[]{:S(2)}, u32[]{:S(2)}) collective-permute-start(bf16[4,2,656,128]{3,2,1,0:T(8,128)(2,1)S(1)} %collective-permute-done.14.refs_2_), channel_id=1, source_target_pairs={{0,1},{1,0},{2,3},{3,2},{4,5},{5,4},{6,7},{7,6},{8,9},{9,8},{10,11... | collective-permute-start | bytes 4030472 | tf_op jit(solution)/shard_map/ppermute | solution.py:411
  91.2 8.3 %copy-start.5 = (bf16[4,2,656,128]{3,2,1,0:T(8,128)(2,1)}, bf16[4,2,656,128]{3,2,1,0:T(8,128)(2,1)S(1)}, u32[]{:S(2)}) copy-start(bf16[4,2,656,128]{3,2,1,0:T(8,128)(2,1)S(1)} %collective-permute-done.16.refs_8_) | copy-start | bytes 4030468
  91.2 7.1 %collective-permute-start.19 = (bf16[4,2,656,128]{3,2,1,0:T(8,128)(2,1)S(1)}, bf16[4,2,656,128]{3,2,1,0:T(8,128)(2,1)S(1)}, u32[]{:S(2)}, u32[]{:S(2)}) collective-permute-start(bf16[4,2,656,128]{3,2,1,0:T(8,128)(2,1)S(1)} %collective-permute-done.12.refs_3_), channel_id=1, source_target_pairs={{0,1},{1,0},{2,3},{3,2},{4,5},{5,4},{6,7},{7,6},{8,9},{9,8},{10,11... | collective-permute-start | bytes 4030472 | tf_op jit(solution)/shard_map/ppermute | solution.py:411
  91.3 8.2 %copy-start.6 = (bf16[4,2,656,128]{3,2,1,0:T(8,128)(2,1)}, bf16[4,2,656,128]{3,2,1,0:T(8,128)(2,1)S(1)}, u32[]{:S(2)}) copy-start(bf16[4,2,656,128]{3,2,1,0:T(8,128)(2,1)S(1)} %collective-permute-done.22.refs_14_) | copy-start | bytes 4030468
  91.3 8.2 %collective-permute-start.23 = (bf16[4,2,656,128]{3,2,1,0:T(8,128)(2,1)S(1)}, bf16[4,2,656,128]{3,2,1,0:T(8,128)(2,1)}, u32[]{:S(2)}, u32[]{:S(2)}) collective-permute-start(bf16[4,2,656,128]{3,2,1,0:T(8,128)(2,1)S(1)} %collective-permute-done.13.refs_7_), channel_id=1, source_target_pairs={{0,1},{1,0},{2,3},{3,2},{4,5},{5,4},{6,7},{7,6},{8,9},{9,8},{10,11... | collective-permute-start | bytes 4030472 | tf_op jit(solution)/shard_map/ppermute | solution.py:411
  96.4 3.1 %copy-start.9 = (bf16[4,2,656,128]{3,2,1,0:T(8,128)(2,1)}, bf16[4,2,656,128]{3,2,1,0:T(8,128)(2,1)S(1)}, u32[]{:S(2)}) copy-start(bf16[4,2,656,128]{3,2,1,0:T(8,128)(2,1)S(1)} %collective-permute-done.18.refs_10_) | copy-start | bytes 4030468
  96.4 3.1 %copy-start.7 = (bf16[4,2,656,128]{3,2,1,0:T(8,128)(2,1)}, bf16[4,2,656,128]{3,2,1,0:T(8,128)(2,1)S(1)}, u32[]{:S(2)}) copy-start(bf16[4,2,656,128]{3,2,1,0:T(8,128)(2,1)S(1)} %collective-permute-done.17.refs_9_) | copy-start | bytes 4030468
  96.4 3.1 %copy-start.8 = (bf16[4,2,656,128]{3,2,1,0:T(8,128)(2,1)}, bf16[4,2,656,128]{3,2,1,0:T(8,128)(2,1)S(1)}, u32[]{:S(2)}) copy-start(bf16[4,2,656,128]{3,2,1,0:T(8,128)(2,1)S(1)} %collective-permute-done.21.refs_13_) | copy-start | bytes 4030468
  98.3 1.1 %copy-start.10 = (bf16[4,2,656,128]{3,2,1,0:T(8,128)(2,1)}, bf16[4,2,656,128]{3,2,1,0:T(8,128)(2,1)S(1)}, u32[]{:S(2)}) copy-start(bf16[4,2,656,128]{3,2,1,0:T(8,128)(2,1)S(1)} %collective-permute-done.19.refs_11_) | copy-start | bytes 4030468
